TPU v7x, 512 devices: a whole 4x4x16 slice. The times are simulated.
512 devices in a mesh: dom: 32 (over z, core), head: 16 (over x, y).
Axes of the slice: x: 4, y: 4, z: 16, core: 2. Of those that a mesh axis runs over, the one named last changes fastest.
Arguments:
- features: bfloat16 [262144, 512], P(('dom', 'head')), may hold values from -16 to 16
- tile_pattern: int32 [2048, 6, 128, 128], P(('dom', 'head')), may hold values 0 or 1
- tile_source: int32 [2048, 6], P(('dom', 'head')), may hold values from 0 to 35
- serve_list: int32 [32, 16, 32, 1], P('dom', 'head'), may hold values from 0 to 3
- key_blocks: int32 [2048, 8], P('dom'), may hold values from 0 to 63, all different within a row
- qkv_weight: bfloat16 [512, 1536], replicated, may hold values from -0.25 to 0.25
- attn_weight: bfloat16 [512, 512], replicated, may hold values from -0.25 to 0.25
- norm_gain: float32 [512], replicated, may hold values from 0.5 to 1.5
- expand_weight: bfloat16 [2048, 512], P('head'), may hold values from -0.25 to 0.25
- reduce_weight: bfloat16 [2048, 512], P('head'), may hold values from -0.125 to 0.125
Outputs:
- output: bfloat16 [262144, 512], P(('dom', 'head'))
Inputs may be any that keep to these rules, and one draw needn't show every extreme that they name: `key_blocks`: the 8 entries of a row are distinct.
All inputs are finite; a program needn't handle non-finite values. No bound on the sum of `tile_pattern` on one device may be relied on, other than what follows from the above.
Results may differ from a plain program's by a relative error of at most 0.01.
The roundings to bfloat16 on the way count: a program that leaves them out, or rounds other values in their place, can miss the bound.
Values may be sent and summed in bfloat16 or wider, within the bound.
No kernel may reach another device: no remote copies, remote signals or barrier semaphores. Data moves between devices by JAX's collectives and lax.ppermute only.
A program may use at most 128 MiB of HBM per device.

v0:
```python
import math

import jax
import jax.numpy as jnp
from jax import lax
from jax.experimental import pallas as pl
from jax.experimental.pallas import tpu as pltpu
from jax.sharding import PartitionSpec as P


HEADS = 16
HDIM = 32
BLOCK = 128
VM = pl.BlockSpec(memory_space=pltpu.VMEM)
SM = pl.BlockSpec(memory_space=pltpu.SMEM)
FAR = pl.BlockSpec(memory_space=pltpu.HBM)
EXP2_SCALE = math.log2(math.e) / math.sqrt(HDIM)


def ring_pieces(x, jobs):
    results = [None] * len(jobs)
    n = lax.axis_size("dom")
    half = n // 4
    cut = x.shape[0] // 2

    def send(v, by):
        return lax.ppermute(v, "dom", [(i, (i + by) % n) for i in range(n)])

    def trade(v):
        return lax.ppermute(v, "dom", [(i, i ^ 1) for i in range(n)])

    up, down = [x], [x]
    up_t, down_t = [trade(x)], []
    for k in range(1, half + 1):
        u_in, d_in = lax.optimization_barrier((up[-1], down[-1]))
        for i, (_, last, _, _) in enumerate(jobs):
            if k == last:
                u_in, results[i] = lax.optimization_barrier((u_in, results[i]))
        if k == half:
            u_in, d_in = u_in[:cut], d_in[cut:]
        if k >= 3:
            u_in, up_t[k - 2] = lax.optimization_barrier((u_in, up_t[k - 2]))
            d_in, down_t[k - 3] = lax.optimization_barrier((d_in, down_t[k - 3]))
        up.append(send(u_in, 2))
        down.append(send(d_in, -2))
        up_t.append(trade(up[-1]))
        down_t.append(trade(down[-1]))
        for i, (first, _, work, operand) in enumerate(jobs):
            if k == first:
                up_t[-1], down_t[-1], operand = lax.optimization_barrier(
                    (up_t[-1], down_t[-1], operand)
                )
                results[i] = work(operand)
    whole = up[:half] + down[1:half] + up_t[:half] + down_t[: half - 1]
    return whole + [up[half], down[half], up_t[half], down_t[half - 1]], results


def piece_sources(d, n):
    core, z = d % 2, d // 2
    chips, half = n // 2, n // 4
    up = [2 * ((z + chips - k) % chips) + core for k in range(half + 1)]
    down = [2 * ((z + k) % chips) + core for k in range(half + 1)]
    near = up[:half] + down[1:half]
    flip = 1 - 2 * core
    return near + [p + flip for p in near] + [up[half], up[half] + flip]


def slot_of_entry(e, d, blocks, n):
    p = jnp.maximum(e - blocks, 0)
    core, z = d % 2, d // 2
    chips, half = n // 2, n // 4
    k = (z + chips - p // 2) % chips
    other = jnp.where((p % 2) == core, 0, 1)
    near = jnp.where(k < half, k, half - 1 + chips - k)
    piece = jnp.where(k == half, 2 * (2 * half - 1) + other, near + other * (2 * half - 1))
    return jnp.where(e < blocks, e, blocks + piece)


def aggregate_kernel(place_ref, entry_ref, serve_ref, pattern_ref, own_ref, wt_ref, *rest):
    pieces, (agg_ref, qkv_ref, table, sems) = rest[:-4], rest[-4:]
    blocks, tiles = pattern_ref.shape[0], pattern_ref.shape[1]
    whole, halves = pieces[:-4], pieces[-4:]
    n_dom = len(pieces) - 2
    d = place_ref[0]
    sources = piece_sources(d, n_dom)
    copies = []

    def copy_of(i, piece, block):
        start = pl.multiple_of(block * BLOCK, BLOCK)
        return pltpu.make_async_copy(
            piece.at[pl.ds(start, BLOCK), :], table.at[blocks + i], sems.at[i]
        )

    for i, piece in enumerate(whole):
        copies.append(copy_of(i, piece, serve_ref[sources[i]]))
        copies[-1].start()
    for i in range(2):
        slot, first = len(whole) + i, blocks // 2
        block = serve_ref[sources[slot]]

        @pl.when(block < first)
        def _(slot=slot, piece=halves[2 * i], block=block):
            copy_of(slot, piece, block).start()

        @pl.when(block >= first)
        def _(slot=slot, piece=halves[2 * i + 1], block=block - first):
            copy_of(slot, piece, block).start()

        copies.append(copy_of(slot, halves[2 * i], 0))
    for b in range(blocks):
        table[b] = own_ref[b * BLOCK : (b + 1) * BLOCK, :]
    for copy in copies:
        copy.wait()

    def one_block(b, carry):
        acc = table[b].astype(jnp.float32)
        count = jnp.zeros((BLOCK, BLOCK), jnp.int32)
        for t in range(0, tiles, 2):
            two = []
            for u in (t, t + 1):
                pattern = pattern_ref[b, u]
                count = count + pattern
                two.append(pattern.astype(jnp.float32).astype(jnp.bfloat16))
            rows = [
                table[slot_of_entry(entry_ref[b, u], d, blocks, n_dom)] for u in (t, t + 1)
            ]
            acc = acc + jnp.dot(
                jnp.concatenate(two, axis=1),
                jnp.concatenate(rows, axis=0),
                preferred_element_type=jnp.float32,
            )
        degree = jnp.sum(count.astype(jnp.float32), axis=1, keepdims=True)
        span = pl.ds(pl.multiple_of(b * BLOCK, BLOCK), BLOCK)
        agg_ref[span, :] = (acc * lax.rsqrt(1.0 + degree)).astype(jnp.bfloat16)
        return carry

    lax.fori_loop(0, blocks, one_block, 0)
    third = qkv_ref.shape[0] // 3

    def one_third(i, carry):
        span = pl.ds(pl.multiple_of(i * third, third), third)
        qkv_ref[span, :] = lax.dot_general(
            wt_ref[span, :], agg_ref[...], (((1,), (1,)), ((), ())),
            preferred_element_type=jnp.float32,
        ).astype(jnp.bfloat16)
        return carry

    lax.fori_loop(0, 3, one_third, 0)


def aggregate(place, entries, serve, pattern, own, weight_t, pieces):
    rows, width = own.shape
    blocks, tiles = pattern.shape[0], pattern.shape[1]
    assert tiles % 2 == 0
    return pl.pallas_call(
        aggregate_kernel,
        out_shape=(
            jax.ShapeDtypeStruct((rows, width), jnp.bfloat16),
            jax.ShapeDtypeStruct((weight_t.shape[0], rows), jnp.bfloat16),
        ),
        in_specs=[SM, SM, SM, VM, VM, VM] + [FAR] * len(pieces),
        out_specs=(VM, VM),
        scratch_shapes=[
            pltpu.VMEM((blocks + len(pieces) - 2, BLOCK, width), jnp.bfloat16),
            pltpu.SemaphoreType.DMA((len(pieces) - 2,)),
        ],
        name="aggregate",
    )(place, entries, serve, pattern, own, weight_t, *pieces)


def attend_kernel(key_ref, qkv_ref, out_ref, q_ref, kv_ref):
    sources, _, rows = qkv_ref.shape
    per = rows // BLOCK
    keys = key_ref.shape[1]

    def unpack(h, carry):
        for j in range(per):
            cols = slice(j * BLOCK, (j + 1) * BLOCK)
            q_ref[h * per + j] = qkv_ref[h, 0:HDIM, cols]
            kv_ref[h * per + j] = qkv_ref[h, HDIM : 3 * HDIM, cols]
        return carry

    lax.fori_loop(0, sources, unpack, 0)
    ones = jnp.ones((16, keys * BLOCK), jnp.bfloat16)

    def chosen(b, part):
        span = slice(part * HDIM, (part + 1) * HDIM)
        return jnp.concatenate([kv_ref[key_ref[b, k], span, :] for k in range(keys)], axis=1)

    def probabilities(scores):
        top = jnp.max(scores, axis=1, keepdims=True)
        return jnp.exp2((scores - top) * EXP2_SCALE).astype(jnp.bfloat16)

    def one_source(h, carry):
        ids = [h * per + j for j in range(per)]
        scores = [
            lax.dot_general(
                q_ref[b], chosen(b, 0), (((0,), (0,)), ((), ())),
                preferred_element_type=jnp.float32,
            )
            for b in ids
        ]
        values = [jnp.concatenate([chosen(b, 1), ones], axis=0) for b in ids]
        terms = [probabilities(s) for s in scores]
        for j in range(per):
            mixed = lax.dot_general(
                values[j], terms[j], (((1,), (1,)), ((), ())),
                preferred_element_type=jnp.float32,
            )
            mixed = mixed[0:HDIM] * (1.0 / mixed[HDIM : HDIM + 1])
            out_ref[h, :, j * BLOCK : (j + 1) * BLOCK] = mixed.astype(jnp.bfloat16)
        return carry

    lax.fori_loop(0, sources, one_source, 0)


def attend(key_blocks, qkv):
    sources, _, rows = qkv.shape
    blocks = sources * (rows // BLOCK)
    return pl.pallas_call(
        attend_kernel,
        out_shape=jax.ShapeDtypeStruct((sources, HDIM, rows), jnp.bfloat16),
        in_specs=[SM, VM],
        out_specs=VM,
        scratch_shapes=[
            pltpu.VMEM((blocks, HDIM, BLOCK), jnp.bfloat16),
            pltpu.VMEM((blocks, 2 * HDIM, BLOCK), jnp.bfloat16),
        ],
        compiler_params=pltpu.CompilerParams(vmem_limit_bytes=16 << 20),
        name="attend",
    )(key_blocks, qkv)


def finish_kernel(context_ref, agg_ref, attn_ref, gain_ref, ffn_ref, out_ref, normed_ref, total_ref):
    _, width = agg_ref.shape
    hidden_units = ffn_ref.shape[0]
    mixed = agg_ref[...].astype(jnp.float32) + jnp.dot(
        context_ref[...].T, attn_ref[...], preferred_element_type=jnp.float32
    )
    mean_square = jnp.mean(mixed * mixed, axis=1, keepdims=True)
    normed = (mixed * lax.rsqrt(mean_square + 1e-06) * gain_ref[...]).astype(jnp.bfloat16)
    normed_ref[...] = normed
    total_ref[...] = normed.astype(jnp.float32)
    chunk = 512

    def one_chunk(c, carry):
        span = pl.ds(pl.multiple_of(c * chunk, chunk), chunk)
        hidden = lax.dot_general(
            normed_ref[...], ffn_ref[span, 0:width], (((1,), (1,)), ((), ())),
            preferred_element_type=jnp.float32,
        )
        hidden = jax.nn.gelu(hidden).astype(jnp.bfloat16)
        total_ref[...] += jnp.dot(
            hidden, ffn_ref[span, width : 2 * width], preferred_element_type=jnp.float32
        )
        return carry

    lax.fori_loop(0, hidden_units // chunk, one_chunk, 0)
    out_ref[...] = total_ref[...].astype(jnp.bfloat16)


def finish(context_t, agg, attn_weight, gain, ffn):
    rows, width = agg.shape
    return pl.pallas_call(
        finish_kernel,
        out_shape=jax.ShapeDtypeStruct((rows, width), jnp.bfloat16),
        in_specs=[VM] * 5,
        out_specs=VM,
        scratch_shapes=[
            pltpu.VMEM((rows, width), jnp.bfloat16),
            pltpu.VMEM((rows, width), jnp.float32),
        ],
        compiler_params=pltpu.CompilerParams(vmem_limit_bytes=20 << 20),
        name="finish",
    )(context_t, agg, attn_weight, gain, ffn)


def shards(
    features,
    tile_pattern,
    tile_source,
    serve_list,
    key_blocks,
    qkv_weight,
    attn_weight,
    norm_gain,
    expand_weight,
    reduce_weight,
):
    n_dom, n_head = lax.axis_size("dom"), lax.axis_size("head")
    width = features.shape[1]
    rows = features.shape[0]

    def exchange_lists(lists):
        return lax.all_to_all(
            lists.reshape(n_dom, 1), "dom", split_axis=0, concat_axis=0, tiled=True
        ).reshape(n_dom)

    def gather_ffn(weights):
        both = jnp.concatenate(weights, axis=1)
        return lax.all_to_all(
            jnp.broadcast_to(both[None], (n_head,) + both.shape),
            "head", split_axis=0, concat_axis=0, tiled=True,
        ).reshape(-1, 2 * width)

    jobs = [
        (1, 5, exchange_lists, serve_list),
        (2, None, gather_ffn, (expand_weight, reduce_weight)),
        (4, 7, jnp.transpose, qkv_weight),
    ]
    pieces, (served, ffn, weight_t) = ring_pieces(features, jobs)
    place = lax.axis_index("dom").reshape(1)
    agg, qkv_t = aggregate(
        place, tile_source, served, tile_pattern, features, weight_t, pieces
    )
    qkv = lax.all_to_all(
        qkv_t.reshape(n_head, 3 * HDIM, rows), "head", split_axis=0, concat_axis=0, tiled=True
    )
    context = attend(key_blocks, qkv)
    context_t = lax.all_to_all(
        context, "head", split_axis=0, concat_axis=0, tiled=True
    ).reshape(HEADS * HDIM, rows)
    return finish(context_t, agg, attn_weight, norm_gain.reshape(1, width), ffn)


def solution(mesh):
    placed = (
        P(("dom", "head"), None),
        P(("dom", "head"), None, None, None),
        P(("dom", "head"), None),
        P("dom", "head", None, None),
        P("dom", None),
        P(),
        P(),
        P(),
        P("head", None),
        P("head", None),
    )

    return jax.shard_map(
        shards, mesh=mesh, in_specs=placed, out_specs=P(("dom", "head"), None), check_vma=False
    )
```

profile of v0, /device:TPU:8, one launch (start us, length us, event | category | flops | bytes accessed | tf_op | source)
XLA Modules:
  0.0 294.0 jit_solution(13353342962825046513)
XLA Ops:
  0.0 3.8 %collective-permute-start = (bf16[512,512]{1,0:T(8,128)(2,1)}, bf16[512,512]{1,0:T(8,128)(2,1)S(1)}, u32[]{:S(2)}, u32[]{:S(2)}) collective-permute-start(bf16[512,512]{1,0:T(8,128)(2,1)} %rest_0_.1), channel_id=1, source_target_pairs={{0,32},{16,48},{32,64},{48,80},{64,96},{80,112},{96,128},{112,144}... | collective-permute-start | bytes 1572872 | tf_op jit(solution)/shard_map/ppermute | solution.py:27
  3.8 9.5 %collective-permute-start.1 = (bf16[512,512]{1,0:T(8,128)(2,1)}, bf16[512,512]{1,0:T(8,128)(2,1)S(1)}, u32[]{:S(2)}, u32[]{:S(2)}) collective-permute-start(bf16[512,512]{1,0:T(8,128)(2,1)} %rest_0_.1), channel_id=1, source_target_pairs={{0,480},{16,496},{32,0},{48,16},{64,32},{80,48},{96,64},{112,80},{... | collective-permute-start | bytes 1572872 | tf_op jit(solution)/shard_map/ppermute | solution.py:27
  13.3 10.2 %collective-permute-done.rest_1_ = bf16[512,512]{1,0:T(8,128)(2,1)S(1)} collective-permute-done((bf16[512,512]{1,0:T(8,128)(2,1)}, bf16[512,512]{1,0:T(8,128)(2,1)S(1)}, u32[]{:S(2)}, u32[]{:S(2)}) %collective-permute-start) | collective-permute-done | bytes 524320 | tf_op jit(solution)/shard_map/ppermute | solution.py:27
  23.5 1.3 collective-permute-done.1.rest_8_
  24.8 1.9 collective-permute-start.2
  26.7 5.5 %collective-permute-start.3 = (bf16[512,512]{1,0:T(8,128)(2,1)S(1)}, bf16[512,512]{1,0:T(8,128)(2,1)S(1)}, u32[]{:S(2)}, u32[]{:S(2)}) collective-permute-start(bf16[512,512]{1,0:T(8,128)(2,1)S(1)} %collective-permute-done.1.rest_8_), channel_id=1, source_target_pairs={{0,480},{16,496},{32,0},{48,16},{64,32},{80,48},{96,64},{112,80},{... | collective-permute-start | bytes 1572872 | tf_op jit(solution)/shard_map/ppermute | solution.py:27
  32.2 1.9 collective-permute-start.4
  34.2 2.4 collective-permute-start.5
  36.6 4.8 %collective-permute-done.2.rest_2_ = bf16[512,512]{1,0:T(8,128)(2,1)S(1)} collective-permute-done((bf16[512,512]{1,0:T(8,128)(2,1)S(1)}, bf16[512,512]{1,0:T(8,128)(2,1)S(1)}, u32[]{:S(2)}, u32[]{:S(2)}) %collective-permute-start.2) | collective-permute-done | bytes 524320 | tf_op jit(solution)/shard_map/ppermute | solution.py:27
  41.4 1.2 collective-permute-done.3.rest_9_
  42.6 5.6 %collective-permute-start.7 = (bf16[512,512]{1,0:T(8,128)(2,1)S(1)}, bf16[512,512]{1,0:T(8,128)(2,1)S(1)}, u32[]{:S(2)}, u32[]{:S(2)}) collective-permute-start(bf16[512,512]{1,0:T(8,128)(2,1)S(1)} %collective-permute-done.3.rest_9_), channel_id=1, source_target_pairs={{0,480},{16,496},{32,0},{48,16},{64,32},{80,48},{96,64},{112,80},{... | collective-permute-start | bytes 1572872 | tf_op jit(solution)/shard_map/ppermute | solution.py:27
  48.2 1.9 collective-permute-start.6
  50.1 1.9 collective-permute-start.8
  52.0 2.4 collective-permute-start.9
  54.4 3.2 %collective-permute-done.7.rest_10_ = bf16[512,512]{1,0:T(8,128)(2,1)S(1)} collective-permute-done((bf16[512,512]{1,0:T(8,128)(2,1)S(1)}, bf16[512,512]{1,0:T(8,128)(2,1)S(1)}, u32[]{:S(2)}, u32[]{:S(2)}) %collective-permute-start.7) | collective-permute-done | bytes 524320 | tf_op jit(solution)/shard_map/ppermute | solution.py:27
  57.6 5.3 %collective-permute-done.6.rest_3_ = bf16[512,512]{1,0:T(8,128)(2,1)S(1)} collective-permute-done((bf16[512,512]{1,0:T(8,128)(2,1)S(1)}, bf16[512,512]{1,0:T(8,128)(2,1)S(1)}, u32[]{:S(2)}, u32[]{:S(2)}) %collective-permute-start.6) | collective-permute-done | bytes 524320 | tf_op jit(solution)/shard_map/ppermute | solution.py:27
  63.0 1.9 collective-permute-start.11
  64.9 3.9 %collective-permute-start.10 = (bf16[512,512]{1,0:T(8,128)(2,1)S(1)}, bf16[512,512]{1,0:T(8,128)(2,1)}, u32[]{:S(2)}, u32[]{:S(2)}) collective-permute-start(bf16[512,512]{1,0:T(8,128)(2,1)S(1)} %collective-permute-done.6.rest_3_), channel_id=1, source_target_pairs={{0,32},{16,48},{32,64},{48,80},{64,96},{80,112},{96,128},{112,144}... | collective-permute-start | bytes 1572872 | tf_op jit(solution)/shard_map/ppermute | solution.py:27
  68.9 1.9 collective-permute-start.12
  70.8 2.4 collective-permute-start.14
  73.2 0.7 copy.16
  74.0 20.7 %all_to_all.24 = s32[32,1,1]{2,1,0:T(1,128)S(1)} all-to-all(s32[32,1,1]{2,1,0:T(1,128)S(1)} %copy.16), channel_id=1, replica_groups=mesh['dom'=32,'head'=16] {'dom'}, dimensions={0} | all-to-all | bytes 256 | tf_op jit(solution)/shard_map/all_to_all | solution.py:295
  94.6 1.2 reduce.serve_ref
  95.9 2.6 collective-permute-start.13
  98.5 4.6 %collective-permute-start.15 = (bf16[512,512]{1,0:T(8,128)(2,1)}, bf16[512,512]{1,0:T(8,128)(2,1)}, u32[]{:S(2)}, u32[]{:S(2)}) collective-permute-start(bf16[512,512]{1,0:T(8,128)(2,1)} %collective-permute-done.11.rest_11_), channel_id=1, source_target_pairs={{0,480},{16,496},{32,0},{48,16},{64,32},{80,48},{96,64},{112,80},{... | collective-permute-start | bytes 1572872 | tf_op jit(solution)/shard_map/ppermute | solution.py:27
  103.1 1.9 collective-permute-start.17
  105.0 2.4 collective-permute-start.16
  107.4 5.4 %collective-permute-done.13.rest_5_ = bf16[512,512]{1,0:T(8,128)(2,1)} collective-permute-done((bf16[512,512]{1,0:T(8,128)(2,1)}, bf16[512,512]{1,0:T(8,128)(2,1)}, u32[]{:S(2)}, u32[]{:S(2)}) %collective-permute-start.13) | collective-permute-done | bytes 524320 | tf_op jit(solution)/shard_map/ppermute | solution.py:27
  112.8 1.2 collective-permute-done.15.rest_12_
  114.0 5.6 %collective-permute-start.19 = (bf16[512,512]{1,0:T(8,128)(2,1)}, bf16[512,512]{1,0:T(8,128)(2,1)}, u32[]{:S(2)}, u32[]{:S(2)}) collective-permute-start(bf16[512,512]{1,0:T(8,128)(2,1)} %collective-permute-done.15.rest_12_), channel_id=1, source_target_pairs={{0,480},{16,496},{32,0},{48,16},{64,32},{80,48},{96,64},{112,80},{... | collective-permute-start | bytes 1572872 | tf_op jit(solution)/shard_map/ppermute | solution.py:27
  119.6 1.9 collective-permute-start.18
  121.6 1.9 collective-permute-start.22
  123.5 2.4 collective-permute-start.20
  125.9 2.6 copy.17
  128.5 1.2 collective-permute-done.19.rest_13_
  129.8 5.3 %collective-permute-done.18.rest_6_ = bf16[512,512]{1,0:T(8,128)(2,1)} collective-permute-done((bf16[512,512]{1,0:T(8,128)(2,1)}, bf16[512,512]{1,0:T(8,128)(2,1)}, u32[]{:S(2)}, u32[]{:S(2)}) %collective-permute-start.18) | collective-permute-done | bytes 524320 | tf_op jit(solution)/shard_map/ppermute | solution.py:27
  135.1 1.9 collective-permute-start.23
  137.0 3.9 %collective-permute-start.21 = (bf16[512,512]{1,0:T(8,128)(2,1)}, bf16[512,512]{1,0:T(8,128)(2,1)S(1)}, u32[]{:S(2)}, u32[]{:S(2)}) collective-permute-start(bf16[512,512]{1,0:T(8,128)(2,1)} %collective-permute-done.18.rest_6_), channel_id=1, source_target_pairs={{0,32},{16,48},{32,64},{48,80},{64,96},{80,112},{96,128},{112,144}... | collective-permute-start | bytes 1572872 | tf_op jit(solution)/shard_map/ppermute | solution.py:27
  140.9 1.9 collective-permute-start.27
  142.9 2.4 collective-permute-start.25
  145.3 1.9 collective-permute-start.24
  147.2 1.1 collective-permute-done.23.rest_14_
  148.3 3.1 %collective-permute-done.21.rest_7_ = bf16[512,512]{1,0:T(8,128)(2,1)S(1)} collective-permute-done((bf16[512,512]{1,0:T(8,128)(2,1)}, bf16[512,512]{1,0:T(8,128)(2,1)S(1)}, u32[]{:S(2)}, u32[]{:S(2)}) %collective-permute-start.21) | collective-permute-done | bytes 524320 | tf_op jit(solution)/shard_map/ppermute | solution.py:27
  151.5 1.9 collective-permute-start.30
  153.5 1.9 collective-permute-start.28
  155.4 2.4 collective-permute-start.26
  157.8 3.9 %collective-permute-start.29 = (bf16[256,512]{1,0:T(8,128)(2,1)S(1)}, bf16[256,512]{1,0:T(8,128)(2,1)}, u32[]{:S(2)}, u32[]{:S(2)}) collective-permute-start(bf16[256,512]{1,0:T(8,128)(2,1)S(1)} %slice.6), channel_id=1, source_target_pairs={{0,32},{16,48},{32,64},{48,80},{64,96},{80,112},{96,128},{112,144}... | collective-permute-start | bytes 786440 | tf_op jit(solution)/shard_map/ppermute | solution.py:27
  161.8 1.9 collective-permute-start.32
  163.7 5.6 %collective-permute-done.29.rest_30_ = bf16[256,512]{1,0:T(8,128)(2,1)} collective-permute-done((bf16[256,512]{1,0:T(8,128)(2,1)S(1)}, bf16[256,512]{1,0:T(8,128)(2,1)}, u32[]{:S(2)}, u32[]{:S(2)}) %collective-permute-start.29) | collective-permute-done | bytes 262176 | tf_op jit(solution)/shard_map/ppermute | solution.py:27
  169.3 1.9 collective-permute-start.31
  171.3 1.8 collective-permute-done.31.rest_32_
  173.1 8.4 %aggregate.1 = (bf16[512,512]{1,0:T(8,128)(2,1)}, bf16[1536,512]{1,0:T(8,128)(2,1)}) custom-call(s32[1]{0:T(128)} %bitcast.place_ref, s32[4,6]{1,0:T(4,128)} %entry_ref.1, s32[32]{0:T(128)} %reduce.serve_ref, s32[4,6,128,128]{3,2,1,0:T(8,128)} %pattern_ref.1, bf16[512,512]{1,0:T(8,128)(2,1)} %rest_0_.1, bf16[1536,512]{1,0:T(8,128)(2,1)} %bitcast.9, ...), custom_call_target="tpu_custom_call" | custom-call | tf_op jit(solution)/shard_map/aggregate/pallas_call | solution.py:155
  181.5 0.0 copy-start.20
  181.5 0.0 copy-start.21
  181.5 7.5 %all-to-all-start.1 = ((bf16[16,96,512]{2,1,0:T(8,128)(2,1)}), bf16[16,96,512]{2,1,0:T(8,128)(2,1)S(1)}, u32[]{:S(2)}, u32[]{:S(2)}) async-start(bf16[16,96,512]{2,1,0:T(8,128)(2,1)} %bitcast.10), calls=%async_computation.1 | async-start | bytes 3145728 | tf_op jit(solution)/shard_map/all_to_all | solution.py:316
  189.1 23.0 %all-to-all-done.1.qkv_ref = bf16[16,96,512]{2,1,0:T(8,128)(2,1)S(1)} async-done(((bf16[16,96,512]{2,1,0:T(8,128)(2,1)}), bf16[16,96,512]{2,1,0:T(8,128)(2,1)S(1)}, u32[]{:S(2)}, u32[]{:S(2)}) %all-to-all-start.1) | async-done | bytes 1572896 | tf_op jit(solution)/shard_map/all_to_all | solution.py:316
  212.0 2.5 broadcast_in_dim.2
  214.6 5.9 %all-to-all-start.3 = ((bf16[16,128,1024]{2,1,0:T(8,128)(2,1)}), bf16[16,128,1024]{2,1,0:T(8,128)(2,1)}, u32[]{:S(2)}, u32[]{:S(2)}) async-start(bf16[16,128,1024]{2,1,0:T(8,128)(2,1)} %broadcast_in_dim.2), calls=%async_computation.3 | async-start | bytes 8388608 | tf_op jit(solution)/shard_map/all_to_all | solution.py:301
  220.4 0.1 copy.18.key_ref
  220.5 0.0 copy-start.2
  220.5 15.7 %attend.1 = bf16[16,32,512]{2,1,0:T(8,128)(2,1)S(1)} custom-call(s32[64,8]{1,0:T(8,128)S(1)} %copy.18.key_ref, bf16[16,96,512]{2,1,0:T(8,128)(2,1)S(1)} %all-to-all-done.1.qkv_ref), custom_call_target="tpu_custom_call" | custom-call | tf_op jit(solution)/shard_map/attend/pallas_call | solution.py:220
  236.2 36.6 %all-to-all-done.3 = bf16[16,128,1024]{2,1,0:T(8,128)(2,1)} async-done(((bf16[16,128,1024]{2,1,0:T(8,128)(2,1)}), bf16[16,128,1024]{2,1,0:T(8,128)(2,1)}, u32[]{:S(2)}, u32[]{:S(2)}) %all-to-all-start.3) | async-done | bytes 4194336 | tf_op jit(solution)/shard_map/all_to_all | solution.py:301
  272.9 13.7 %all_to_all.25 = bf16[16,32,512]{2,1,0:T(8,128)(2,1)S(1)} all-to-all(bf16[16,32,512]{2,1,0:T(8,128)(2,1)S(1)} %attend.1), channel_id=1, replica_groups=mesh['dom'=32,'head'=16] {'head'}, dimensions={0} | all-to-all | bytes 1048576 | tf_op jit(solution)/shard_map/all_to_all | solution.py:320
  286.6 7.4 %finish.1 = bf16[512,512]{1,0:T(8,128)(2,1)} custom-call(bf16[512,512]{1,0:T(8,128)(2,1)S(1)} %bitcast.7, bf16[512,512]{1,0:T(8,128)(2,1)S(1)} %copy-done.1, bf16[512,512]{1,0:T(8,128)(2,1)S(1)} %copy-done, f32[1,512]{1,0:T(1,128)S(1)} %bitcast.8, bf16[2048,1024]{1,0:T(8,128)(2,1)} %bitcast.6.ffn_ref), custom_call_target="tpu_custom_call" | custom-call | tf_op jit(solution)/shard_map/finish/pallas_call | solution.py:264
  (65 shorter events, 0.2 us)
Async XLA Ops:
  0.0 23.5 %collective-permute-start = (bf16[512,512]{1,0:T(8,128)(2,1)}, bf16[512,512]{1,0:T(8,128)(2,1)S(1)}, u32[]{:S(2)}, u32[]{:S(2)}) collective-permute-start(bf16[512,512]{1,0:T(8,128)(2,1)} %rest_0_.1), channel_id=1, source_target_pairs={{0,32},{16,48},{32,64},{48,80},{64,96},{80,112},{96,128},{112,144}... | collective-permute-start | bytes 1572872 | tf_op jit(solution)/shard_map/ppermute | solution.py:27
  3.8 21.0 %collective-permute-start.1 = (bf16[512,512]{1,0:T(8,128)(2,1)}, bf16[512,512]{1,0:T(8,128)(2,1)S(1)}, u32[]{:S(2)}, u32[]{:S(2)}) collective-permute-start(bf16[512,512]{1,0:T(8,128)(2,1)} %rest_0_.1), channel_id=1, source_target_pairs={{0,480},{16,496},{32,0},{48,16},{64,32},{80,48},{96,64},{112,80},{... | collective-permute-start | bytes 1572872 | tf_op jit(solution)/shard_map/ppermute | solution.py:27
  23.5 105.0 %copy-start.6 = (bf16[512,512]{1,0:T(8,128)(2,1)}, bf16[512,512]{1,0:T(8,128)(2,1)S(1)}, u32[]{:S(2)}) copy-start(bf16[512,512]{1,0:T(8,128)(2,1)S(1)} %collective-permute-done.rest_1_) | copy-start | bytes 1572868
  24.8 103.7 %copy-start.7 = (bf16[512,512]{1,0:T(8,128)(2,1)}, bf16[512,512]{1,0:T(8,128)(2,1)S(1)}, u32[]{:S(2)}) copy-start(bf16[512,512]{1,0:T(8,128)(2,1)S(1)} %collective-permute-done.1.rest_8_) | copy-start | bytes 1572868
  24.8 16.5 %collective-permute-start.2 = (bf16[512,512]{1,0:T(8,128)(2,1)S(1)}, bf16[512,512]{1,0:T(8,128)(2,1)S(1)}, u32[]{:S(2)}, u32[]{:S(2)}) collective-permute-start(bf16[512,512]{1,0:T(8,128)(2,1)S(1)} %collective-permute-done.rest_1_), channel_id=1, source_target_pairs={{0,32},{16,48},{32,64},{48,80},{64,96},{80,112},{96,128},{112,144}... | collective-permute-start | bytes 1572872 | tf_op jit(solution)/shard_map/ppermute | solution.py:27
  26.7 15.8 %collective-permute-start.3 = (bf16[512,512]{1,0:T(8,128)(2,1)S(1)}, bf16[512,512]{1,0:T(8,128)(2,1)S(1)}, u32[]{:S(2)}, u32[]{:S(2)}) collective-permute-start(bf16[512,512]{1,0:T(8,128)(2,1)S(1)} %collective-permute-done.1.rest_8_), channel_id=1, source_target_pairs={{0,480},{16,496},{32,0},{48,16},{64,32},{80,48},{96,64},{112,80},{... | collective-permute-start | bytes 1572872 | tf_op jit(solution)/shard_map/ppermute | solution.py:27
  32.2 10.3 %collective-permute-start.4 = (bf16[512,512]{1,0:T(8,128)(2,1)S(1)}, bf16[512,512]{1,0:T(8,128)(2,1)S(1)}, u32[]{:S(2)}, u32[]{:S(2)}) collective-permute-start(bf16[512,512]{1,0:T(8,128)(2,1)S(1)} %collective-permute-done.rest_1_), channel_id=1, source_target_pairs={{0,16},{16,0},{32,48},{48,32},{64,80},{80,64},{96,112},{112,96},{1... | collective-permute-start | bytes 1572872 | tf_op jit(solution)/shard_map/ppermute | solution.py:30
  34.2 8.4 %collective-permute-start.5 = (bf16[512,512]{1,0:T(8,128)(2,1)S(1)}, bf16[512,512]{1,0:T(8,128)(2,1)S(1)}, u32[]{:S(2)}, u32[]{:S(2)}) collective-permute-start(bf16[512,512]{1,0:T(8,128)(2,1)S(1)} %collective-permute-done.1.rest_8_), channel_id=1, source_target_pairs={{0,16},{16,0},{32,48},{48,32},{64,80},{80,64},{96,112},{112,96},{1... | collective-permute-start | bytes 1572872 | tf_op jit(solution)/shard_map/ppermute | solution.py:30
  41.4 87.2 %copy-start.8 = (bf16[512,512]{1,0:T(8,128)(2,1)}, bf16[512,512]{1,0:T(8,128)(2,1)S(1)}, u32[]{:S(2)}) copy-start(bf16[512,512]{1,0:T(8,128)(2,1)S(1)} %collective-permute-done.2.rest_2_) | copy-start | bytes 1572868
  42.5 20.4 %copy-start.9 = (bf16[512,512]{1,0:T(8,128)(2,1)}, bf16[512,512]{1,0:T(8,128)(2,1)S(1)}, u32[]{:S(2)}) copy-start(bf16[512,512]{1,0:T(8,128)(2,1)S(1)} %collective-permute-done.3.rest_9_) | copy-start | bytes 1572868
  42.5 20.4 %copy-start.10 = (bf16[512,512]{1,0:T(8,128)(2,1)}, bf16[512,512]{1,0:T(8,128)(2,1)S(1)}, u32[]{:S(2)}) copy-start(bf16[512,512]{1,0:T(8,128)(2,1)S(1)} %collective-permute-done.4.rest_16_) | copy-start | bytes 1572868
  42.5 22.4 %copy-start.11 = (bf16[512,512]{1,0:T(8,128)(2,1)}, bf16[512,512]{1,0:T(8,128)(2,1)S(1)}, u32[]{:S(2)}) copy-start(bf16[512,512]{1,0:T(8,128)(2,1)S(1)} %collective-permute-done.5.rest_23_) | copy-start | bytes 1572868
  42.6 15.1 %collective-permute-start.7 = (bf16[512,512]{1,0:T(8,128)(2,1)S(1)}, bf16[512,512]{1,0:T(8,128)(2,1)S(1)}, u32[]{:S(2)}, u32[]{:S(2)}) collective-permute-start(bf16[512,512]{1,0:T(8,128)(2,1)S(1)} %collective-permute-done.3.rest_9_), channel_id=1, source_target_pairs={{0,480},{16,496},{32,0},{48,16},{64,32},{80,48},{96,64},{112,80},{... | collective-permute-start | bytes 1572872 | tf_op jit(solution)/shard_map/ppermute | solution.py:27
  48.2 14.8 %collective-permute-start.6 = (bf16[512,512]{1,0:T(8,128)(2,1)S(1)}, bf16[512,512]{1,0:T(8,128)(2,1)S(1)}, u32[]{:S(2)}, u32[]{:S(2)}) collective-permute-start(bf16[512,512]{1,0:T(8,128)(2,1)S(1)} %collective-permute-done.2.rest_2_), channel_id=1, source_target_pairs={{0,32},{16,48},{32,64},{48,80},{64,96},{80,112},{96,128},{112,144}... | collective-permute-start | bytes 1572872 | tf_op jit(solution)/shard_map/ppermute | solution.py:27
  50.1 12.9 %collective-permute-start.8 = (bf16[512,512]{1,0:T(8,128)(2,1)S(1)}, bf16[512,512]{1,0:T(8,128)(2,1)S(1)}, u32[]{:S(2)}, u32[]{:S(2)}) collective-permute-start(bf16[512,512]{1,0:T(8,128)(2,1)S(1)} %collective-permute-done.2.rest_2_), channel_id=1, source_target_pairs={{0,16},{16,0},{32,48},{48,32},{64,80},{80,64},{96,112},{112,96},{1... | collective-permute-start | bytes 1572872 | tf_op jit(solution)/shard_map/ppermute | solution.py:30
  52.0 10.9 %collective-permute-start.9 = (bf16[512,512]{1,0:T(8,128)(2,1)S(1)}, bf16[512,512]{1,0:T(8,128)(2,1)S(1)}, u32[]{:S(2)}, u32[]{:S(2)}) collective-permute-start(bf16[512,512]{1,0:T(8,128)(2,1)S(1)} %collective-permute-done.3.rest_9_), channel_id=1, source_target_pairs={{0,16},{16,0},{32,48},{48,32},{64,80},{80,64},{96,112},{112,96},{1... | collective-permute-start | bytes 1572872 | tf_op jit(solution)/shard_map/ppermute | solution.py:30
  57.6 70.9 %copy-start.12 = (bf16[512,512]{1,0:T(8,128)(2,1)}, bf16[512,512]{1,0:T(8,128)(2,1)S(1)}, u32[]{:S(2)}) copy-start(bf16[512,512]{1,0:T(8,128)(2,1)S(1)} %collective-permute-done.7.rest_10_) | copy-start | bytes 1572868
  62.9 65.6 %copy-start.13 = (bf16[512,512]{1,0:T(8,128)(2,1)}, bf16[512,512]{1,0:T(8,128)(2,1)S(1)}, u32[]{:S(2)}) copy-start(bf16[512,512]{1,0:T(8,128)(2,1)S(1)} %collective-permute-done.6.rest_3_) | copy-start | bytes 1572868
  63.0 5.9 %copy-start.14 = (bf16[512,512]{1,0:T(8,128)(2,1)}, bf16[512,512]{1,0:T(8,128)(2,1)S(1)}, u32[]{:S(2)}) copy-start(bf16[512,512]{1,0:T(8,128)(2,1)S(1)} %collective-permute-done.8.rest_17_) | copy-start | bytes 1572868
  63.0 7.8 %copy-start.15 = (bf16[512,512]{1,0:T(8,128)(2,1)}, bf16[512,512]{1,0:T(8,128)(2,1)S(1)}, u32[]{:S(2)}) copy-start(bf16[512,512]{1,0:T(8,128)(2,1)S(1)} %collective-permute-done.9.rest_24_) | copy-start | bytes 1572868
  63.0 32.9 %collective-permute-start.11 = (bf16[512,512]{1,0:T(8,128)(2,1)S(1)}, bf16[512,512]{1,0:T(8,128)(2,1)}, u32[]{:S(2)}, u32[]{:S(2)}) collective-permute-start(bf16[512,512]{1,0:T(8,128)(2,1)S(1)} %collective-permute-done.7.rest_10_), channel_id=1, source_target_pairs={{0,480},{16,496},{32,0},{48,16},{64,32},{80,48},{96,64},{112,80},{... | collective-permute-start | bytes 1572872 | tf_op jit(solution)/shard_map/ppermute | solution.py:27
  64.9 30.9 %collective-permute-start.10 = (bf16[512,512]{1,0:T(8,128)(2,1)S(1)}, bf16[512,512]{1,0:T(8,128)(2,1)}, u32[]{:S(2)}, u32[]{:S(2)}) collective-permute-start(bf16[512,512]{1,0:T(8,128)(2,1)S(1)} %collective-permute-done.6.rest_3_), channel_id=1, source_target_pairs={{0,32},{16,48},{32,64},{48,80},{64,96},{80,112},{96,128},{112,144}... | collective-permute-start | bytes 1572872 | tf_op jit(solution)/shard_map/ppermute | solution.py:27
  68.9 27.0 %collective-permute-start.12 = (bf16[512,512]{1,0:T(8,128)(2,1)S(1)}, bf16[512,512]{1,0:T(8,128)(2,1)}, u32[]{:S(2)}, u32[]{:S(2)}) collective-permute-start(bf16[512,512]{1,0:T(8,128)(2,1)S(1)} %collective-permute-done.6.rest_3_), channel_id=1, source_target_pairs={{0,16},{16,0},{32,48},{48,32},{64,80},{80,64},{96,112},{112,96},{1... | collective-permute-start | bytes 1572872 | tf_op jit(solution)/shard_map/ppermute | solution.py:30
  70.8 27.7 %collective-permute-start.14 = (bf16[512,512]{1,0:T(8,128)(2,1)S(1)}, bf16[512,512]{1,0:T(8,128)(2,1)}, u32[]{:S(2)}, u32[]{:S(2)}) collective-permute-start(bf16[512,512]{1,0:T(8,128)(2,1)S(1)} %collective-permute-done.7.rest_10_), channel_id=1, source_target_pairs={{0,16},{16,0},{32,48},{48,32},{64,80},{80,64},{96,112},{112,96},{1... | collective-permute-start | bytes 1572872 | tf_op jit(solution)/shard_map/ppermute | solution.py:30
  95.8 49.4 %copy-start.3 = (bf16[512,512]{1,0:T(8,128)(2,1)S(1)}, bf16[512,512]{1,0:T(8,128)(2,1)}, u32[]{:S(2)}) copy-start(bf16[512,512]{1,0:T(8,128)(2,1)} %rest_0_.1) | copy-start | bytes 1572868
  95.9 17.0 %collective-permute-start.13 = (bf16[512,512]{1,0:T(8,128)(2,1)}, bf16[512,512]{1,0:T(8,128)(2,1)}, u32[]{:S(2)}, u32[]{:S(2)}) collective-permute-start(bf16[512,512]{1,0:T(8,128)(2,1)} %collective-permute-done.10.rest_4_), channel_id=1, source_target_pairs={{0,32},{16,48},{32,64},{48,80},{64,96},{80,112},{96,128},{112,144}... | collective-permute-start | bytes 1572872 | tf_op jit(solution)/shard_map/ppermute | solution.py:27
  98.5 15.5 %collective-permute-start.15 = (bf16[512,512]{1,0:T(8,128)(2,1)}, bf16[512,512]{1,0:T(8,128)(2,1)}, u32[]{:S(2)}, u32[]{:S(2)}) collective-permute-start(bf16[512,512]{1,0:T(8,128)(2,1)} %collective-permute-done.11.rest_11_), channel_id=1, source_target_pairs={{0,480},{16,496},{32,0},{48,16},{64,32},{80,48},{96,64},{112,80},{... | collective-permute-start | bytes 1572872 | tf_op jit(solution)/shard_map/ppermute | solution.py:27
  103.1 11.0 %collective-permute-start.17 = (bf16[512,512]{1,0:T(8,128)(2,1)}, bf16[512,512]{1,0:T(8,128)(2,1)}, u32[]{:S(2)}, u32[]{:S(2)}) collective-permute-start(bf16[512,512]{1,0:T(8,128)(2,1)} %collective-permute-done.11.rest_11_), channel_id=1, source_target_pairs={{0,16},{16,0},{32,48},{48,32},{64,80},{80,64},{96,112},{112,96},{1... | collective-permute-start | bytes 1572872 | tf_op jit(solution)/shard_map/ppermute | solution.py:30
  105.0 9.0 %collective-permute-start.16 = (bf16[512,512]{1,0:T(8,128)(2,1)}, bf16[512,512]{1,0:T(8,128)(2,1)}, u32[]{:S(2)}, u32[]{:S(2)}) collective-permute-start(bf16[512,512]{1,0:T(8,128)(2,1)} %collective-permute-done.10.rest_4_), channel_id=1, source_target_pairs={{0,16},{16,0},{32,48},{48,32},{64,80},{80,64},{96,112},{112,96},{1... | collective-permute-start | bytes 1572872 | tf_op jit(solution)/shard_map/ppermute | solution.py:30
  114.0 15.7 %collective-permute-start.19 = (bf16[512,512]{1,0:T(8,128)(2,1)}, bf16[512,512]{1,0:T(8,128)(2,1)}, u32[]{:S(2)}, u32[]{:S(2)}) collective-permute-start(bf16[512,512]{1,0:T(8,128)(2,1)} %collective-permute-done.15.rest_12_), channel_id=1, source_target_pairs={{0,480},{16,496},{32,0},{48,16},{64,32},{80,48},{96,64},{112,80},{... | collective-permute-start | bytes 1572872 | tf_op jit(solution)/shard_map/ppermute | solution.py:27
  119.6 15.4 %collective-permute-start.18 = (bf16[512,512]{1,0:T(8,128)(2,1)}, bf16[512,512]{1,0:T(8,128)(2,1)}, u32[]{:S(2)}, u32[]{:S(2)}) collective-permute-start(bf16[512,512]{1,0:T(8,128)(2,1)} %collective-permute-done.13.rest_5_), channel_id=1, source_target_pairs={{0,32},{16,48},{32,64},{48,80},{64,96},{80,112},{96,128},{112,144}... | collective-permute-start | bytes 1572872 | tf_op jit(solution)/shard_map/ppermute | solution.py:27
  121.6 13.5 %collective-permute-start.22 = (bf16[512,512]{1,0:T(8,128)(2,1)}, bf16[512,512]{1,0:T(8,128)(2,1)}, u32[]{:S(2)}, u32[]{:S(2)}) collective-permute-start(bf16[512,512]{1,0:T(8,128)(2,1)} %collective-permute-done.15.rest_12_), channel_id=1, source_target_pairs={{0,16},{16,0},{32,48},{48,32},{64,80},{80,64},{96,112},{112,96},{1... | collective-permute-start | bytes 1572872 | tf_op jit(solution)/shard_map/ppermute | solution.py:30
  123.5 13.5 %collective-permute-start.20 = (bf16[512,512]{1,0:T(8,128)(2,1)}, bf16[512,512]{1,0:T(8,128)(2,1)}, u32[]{:S(2)}, u32[]{:S(2)}) collective-permute-start(bf16[512,512]{1,0:T(8,128)(2,1)} %collective-permute-done.13.rest_5_), channel_id=1, source_target_pairs={{0,16},{16,0},{32,48},{48,32},{64,80},{80,64},{96,112},{112,96},{1... | collective-permute-start | bytes 1572872 | tf_op jit(solution)/shard_map/ppermute | solution.py:30
  135.1 13.3 %collective-permute-start.23 = (bf16[512,512]{1,0:T(8,128)(2,1)}, bf16[512,512]{1,0:T(8,128)(2,1)S(1)}, u32[]{:S(2)}, u32[]{:S(2)}) collective-permute-start(bf16[512,512]{1,0:T(8,128)(2,1)} %collective-permute-done.19.rest_13_), channel_id=1, source_target_pairs={{0,480},{16,496},{32,0},{48,16},{64,32},{80,48},{96,64},{112,80},{... | collective-permute-start | bytes 1572872 | tf_op jit(solution)/shard_map/ppermute | solution.py:27
  137.0 14.5 %collective-permute-start.21 = (bf16[512,512]{1,0:T(8,128)(2,1)}, bf16[512,512]{1,0:T(8,128)(2,1)S(1)}, u32[]{:S(2)}, u32[]{:S(2)}) collective-permute-start(bf16[512,512]{1,0:T(8,128)(2,1)} %collective-permute-done.18.rest_6_), channel_id=1, source_target_pairs={{0,32},{16,48},{32,64},{48,80},{64,96},{80,112},{96,128},{112,144}... | collective-permute-start | bytes 1572872 | tf_op jit(solution)/shard_map/ppermute | solution.py:27
  140.9 10.6 %collective-permute-start.27 = (bf16[512,512]{1,0:T(8,128)(2,1)}, bf16[512,512]{1,0:T(8,128)(2,1)S(1)}, u32[]{:S(2)}, u32[]{:S(2)}) collective-permute-start(bf16[512,512]{1,0:T(8,128)(2,1)} %collective-permute-done.19.rest_13_), channel_id=1, source_target_pairs={{0,16},{16,0},{32,48},{48,32},{64,80},{80,64},{96,112},{112,96},{1... | collective-permute-start | bytes 1572872 | tf_op jit(solution)/shard_map/ppermute | solution.py:30
  142.9 10.6 %collective-permute-start.25 = (bf16[512,512]{1,0:T(8,128)(2,1)}, bf16[512,512]{1,0:T(8,128)(2,1)S(1)}, u32[]{:S(2)}, u32[]{:S(2)}) collective-permute-start(bf16[512,512]{1,0:T(8,128)(2,1)} %collective-permute-done.18.rest_6_), channel_id=1, source_target_pairs={{0,16},{16,0},{32,48},{48,32},{64,80},{80,64},{96,112},{112,96},{1... | collective-permute-start | bytes 1572872 | tf_op jit(solution)/shard_map/ppermute | solution.py:30
  145.3 25.9 %collective-permute-start.24 = (bf16[512,512]{1,0:T(8,128)(2,1)S(1)}, bf16[512,512]{1,0:T(8,128)(2,1)S(1)}, u32[]{:S(2)}, u32[]{:S(2)}) collective-permute-start(bf16[512,512]{1,0:T(8,128)(2,1)S(1)} %copy-done.3), channel_id=1, source_target_pairs={{0,16},{16,0},{32,48},{48,32},{64,80},{80,64},{96,112},{112,96},{1... | collective-permute-start | bytes 1572872 | tf_op jit(solution)/shard_map/ppermute | solution.py:30
  148.3 24.7 %copy-start.4 = (bf16[512,512]{1,0:T(8,128)(2,1)}, bf16[512,512]{1,0:T(8,128)(2,1)S(1)}, u32[]{:S(2)}) copy-start(bf16[512,512]{1,0:T(8,128)(2,1)S(1)} %collective-permute-done.23.rest_14_) | copy-start | bytes 1572868
  151.5 21.6 %copy-start.5 = (bf16[512,512]{1,0:T(8,128)(2,1)}, bf16[512,512]{1,0:T(8,128)(2,1)S(1)}, u32[]{:S(2)}) copy-start(bf16[512,512]{1,0:T(8,128)(2,1)S(1)} %collective-permute-done.21.rest_7_) | copy-start | bytes 1572868
  151.5 21.5 %copy-start.16 = (bf16[512,512]{1,0:T(8,128)(2,1)}, bf16[512,512]{1,0:T(8,128)(2,1)S(1)}, u32[]{:S(2)}) copy-start(bf16[512,512]{1,0:T(8,128)(2,1)S(1)} %collective-permute-done.27.rest_28_) | copy-start | bytes 1572868
  151.5 10.3 %collective-permute-start.30 = (bf16[256,512]{1,0:T(8,128)(2,1)S(1)}, bf16[256,512]{1,0:T(8,128)(2,1)S(1)}, u32[]{:S(2)}, u32[]{:S(2)}) collective-permute-start(bf16[256,512]{1,0:T(8,128)(2,1)S(1)} %slice.7), channel_id=1, source_target_pairs={{0,480},{16,496},{32,0},{48,16},{64,32},{80,48},{96,64},{112,80},{... | collective-permute-start | bytes 786440 | tf_op jit(solution)/shard_map/ppermute | solution.py:27
  153.5 19.6 %copy-start.17 = (bf16[512,512]{1,0:T(8,128)(2,1)}, bf16[512,512]{1,0:T(8,128)(2,1)S(1)}, u32[]{:S(2)}) copy-start(bf16[512,512]{1,0:T(8,128)(2,1)S(1)} %collective-permute-done.25.rest_21_) | copy-start | bytes 1572868
  153.5 17.7 %collective-permute-start.28 = (bf16[512,512]{1,0:T(8,128)(2,1)S(1)}, bf16[512,512]{1,0:T(8,128)(2,1)}, u32[]{:S(2)}, u32[]{:S(2)}) collective-permute-start(bf16[512,512]{1,0:T(8,128)(2,1)S(1)} %collective-permute-done.23.rest_14_), channel_id=1, source_target_pairs={{0,16},{16,0},{32,48},{48,32},{64,80},{80,64},{96,112},{112,96},{1... | collective-permute-start | bytes 1572872 | tf_op jit(solution)/shard_map/ppermute | solution.py:30
  155.4 15.8 %collective-permute-start.26 = (bf16[512,512]{1,0:T(8,128)(2,1)S(1)}, bf16[512,512]{1,0:T(8,128)(2,1)}, u32[]{:S(2)}, u32[]{:S(2)}) collective-permute-start(bf16[512,512]{1,0:T(8,128)(2,1)S(1)} %collective-permute-done.21.rest_7_), channel_id=1, source_target_pairs={{0,16},{16,0},{32,48},{48,32},{64,80},{80,64},{96,112},{112,96},{1... | collective-permute-start | bytes 1572872 | tf_op jit(solution)/shard_map/ppermute | solution.py:30
  157.8 11.4 %collective-permute-start.29 = (bf16[256,512]{1,0:T(8,128)(2,1)S(1)}, bf16[256,512]{1,0:T(8,128)(2,1)}, u32[]{:S(2)}, u32[]{:S(2)}) collective-permute-start(bf16[256,512]{1,0:T(8,128)(2,1)S(1)} %slice.6), channel_id=1, source_target_pairs={{0,32},{16,48},{32,64},{48,80},{64,96},{80,112},{96,128},{112,144}... | collective-permute-start | bytes 786440 | tf_op jit(solution)/shard_map/ppermute | solution.py:27
  161.8 11.3 %copy-start.19 = (bf16[256,512]{1,0:T(8,128)(2,1)}, bf16[256,512]{1,0:T(8,128)(2,1)S(1)}, u32[]{:S(2)}) copy-start(bf16[256,512]{1,0:T(8,128)(2,1)S(1)} %collective-permute-done.30.rest_31_) | copy-start | bytes 786436
  161.8 9.4 %collective-permute-start.32 = (bf16[256,512]{1,0:T(8,128)(2,1)S(1)}, bf16[256,512]{1,0:T(8,128)(2,1)}, u32[]{:S(2)}, u32[]{:S(2)}) collective-permute-start(bf16[256,512]{1,0:T(8,128)(2,1)S(1)} %collective-permute-done.30.rest_31_), channel_id=1, source_target_pairs={{0,16},{16,0},{32,48},{48,32},{64,80},{80,64},{96,112},{112,96},{1... | collective-permute-start | bytes 786440 | tf_op jit(solution)/shard_map/ppermute | solution.py:30
  169.3 3.8 %collective-permute-start.31 = (bf16[256,512]{1,0:T(8,128)(2,1)}, bf16[256,512]{1,0:T(8,128)(2,1)}, u32[]{:S(2)}, u32[]{:S(2)}) collective-permute-start(bf16[256,512]{1,0:T(8,128)(2,1)} %collective-permute-done.29.rest_30_), channel_id=1, source_target_pairs={{0,16},{16,0},{32,48},{48,32},{64,80},{80,64},{96,112},{112,96},{1... | collective-permute-start | bytes 786440 | tf_op jit(solution)/shard_map/ppermute | solution.py:30
  171.2 1.9 copy-start.18
  181.5 7.6 %copy-start.20 = (bf16[128,512]{1,0:T(8,128)(2,1)S(1)}, bf16[128,512]{1,0:T(8,128)(2,1)}, u32[]{:S(2)}) copy-start(bf16[128,512]{1,0:T(8,128)(2,1)} %param.19) | copy-start | bytes 393220
  181.5 7.6 %copy-start.21 = (bf16[128,512]{1,0:T(8,128)(2,1)S(1)}, bf16[128,512]{1,0:T(8,128)(2,1)}, u32[]{:S(2)}) copy-start(bf16[128,512]{1,0:T(8,128)(2,1)} %param.18) | copy-start | bytes 393220
  181.5 30.5 %all-to-all-start.1 = ((bf16[16,96,512]{2,1,0:T(8,128)(2,1)}), bf16[16,96,512]{2,1,0:T(8,128)(2,1)S(1)}, u32[]{:S(2)}, u32[]{:S(2)}) async-start(bf16[16,96,512]{2,1,0:T(8,128)(2,1)} %bitcast.10), calls=%async_computation.1 | async-start | bytes 3145728 | tf_op jit(solution)/shard_map/all_to_all | solution.py:316
  214.6 5.9 %copy-start.22 = (s32[64,8]{0,1:T(8,128)S(1)}, s32[64,8]{0,1:T(8,128)}, u32[]{:S(2)}) copy-start(s32[64,8]{0,1:T(8,128)} %param.14) | copy-start | bytes 6148
  214.6 58.3 %all-to-all-start.3 = ((bf16[16,128,1024]{2,1,0:T(8,128)(2,1)}), bf16[16,128,1024]{2,1,0:T(8,128)(2,1)}, u32[]{:S(2)}, u32[]{:S(2)}) async-start(bf16[16,128,1024]{2,1,0:T(8,128)(2,1)} %broadcast_in_dim.2), calls=%async_computation.3 | async-start | bytes 8388608 | tf_op jit(solution)/shard_map/all_to_all | solution.py:301
  220.5 66.1 %copy-start = (bf16[512,512]{1,0:T(8,128)(2,1)S(1)}, bf16[512,512]{1,0:T(8,128)(2,1)}, u32[]{:S(2)}) copy-start(bf16[512,512]{1,0:T(8,128)(2,1)} %attn_ref.1) | copy-start | bytes 1572868
  220.5 66.1 %copy-start.1 = (bf16[512,512]{1,0:T(8,128)(2,1)S(1)}, bf16[512,512]{1,0:T(8,128)(2,1)}, u32[]{:S(2)}) copy-start(bf16[512,512]{1,0:T(8,128)(2,1)} %get-tuple-element.114.agg_ref) | copy-start | bytes 1572868
  220.5 66.0 %copy-start.2 = (f32[512]{0:T(512)S(1)}, f32[512]{0:T(512)}, u32[]{:S(2)}) copy-start(f32[512]{0:T(512)} %param.17) | copy-start | bytes 6148
where the time goes:
time: 295 us; the launch traced here: 294 us
  starting transfers between devices  110 us (37%)
  waiting for transfers between devices  110 us (37%)
  blocking collectives  34.4 us (12%)
  Pallas kernels  31.5 us (11%)
  local copies, waits for them, and re-layouts  6.08 us (2%)
    ppermute x16, starting transfers between devices, send(): return lax.ppermute(v, 'dom', [(i, (i + by) % n) for i in range(n)])  60.5 us
    ppermute x16, waiting for transfers between devices, send(): return lax.ppermute(v, 'dom', [(i, (i + by) % n) for i in range(n)])  48.9 us
    all_to_all x1, waiting for transfers between devices, gather_ffn(): lax.all_to_all(jnp.broadcast_to(both[None], (n_head,) + both.shape), 'hea...  36.6 us
    ppermute x17, starting transfers between devices, trade(): return lax.ppermute(v, 'dom', [(i, i ^ 1) for i in range(n)])  36 us
    all_to_all x1, waiting for transfers between devices, shards(): lax.all_to_all(qkv_t.reshape(n_head, 3 * HDIM, rows), 'head', split_axis=...  23 us
    all_to_all x1, blocking collectives, exchange_lists(): lax.all_to_all(lists.reshape(n_dom, 1), 'dom', split_axis=0, concat_axis=...  20.7 us
    pallas_call x1, Pallas kernels, attend(): pl.pallas_call(attend_kernel, out_shape=jax.ShapeDtypeStruct((sources, HD...  15.7 us
    all_to_all x1, blocking collectives, shards(): lax.all_to_all(context, 'head', split_axis=0, concat_axis=0, tiled=True)  13.7 us
  transfers between devices with their start and end apart: 35, of which 16 were waited for; matrix products, arithmetic and copies ran while one was open for 2% of the time, Pallas kernels for 5%

commit v1 on v0

--- a/solution.py
+++ b/solution.py
@@ -1,3 +1,4 @@
+import functools
 import math
 
 import jax
@@ -17,9 +18,56 @@
 EXP2_SCALE = math.log2(math.e) / math.sqrt(HDIM)
 
 
-def ring_pieces(x, jobs):
-    results = [None] * len(jobs)
-    n = lax.axis_size("dom")
+def pick_kernel(steps, place_ref, wanted_ref, *refs):
+    pieces, out_ref, sems = refs[:-2], refs[-2], refs[-1]
+    n = wanted_ref.shape[0]
+    core, z = place_ref[0] % 2, place_ref[0] // 2
+    chips = n // 2
+
+    def copy_of(i, piece, block):
+        rows = pl.ds(pl.multiple_of(block * BLOCK, BLOCK), BLOCK)
+        return pltpu.make_async_copy(
+            piece.at[rows, :], out_ref.at[pl.ds(i * BLOCK, BLOCK), :], sems.at[i]
+        )
+
+    def wanted(step):
+        return wanted_ref[2 * ((z + chips - step) % chips) + core]
+
+    if len(steps) < len(pieces):
+        block, first = wanted(steps[0]), pieces[0].shape[0] // BLOCK
+
+        @pl.when(block < first)
+        def _():
+            copy_of(0, pieces[0], block).start()
+
+        @pl.when(block >= first)
+        def _():
+            copy_of(0, pieces[1], block - first).start()
+
+        copy_of(0, pieces[0], 0).wait()
+        return
+    copies = [copy_of(i, pieces[i], wanted(step)) for i, step in enumerate(steps)]
+    for copy in copies:
+        copy.start()
+    for copy in copies:
+        copy.wait()
+
+
+def pick(place, wanted, pieces, steps):
+    width = pieces[0].shape[1]
+    return pl.pallas_call(
+        functools.partial(pick_kernel, steps),
+        out_shape=jax.ShapeDtypeStruct((len(steps) * BLOCK, width), jnp.bfloat16),
+        in_specs=[SM, SM] + [pl.BlockSpec(memory_space=pl.ANY)] * len(pieces),
+        out_specs=VM,
+        scratch_shapes=[pltpu.SemaphoreType.DMA((len(steps),))],
+        compiler_params=pltpu.CompilerParams(vmem_limit_bytes=2 << 20),
+        name="pick",
+    )(place, wanted, *pieces)
+
+
+def ring_pieces(x, place, lists, weights):
+    n, n_head = lax.axis_size("dom"), lax.axis_size("head")
     half = n // 4
     cut = x.shape[0] // 2
 
@@ -29,40 +77,45 @@
     def trade(v):
         return lax.ppermute(v, "dom", [(i, i ^ 1) for i in range(n)])
 
-    up, down = [x], [x]
-    up_t, down_t = [trade(x)], []
+    up, down, traded = [x], [x], []
+    served = ffn = None
     for k in range(1, half + 1):
         u_in, d_in = lax.optimization_barrier((up[-1], down[-1]))
-        for i, (_, last, _, _) in enumerate(jobs):
-            if k == last:
-                u_in, results[i] = lax.optimization_barrier((u_in, results[i]))
         if k == half:
             u_in, d_in = u_in[:cut], d_in[cut:]
-        if k >= 3:
-            u_in, up_t[k - 2] = lax.optimization_barrier((u_in, up_t[k - 2]))
-            d_in, down_t[k - 3] = lax.optimization_barrier((d_in, down_t[k - 3]))
+        if k >= 4:
+            u_in, d_in, traded[k - 3] = lax.optimization_barrier((u_in, d_in, traded[k - 3]))
         up.append(send(u_in, 2))
         down.append(send(d_in, -2))
-        up_t.append(trade(up[-1]))
-        down_t.append(trade(down[-1]))
-        for i, (first, _, work, operand) in enumerate(jobs):
-            if k == first:
-                up_t[-1], down_t[-1], operand = lax.optimization_barrier(
-                    (up_t[-1], down_t[-1], operand)
-                )
-                results[i] = work(operand)
-    whole = up[:half] + down[1:half] + up_t[:half] + down_t[: half - 1]
-    return whole + [up[half], down[half], up_t[half], down_t[half - 1]], results
-
-
-def piece_sources(d, n):
-    core, z = d % 2, d // 2
-    chips, half = n // 2, n // 4
-    up = [2 * ((z + chips - k) % chips) + core for k in range(half + 1)]
-    down = [2 * ((z + k) % chips) + core for k in range(half + 1)]
-    near = up[:half] + down[1:half]
-    flip = 1 - 2 * core
-    return near + [p + flip for p in near] + [up[half], up[half] + flip]
+        if k == 1:
+            mine = lists.reshape(n)
+            swapped = mine.reshape(n // 2, 2)[:, ::-1].reshape(n)
+            served = lax.all_to_all(
+                jnp.stack([mine, swapped], axis=1),
+                "dom", split_axis=0, concat_axis=0, tiled=True,
+            )
+            served, wanted = served[:, 0], served[:, 1]
+        if k == 2:
+            traded.append(trade(pick(place, wanted, [x], [0])))
+        if k == 3:
+            both = jnp.concatenate(weights, axis=1)
+            both, traded[0] = lax.optimization_barrier((both, traded[0]))
+            ffn = lax.all_to_all(
+                jnp.broadcast_to(both[None], (n_head,) + both.shape),
+                "head", split_axis=0, concat_axis=0, tiled=True,
+            )
+        if k == half:
+            last = pick(place, wanted, [up[-1], down[-1]], [half])
+            traded.append(trade(last))
+        elif k >= 2:
+            if k == 2:
+                traded.append(trade(pick(place, wanted, [up[1], down[1]], [1, n // 2 - 1])))
+            pair = pick(place, wanted, [up[k], down[k]], [k, n // 2 - k])
+            if k == half - 1:
+                pair, ffn = lax.optimization_barrier((pair, ffn))
+            traded.append(trade(pair))
+    ffn = ffn.reshape(-1, ffn.shape[-1])
+    return up[:half] + down[1:half], [up[half], down[half]], traded, served, ffn
 
 
 def slot_of_entry(e, d, blocks, n):
@@ -70,43 +123,53 @@
     core, z = d % 2, d // 2
     chips, half = n // 2, n // 4
     k = (z + chips - p // 2) % chips
-    other = jnp.where((p % 2) == core, 0, 1)
+    other = jnp.where((p % 2) == core, 0, chips)
     near = jnp.where(k < half, k, half - 1 + chips - k)
-    piece = jnp.where(k == half, 2 * (2 * half - 1) + other, near + other * (2 * half - 1))
-    return jnp.where(e < blocks, e, blocks + piece)
+    near = jnp.where(k == half, chips - 1, near)
+    return jnp.where(e < blocks, e, blocks + other + near)
 
 
 def aggregate_kernel(place_ref, entry_ref, serve_ref, pattern_ref, own_ref, wt_ref, *rest):
     pieces, (agg_ref, qkv_ref, table, sems) = rest[:-4], rest[-4:]
     blocks, tiles = pattern_ref.shape[0], pattern_ref.shape[1]
-    whole, halves = pieces[:-4], pieces[-4:]
-    n_dom = len(pieces) - 2
+    n_dom = serve_ref.shape[0]
+    chips, half = n_dom // 2, n_dom // 4
+    whole, halves, traded = pieces[: chips - 1], pieces[chips - 1 : chips + 1], pieces[chips + 1 :]
     d = place_ref[0]
-    sources = piece_sources(d, n_dom)
+    core, z = d % 2, d // 2
     copies = []
 
-    def copy_of(i, piece, block):
-        start = pl.multiple_of(block * BLOCK, BLOCK)
+    def copy_of(slot, piece, block):
+        rows = pl.ds(pl.multiple_of(block * BLOCK, BLOCK), BLOCK)
         return pltpu.make_async_copy(
-            piece.at[pl.ds(start, BLOCK), :], table.at[blocks + i], sems.at[i]
+            piece.at[rows, :], table.at[blocks + slot], sems.at[slot]
         )
 
-    for i, piece in enumerate(whole):
-        copies.append(copy_of(i, piece, serve_ref[sources[i]]))
+    def served(step):
+        return serve_ref[2 * ((z + chips - step) % chips) + core]
+
+    steps = list(range(half)) + [chips - k for k in range(1, half)]
+    for slot, (piece, step) in enumerate(zip(whole, steps)):
+        copies.append(copy_of(slot, piece, served(step)))
         copies[-1].start()
-    for i in range(2):
-        slot, first = len(whole) + i, blocks // 2
-        block = serve_ref[sources[slot]]
-
-        @pl.when(block < first)
-        def _(slot=slot, piece=halves[2 * i], block=block):
-            copy_of(slot, piece, block).start()
-
-        @pl.when(block >= first)
-        def _(slot=slot, piece=halves[2 * i + 1], block=block - first):
-            copy_of(slot, piece, block).start()
-
-        copies.append(copy_of(slot, halves[2 * i], 0))
+    slot, first = chips - 1, blocks // 2
+    block = served(half)
+
+    @pl.when(block < first)
+    def _():
+        copy_of(slot, halves[0], block).start()
+
+    @pl.when(block >= first)
+    def _():
+        copy_of(slot, halves[1], block - first).start()
+
+    copies.append(copy_of(slot, halves[0], 0))
+    handed = [(chips, traded[0], 0)]
+    for k in range(1, half):
+        handed += [(chips + k, traded[k], 0), (chips + half - 1 + k, traded[k], 1)]
+    for slot, piece, block in handed + [(n_dom - 1, traded[half], 0)]:
+        copies.append(copy_of(slot, piece, block))
+        copies[-1].start()
     for b in range(blocks):
         table[b] = own_ref[b * BLOCK : (b + 1) * BLOCK, :]
     for copy in copies:
@@ -161,8 +224,8 @@
         in_specs=[SM, SM, SM, VM, VM, VM] + [FAR] * len(pieces),
         out_specs=(VM, VM),
         scratch_shapes=[
-            pltpu.VMEM((blocks + len(pieces) - 2, BLOCK, width), jnp.bfloat16),
-            pltpu.SemaphoreType.DMA((len(pieces) - 2,)),
+            pltpu.VMEM((blocks + serve.shape[0], BLOCK, width), jnp.bfloat16),
+            pltpu.SemaphoreType.DMA((serve.shape[0],)),
         ],
         name="aggregate",
     )(place, entries, serve, pattern, own, weight_t, *pieces)
@@ -287,31 +350,17 @@
     expand_weight,
     reduce_weight,
 ):
-    n_dom, n_head = lax.axis_size("dom"), lax.axis_size("head")
+    n_head = lax.axis_size("head")
     width = features.shape[1]
     rows = features.shape[0]
 
-    def exchange_lists(lists):
-        return lax.all_to_all(
-            lists.reshape(n_dom, 1), "dom", split_axis=0, concat_axis=0, tiled=True
-        ).reshape(n_dom)
-
-    def gather_ffn(weights):
-        both = jnp.concatenate(weights, axis=1)
-        return lax.all_to_all(
-            jnp.broadcast_to(both[None], (n_head,) + both.shape),
-            "head", split_axis=0, concat_axis=0, tiled=True,
-        ).reshape(-1, 2 * width)
-
-    jobs = [
-        (1, 5, exchange_lists, serve_list),
-        (2, None, gather_ffn, (expand_weight, reduce_weight)),
-        (4, 7, jnp.transpose, qkv_weight),
-    ]
-    pieces, (served, ffn, weight_t) = ring_pieces(features, jobs)
     place = lax.axis_index("dom").reshape(1)
+    whole, halves, traded, served, ffn = ring_pieces(
+        features, place, serve_list, (expand_weight, reduce_weight)
+    )
+    weight_t = qkv_weight.T
     agg, qkv_t = aggregate(
-        place, tile_source, served, tile_pattern, features, weight_t, pieces
+        place, tile_source, served, tile_pattern, features, weight_t, whole + halves + traded
     )
     qkv = lax.all_to_all(
         qkv_t.reshape(n_head, 3 * HDIM, rows), "head", split_axis=0, concat_axis=0, tiled=True

time: 295 us -> 258 us (0.87)
  waiting for transfers between devices: 110 us -> 82.9 us
  blocking collectives: 34.4 us -> 14.2 us
  Pallas kernels: 31.5 us -> 39.4 us
  local copies, waits for them, and re-layouts: 6.08 us -> 9.27 us
  starting transfers between devices: 110 us -> 107 us
    all_to_all x1 -> x2, waiting for transfers between devices: 36.6 us -> 12.4 us  [the longest x1 12.4 us: ring_pieces(): lax.all_to_all(jnp.stack([mine, swapped], axis=1), 'dom', split_axis=0, c...]
    all_to_all x1 -> x0, blocking collectives: 20.7 us -> none  [exchange_lists(): lax.all_to_all(lists.reshape(n_dom, 1), 'dom', split_axis=0, concat_axis=...]
    ppermute x17 -> x9, starting transfers between devices: 36 us -> 17.8 us  [trade(): return lax.ppermute(v, 'dom', [(i, i ^ 1) for i in range(n)])]
    all_to_all x1 -> x2, starting transfers between devices: 5.86 us -> 23 us  [the longest x1 15.5 us: ring_pieces(): lax.all_to_all(jnp.stack([mine, swapped], axis=1), 'dom', split_axis=0, c...]
    pallas_call x0 -> x9, Pallas kernels: none -> 7.91 us  [pick(): pl.pallas_call(functools.partial(pick_kernel, steps), out_shape=jax.Shape...]
    unnamed x47 -> x65, local copies, waits for them, and re-layouts: 0.18 us -> 5.15 us
  transfers between devices with their start and end apart: 35 -> 28, of which waited for: 16 -> 17; matrix products, arithmetic and copies ran while one was open for 2% -> 1% of each run, Pallas kernels for 5% -> 3%
where the time goes in v1:
time: 258 us; the launch traced here: 257 us
  starting transfers between devices  107 us (41%)
  waiting for transfers between devices  82.9 us (32%)
  Pallas kernels  39.4 us (15%)
  blocking collectives  14.2 us (6%)
  local copies, waits for them, and re-layouts  9.27 us (4%)
  other arithmetic  2.97 us (1%)
    ppermute x16, starting transfers between devices, send(): return lax.ppermute(v, 'dom', [(i, (i + by) % n) for i in range(n)])  59.7 us
    ppermute x16, waiting for transfers between devices, send(): return lax.ppermute(v, 'dom', [(i, (i + by) % n) for i in range(n)])  46.5 us
    all_to_all x1, waiting for transfers between devices, shards(): lax.all_to_all(qkv_t.reshape(n_head, 3 * HDIM, rows), 'head', split_axis=...  23.7 us
    ppermute x9, starting transfers between devices, trade(): return lax.ppermute(v, 'dom', [(i, i ^ 1) for i in range(n)])  17.8 us
    pallas_call x1, Pallas kernels, attend(): pl.pallas_call(attend_kernel, out_shape=jax.ShapeDtypeStruct((sources, HD...  15.7 us
    all_to_all x1, starting transfers between devices, ring_pieces(): lax.all_to_all(jnp.stack([mine, swapped], axis=1), 'dom', split_axis=0, c...  15.5 us
    all_to_all x1, blocking collectives, shards(): lax.all_to_all(context, 'head', split_axis=0, concat_axis=0, tiled=True)  14.2 us
    all_to_all x1, waiting for transfers between devices, ring_pieces(): lax.all_to_all(jnp.stack([mine, swapped], axis=1), 'dom', split_axis=0, c...  12.4 us
  transfers between devices with their start and end apart: 28, of which 17 were waited for; matrix products, arithmetic and copies ran while one was open for 1% of the time, Pallas kernels for 3%

profile of v1, /device:TPU:8, one launch (start us, length us, event | category | flops | bytes accessed | tf_op | source)
XLA Modules:
  0.0 256.6 jit_solution(7513907842479073245)
XLA Ops:
  0.5 1.3 reduce.3
  2.1 0.7 add_bitcast_fusion
  2.8 0.7 copy.15
  3.5 15.5 %all-to-all-start = ((s32[32,1,2]{2,1,0:T(1,128)}), s32[32,1,2]{2,1,0:T(1,128)S(1)}, u32[]{:S(2)}, u32[]{:S(2)}) async-start(s32[32,1,2]{2,1,0:T(1,128)} %copy.15), calls=%async_computation | async-start | bytes 32768 | tf_op jit(solution)/shard_map/all_to_all | solution.py:93
  18.9 12.4 %all-to-all-done = s32[32,1,2]{2,1,0:T(1,128)S(1)} async-done(((s32[32,1,2]{2,1,0:T(1,128)}), s32[32,1,2]{2,1,0:T(1,128)S(1)}, u32[]{:S(2)}, u32[]{:S(2)}) %all-to-all-start) | async-done | bytes 288 | tf_op jit(solution)/shard_map/all_to_all | solution.py:93
  32.0 1.0 copy-done
  33.0 0.7 pick.14
  33.7 1.9 collective-permute-start.21
  35.7 1.0 pad_maximum_fusion
  37.0 2.5 broadcast_in_dim.2
  39.5 7.5 %all-to-all-start.1 = ((bf16[16,128,1024]{2,1,0:T(8,128)(2,1)}), bf16[16,128,1024]{2,1,0:T(8,128)(2,1)}, u32[]{:S(2)}, u32[]{:S(2)}) async-start(bf16[16,128,1024]{2,1,0:T(8,128)(2,1)} %broadcast_in_dim.2), calls=%async_computation.1 | async-start | bytes 8388608 | tf_op jit(solution)/shard_map/all_to_all | solution.py:103
  47.1 2.5 collective-permute-start
  49.5 4.6 %collective-permute-start.1 = (bf16[512,512]{1,0:T(8,128)(2,1)S(1)}, bf16[512,512]{1,0:T(8,128)(2,1)S(1)}, u32[]{:S(2)}, u32[]{:S(2)}) collective-permute-start(bf16[512,512]{1,0:T(8,128)(2,1)S(1)} %copy-done.1), channel_id=1, source_target_pairs={{0,480},{16,496},{32,0},{48,16},{64,32},{80,48},{96,64},{112,80},{... | collective-permute-start | bytes 1572872 | tf_op jit(solution)/shard_map/ppermute | solution.py:75
  54.1 9.5 %collective-permute-done.refs_0_.rest_1_ = bf16[512,512]{1,0:T(8,128)(2,1)S(1)} collective-permute-done((bf16[512,512]{1,0:T(8,128)(2,1)S(1)}, bf16[512,512]{1,0:T(8,128)(2,1)S(1)}, u32[]{:S(2)}, u32[]{:S(2)}) %collective-permute-start) | collective-permute-done | bytes 524320 | tf_op jit(solution)/shard_map/ppermute | solution.py:75
  63.6 1.2 collective-permute-done.1.refs_1_.rest_8_
  64.8 2.2 collective-permute-start.2
  67.0 5.3 %collective-permute-start.3 = (bf16[512,512]{1,0:T(8,128)(2,1)S(1)}, bf16[512,512]{1,0:T(8,128)(2,1)S(1)}, u32[]{:S(2)}, u32[]{:S(2)}) collective-permute-start(bf16[512,512]{1,0:T(8,128)(2,1)S(1)} %collective-permute-done.1.refs_1_.rest_8_), channel_id=1, source_target_pairs={{0,480},{16,496},{32,0},{48,16},{64,32},{80,48},{96,64},{112,80},{... | collective-permute-start | bytes 1572872 | tf_op jit(solution)/shard_map/ppermute | solution.py:75
  72.3 8.8 %collective-permute-done.2.refs_0_.rest_2_ = bf16[512,512]{1,0:T(8,128)(2,1)S(1)} collective-permute-done((bf16[512,512]{1,0:T(8,128)(2,1)S(1)}, bf16[512,512]{1,0:T(8,128)(2,1)S(1)}, u32[]{:S(2)}, u32[]{:S(2)}) %collective-permute-start.2) | collective-permute-done | bytes 524320 | tf_op jit(solution)/shard_map/ppermute | solution.py:75
  81.1 1.2 collective-permute-done.3.refs_1_.rest_9_
  82.3 1.9 collective-permute-start.4
  84.2 5.6 %collective-permute-start.5 = (bf16[512,512]{1,0:T(8,128)(2,1)S(1)}, bf16[512,512]{1,0:T(8,128)(2,1)S(1)}, u32[]{:S(2)}, u32[]{:S(2)}) collective-permute-start(bf16[512,512]{1,0:T(8,128)(2,1)S(1)} %collective-permute-done.3.refs_1_.rest_9_), channel_id=1, source_target_pairs={{0,480},{16,496},{32,0},{48,16},{64,32},{80,48},{96,64},{112,80},{... | collective-permute-start | bytes 1572872 | tf_op jit(solution)/shard_map/ppermute | solution.py:75
  89.8 0.9 pick.9
  90.7 1.9 collective-permute-start.6
  92.7 5.1 %collective-permute-done.4.refs_0_.rest_3_ = bf16[512,512]{1,0:T(8,128)(2,1)S(1)} collective-permute-done((bf16[512,512]{1,0:T(8,128)(2,1)S(1)}, bf16[512,512]{1,0:T(8,128)(2,1)S(1)}, u32[]{:S(2)}, u32[]{:S(2)}) %collective-permute-start.4) | collective-permute-done | bytes 524320 | tf_op jit(solution)/shard_map/ppermute | solution.py:75
  97.8 1.2 collective-permute-done.5.refs_1_.rest_10_
  99.0 1.9 collective-permute-start.7
  100.9 5.6 %collective-permute-start.8 = (bf16[512,512]{1,0:T(8,128)(2,1)S(1)}, bf16[512,512]{1,0:T(8,128)(2,1)S(1)}, u32[]{:S(2)}, u32[]{:S(2)}) collective-permute-start(bf16[512,512]{1,0:T(8,128)(2,1)S(1)} %collective-permute-done.5.refs_1_.rest_10_), channel_id=1, source_target_pairs={{0,480},{16,496},{32,0},{48,16},{64,32},{80,48},{96,64},{112,80},{... | collective-permute-start | bytes 1572872 | tf_op jit(solution)/shard_map/ppermute | solution.py:75
  106.5 0.9 pick.10
  107.4 1.9 collective-permute-start.9
  109.4 4.4 %collective-permute-done.7.refs_0_.rest_4_ = bf16[512,512]{1,0:T(8,128)(2,1)S(1)} collective-permute-done((bf16[512,512]{1,0:T(8,128)(2,1)S(1)}, bf16[512,512]{1,0:T(8,128)(2,1)S(1)}, u32[]{:S(2)}, u32[]{:S(2)}) %collective-permute-start.7) | collective-permute-done | bytes 524320 | tf_op jit(solution)/shard_map/ppermute | solution.py:75
  113.8 1.2 collective-permute-done.8.refs_1_.rest_11_
  115.0 1.9 collective-permute-start.10
  116.9 5.6 %collective-permute-start.11 = (bf16[512,512]{1,0:T(8,128)(2,1)S(1)}, bf16[512,512]{1,0:T(8,128)(2,1)S(1)}, u32[]{:S(2)}, u32[]{:S(2)}) collective-permute-start(bf16[512,512]{1,0:T(8,128)(2,1)S(1)} %collective-permute-done.8.refs_1_.rest_11_), channel_id=1, source_target_pairs={{0,480},{16,496},{32,0},{48,16},{64,32},{80,48},{96,64},{112,80},{... | collective-permute-start | bytes 1572872 | tf_op jit(solution)/shard_map/ppermute | solution.py:75
  122.5 0.9 pick.11
  123.5 1.9 collective-permute-start.12
  125.4 3.5 %collective-permute-done.10.refs_0_.rest_5_ = bf16[512,512]{1,0:T(8,128)(2,1)S(1)} collective-permute-done((bf16[512,512]{1,0:T(8,128)(2,1)S(1)}, bf16[512,512]{1,0:T(8,128)(2,1)S(1)}, u32[]{:S(2)}, u32[]{:S(2)}) %collective-permute-start.10) | collective-permute-done | bytes 524320 | tf_op jit(solution)/shard_map/ppermute | solution.py:75
  128.9 1.2 collective-permute-done.11.refs_1_.rest_12_
  130.1 1.9 collective-permute-start.13
  132.0 5.6 %collective-permute-start.14 = (bf16[512,512]{1,0:T(8,128)(2,1)S(1)}, bf16[512,512]{1,0:T(8,128)(2,1)S(1)}, u32[]{:S(2)}, u32[]{:S(2)}) collective-permute-start(bf16[512,512]{1,0:T(8,128)(2,1)S(1)} %collective-permute-done.11.refs_1_.rest_12_), channel_id=1, source_target_pairs={{0,480},{16,496},{32,0},{48,16},{64,32},{80,48},{96,64},{112,80},{... | collective-permute-start | bytes 1572872 | tf_op jit(solution)/shard_map/ppermute | solution.py:75
  137.6 0.9 pick.12
  138.5 1.9 collective-permute-start.15
  140.5 3.5 %collective-permute-done.13.refs_0_.rest_6_ = bf16[512,512]{1,0:T(8,128)(2,1)S(1)} collective-permute-done((bf16[512,512]{1,0:T(8,128)(2,1)S(1)}, bf16[512,512]{1,0:T(8,128)(2,1)S(1)}, u32[]{:S(2)}, u32[]{:S(2)}) %collective-permute-start.13) | collective-permute-done | bytes 524320 | tf_op jit(solution)/shard_map/ppermute | solution.py:75
  143.9 1.2 collective-permute-done.14.refs_1_.rest_13_
  145.1 1.9 collective-permute-start.16
  147.1 5.6 %collective-permute-start.17 = (bf16[512,512]{1,0:T(8,128)(2,1)S(1)}, bf16[512,512]{1,0:T(8,128)(2,1)S(1)}, u32[]{:S(2)}, u32[]{:S(2)}) collective-permute-start(bf16[512,512]{1,0:T(8,128)(2,1)S(1)} %collective-permute-done.14.refs_1_.rest_13_), channel_id=1, source_target_pairs={{0,480},{16,496},{32,0},{48,16},{64,32},{80,48},{96,64},{112,80},{... | collective-permute-start | bytes 1572872 | tf_op jit(solution)/shard_map/ppermute | solution.py:75
  152.7 0.9 pick.13
  153.6 1.9 collective-permute-start.18
  155.5 3.5 %collective-permute-done.16.refs_0_.rest_7_ = bf16[512,512]{1,0:T(8,128)(2,1)S(1)} collective-permute-done((bf16[512,512]{1,0:T(8,128)(2,1)S(1)}, bf16[512,512]{1,0:T(8,128)(2,1)S(1)}, u32[]{:S(2)}, u32[]{:S(2)}) %collective-permute-start.16) | collective-permute-done | bytes 524320 | tf_op jit(solution)/shard_map/ppermute | solution.py:75
  159.1 1.2 collective-permute-done.17.refs_1_.rest_14_
  160.3 1.9 collective-permute-start.19
  162.2 5.6 %collective-permute-start.20 = (bf16[256,512]{1,0:T(8,128)(2,1)S(1)}, bf16[256,512]{1,0:T(8,128)(2,1)S(1)}, u32[]{:S(2)}, u32[]{:S(2)}) collective-permute-start(bf16[256,512]{1,0:T(8,128)(2,1)S(1)} %slice.15), channel_id=1, source_target_pairs={{0,480},{16,496},{32,0},{48,16},{64,32},{80,48},{96,64},{112,80},{... | collective-permute-start | bytes 786440 | tf_op jit(solution)/shard_map/ppermute | solution.py:75
  167.8 0.9 pick.15
  168.8 1.9 collective-permute-start.22
  170.7 0.9 pick.16
  171.7 2.4 collective-permute-start.23
  174.1 0.7 pick.17
  174.9 1.9 collective-permute-start.24
  176.8 2.6 %copy.17 = bf16[512,1536]{0,1:T(8,128)(2,1)} copy(bf16[512,1536]{1,0:T(8,128)(2,1)} %param.15) | data formatting | bytes 3145728 | tf_op args[5]
  180.3 8.3 %aggregate.1 = (bf16[512,512]{1,0:T(8,128)(2,1)}, bf16[1536,512]{1,0:T(8,128)(2,1)}) custom-call(s32[1]{0:T(128)} %bitcast.place_ref, s32[4,6]{1,0:T(4,128)} %entry_ref.1, s32[32]{0:T(128)} %get-tuple-element.80.serve_ref, s32[4,6,128,128]{3,2,1,0:T(8,128)} %pattern_ref.1, bf16[512,512]{1,0:T(8,128)(2,1)} %rest_0_.1, bf16[1536,512]{1,0:T(8,128)(2,1)} %bitcast.17, ...), custom_call_target="tpu_custom_call" | custom-call | tf_op jit(solution)/shard_map/aggregate/pallas_call | solution.py:218
  188.6 6.7 %all-to-all-start.2 = ((bf16[16,96,512]{2,1,0:T(8,128)(2,1)}), bf16[16,96,512]{2,1,0:T(8,128)(2,1)S(1)}, u32[]{:S(2)}, u32[]{:S(2)}) async-start(bf16[16,96,512]{2,1,0:T(8,128)(2,1)} %bitcast.18), calls=%async_computation.2 | async-start | bytes 3145728 | tf_op jit(solution)/shard_map/all_to_all | solution.py:365
  195.5 23.7 %all-to-all-done.2.qkv_ref = bf16[16,96,512]{2,1,0:T(8,128)(2,1)S(1)} async-done(((bf16[16,96,512]{2,1,0:T(8,128)(2,1)}), bf16[16,96,512]{2,1,0:T(8,128)(2,1)S(1)}, u32[]{:S(2)}, u32[]{:S(2)}) %all-to-all-start.2) | async-done | bytes 1572896 | tf_op jit(solution)/shard_map/all_to_all | solution.py:365
  219.1 15.7 %attend.1 = bf16[16,32,512]{2,1,0:T(8,128)(2,1)S(1)} custom-call(s32[64,8]{1,0:T(8,128)S(1)} %copy.18.key_ref, bf16[16,96,512]{2,1,0:T(8,128)(2,1)S(1)} %all-to-all-done.2.qkv_ref), custom_call_target="tpu_custom_call" | custom-call | tf_op jit(solution)/shard_map/attend/pallas_call | solution.py:283
  234.8 14.2 %all_to_all.27 = bf16[16,32,512]{2,1,0:T(8,128)(2,1)S(1)} all-to-all(bf16[16,32,512]{2,1,0:T(8,128)(2,1)S(1)} %attend.1), channel_id=1, replica_groups=mesh['dom'=32,'head'=16] {'head'}, dimensions={0} | all-to-all | bytes 1048576 | tf_op jit(solution)/shard_map/all_to_all | solution.py:369
  249.1 7.5 %finish.1 = bf16[512,512]{1,0:T(8,128)(2,1)} custom-call(bf16[512,512]{1,0:T(8,128)(2,1)S(1)} %bitcast.15, bf16[512,512]{1,0:T(8,128)(2,1)S(1)} %copy-done.19, bf16[512,512]{1,0:T(8,128)(2,1)S(1)} %copy-done.18, f32[1,512]{1,0:T(1,128)S(1)} %bitcast.16, bf16[2048,1024]{1,0:T(8,128)(2,1)} %bitcast.10.ffn_ref), custom_call_target="tpu_custom_call" | custom-call | tf_op jit(solution)/shard_map/finish/pallas_call | solution.py:327
  (82 shorter events, 2.7 us)
Async XLA Ops:
  3.5 27.9 %all-to-all-start = ((s32[32,1,2]{2,1,0:T(1,128)}), s32[32,1,2]{2,1,0:T(1,128)S(1)}, u32[]{:S(2)}, u32[]{:S(2)}) async-start(s32[32,1,2]{2,1,0:T(1,128)} %copy.15), calls=%async_computation | async-start | bytes 32768 | tf_op jit(solution)/shard_map/all_to_all | solution.py:93
  32.0 1.0 copy-start
  33.7 3.2 %collective-permute-start.21 = (bf16[128,512]{1,0:T(8,128)(2,1)S(1)}, bf16[128,512]{1,0:T(8,128)(2,1)S(1)}, u32[]{:S(2)}, u32[]{:S(2)}) collective-permute-start(bf16[128,512]{1,0:T(8,128)(2,1)S(1)} %pick.14), channel_id=1, source_target_pairs={{0,16},{16,0},{32,48},{48,32},{64,80},{80,64},{96,112},{112,96},{1... | collective-permute-start | bytes 393224 | tf_op jit(solution)/shard_map/ppermute | solution.py:78
  37.0 2.5 copy-start.28
  39.5 7.5 %copy-start.1 = (bf16[512,512]{1,0:T(8,128)(2,1)S(1)}, bf16[512,512]{1,0:T(8,128)(2,1)}, u32[]{:S(2)}) copy-start(bf16[512,512]{1,0:T(8,128)(2,1)} %rest_0_.1) | copy-start | bytes 1572868
  39.5 132.1 %all-to-all-start.1 = ((bf16[16,128,1024]{2,1,0:T(8,128)(2,1)}), bf16[16,128,1024]{2,1,0:T(8,128)(2,1)}, u32[]{:S(2)}, u32[]{:S(2)}) async-start(bf16[16,128,1024]{2,1,0:T(8,128)(2,1)} %broadcast_in_dim.2), calls=%async_computation.1 | async-start | bytes 8388608 | tf_op jit(solution)/shard_map/all_to_all | solution.py:103
  47.1 16.6 %collective-permute-start = (bf16[512,512]{1,0:T(8,128)(2,1)S(1)}, bf16[512,512]{1,0:T(8,128)(2,1)S(1)}, u32[]{:S(2)}, u32[]{:S(2)}) collective-permute-start(bf16[512,512]{1,0:T(8,128)(2,1)S(1)} %copy-done.1), channel_id=1, source_target_pairs={{0,32},{16,48},{32,64},{48,80},{64,96},{80,112},{96,128},{112,144}... | collective-permute-start | bytes 1572872 | tf_op jit(solution)/shard_map/ppermute | solution.py:75
  49.5 15.3 %collective-permute-start.1 = (bf16[512,512]{1,0:T(8,128)(2,1)S(1)}, bf16[512,512]{1,0:T(8,128)(2,1)S(1)}, u32[]{:S(2)}, u32[]{:S(2)}) collective-permute-start(bf16[512,512]{1,0:T(8,128)(2,1)S(1)} %copy-done.1), channel_id=1, source_target_pairs={{0,480},{16,496},{32,0},{48,16},{64,32},{80,48},{96,64},{112,80},{... | collective-permute-start | bytes 1572872 | tf_op jit(solution)/shard_map/ppermute | solution.py:75
  63.6 59.8 %copy-start.4 = (bf16[512,512]{1,0:T(8,128)(2,1)}, bf16[512,512]{1,0:T(8,128)(2,1)S(1)}, u32[]{:S(2)}) copy-start(bf16[512,512]{1,0:T(8,128)(2,1)S(1)} %collective-permute-done.refs_0_.rest_1_) | copy-start | bytes 1572868
  64.8 58.6 %copy-start.5 = (bf16[512,512]{1,0:T(8,128)(2,1)}, bf16[512,512]{1,0:T(8,128)(2,1)S(1)}, u32[]{:S(2)}) copy-start(bf16[512,512]{1,0:T(8,128)(2,1)S(1)} %collective-permute-done.1.refs_1_.rest_8_) | copy-start | bytes 1572868
  64.8 16.3 %collective-permute-start.2 = (bf16[512,512]{1,0:T(8,128)(2,1)S(1)}, bf16[512,512]{1,0:T(8,128)(2,1)S(1)}, u32[]{:S(2)}, u32[]{:S(2)}) collective-permute-start(bf16[512,512]{1,0:T(8,128)(2,1)S(1)} %collective-permute-done.refs_0_.rest_1_), channel_id=1, source_target_pairs={{0,32},{16,48},{32,64},{48,80},{64,96},{80,112},{96,128},{112,144}... | collective-permute-start | bytes 1572872 | tf_op jit(solution)/shard_map/ppermute | solution.py:75
  67.0 15.3 %collective-permute-start.3 = (bf16[512,512]{1,0:T(8,128)(2,1)S(1)}, bf16[512,512]{1,0:T(8,128)(2,1)S(1)}, u32[]{:S(2)}, u32[]{:S(2)}) collective-permute-start(bf16[512,512]{1,0:T(8,128)(2,1)S(1)} %collective-permute-done.1.refs_1_.rest_8_), channel_id=1, source_target_pairs={{0,480},{16,496},{32,0},{48,16},{64,32},{80,48},{96,64},{112,80},{... | collective-permute-start | bytes 1572872 | tf_op jit(solution)/shard_map/ppermute | solution.py:75
  81.1 42.3 %copy-start.6 = (bf16[512,512]{1,0:T(8,128)(2,1)}, bf16[512,512]{1,0:T(8,128)(2,1)S(1)}, u32[]{:S(2)}) copy-start(bf16[512,512]{1,0:T(8,128)(2,1)S(1)} %collective-permute-done.2.refs_0_.rest_2_) | copy-start | bytes 1572868
  82.3 41.2 %copy-start.7 = (bf16[512,512]{1,0:T(8,128)(2,1)}, bf16[512,512]{1,0:T(8,128)(2,1)S(1)}, u32[]{:S(2)}) copy-start(bf16[512,512]{1,0:T(8,128)(2,1)S(1)} %collective-permute-done.3.refs_1_.rest_9_) | copy-start | bytes 1572868
  82.3 15.5 %collective-permute-start.4 = (bf16[512,512]{1,0:T(8,128)(2,1)S(1)}, bf16[512,512]{1,0:T(8,128)(2,1)S(1)}, u32[]{:S(2)}, u32[]{:S(2)}) collective-permute-start(bf16[512,512]{1,0:T(8,128)(2,1)S(1)} %collective-permute-done.2.refs_0_.rest_2_), channel_id=1, source_target_pairs={{0,32},{16,48},{32,64},{48,80},{64,96},{80,112},{96,128},{112,144}... | collective-permute-start | bytes 1572872 | tf_op jit(solution)/shard_map/ppermute | solution.py:75
  84.2 14.8 %collective-permute-start.5 = (bf16[512,512]{1,0:T(8,128)(2,1)S(1)}, bf16[512,512]{1,0:T(8,128)(2,1)S(1)}, u32[]{:S(2)}, u32[]{:S(2)}) collective-permute-start(bf16[512,512]{1,0:T(8,128)(2,1)S(1)} %collective-permute-done.3.refs_1_.rest_9_), channel_id=1, source_target_pairs={{0,480},{16,496},{32,0},{48,16},{64,32},{80,48},{96,64},{112,80},{... | collective-permute-start | bytes 1572872 | tf_op jit(solution)/shard_map/ppermute | solution.py:75
  90.7 8.3 %collective-permute-start.6 = (bf16[256,512]{1,0:T(8,128)(2,1)S(1)}, bf16[256,512]{1,0:T(8,128)(2,1)S(1)}, u32[]{:S(2)}, u32[]{:S(2)}) collective-permute-start(bf16[256,512]{1,0:T(8,128)(2,1)S(1)} %pick.9), channel_id=1, source_target_pairs={{0,16},{16,0},{32,48},{48,32},{64,80},{80,64},{96,112},{112,96},{1... | collective-permute-start | bytes 786440 | tf_op jit(solution)/shard_map/ppermute | solution.py:78
  97.8 40.7 %copy-start.8 = (bf16[512,512]{1,0:T(8,128)(2,1)}, bf16[512,512]{1,0:T(8,128)(2,1)S(1)}, u32[]{:S(2)}) copy-start(bf16[512,512]{1,0:T(8,128)(2,1)S(1)} %collective-permute-done.4.refs_0_.rest_3_) | copy-start | bytes 1572868
  99.0 26.4 %copy-start.9 = (bf16[512,512]{1,0:T(8,128)(2,1)}, bf16[512,512]{1,0:T(8,128)(2,1)S(1)}, u32[]{:S(2)}) copy-start(bf16[512,512]{1,0:T(8,128)(2,1)S(1)} %collective-permute-done.5.refs_1_.rest_10_) | copy-start | bytes 1572868
  99.0 39.6 %copy-start.21 = (bf16[256,512]{1,0:T(8,128)(2,1)}, bf16[256,512]{1,0:T(8,128)(2,1)S(1)}, u32[]{:S(2)}) copy-start(bf16[256,512]{1,0:T(8,128)(2,1)S(1)} %collective-permute-done.6.rest_18_) | copy-start | bytes 786436
  99.0 14.8 %collective-permute-start.7 = (bf16[512,512]{1,0:T(8,128)(2,1)S(1)}, bf16[512,512]{1,0:T(8,128)(2,1)S(1)}, u32[]{:S(2)}, u32[]{:S(2)}) collective-permute-start(bf16[512,512]{1,0:T(8,128)(2,1)S(1)} %collective-permute-done.4.refs_0_.rest_3_), channel_id=1, source_target_pairs={{0,32},{16,48},{32,64},{48,80},{64,96},{80,112},{96,128},{112,144}... | collective-permute-start | bytes 1572872 | tf_op jit(solution)/shard_map/ppermute | solution.py:75
  100.9 14.0 %collective-permute-start.8 = (bf16[512,512]{1,0:T(8,128)(2,1)S(1)}, bf16[512,512]{1,0:T(8,128)(2,1)S(1)}, u32[]{:S(2)}, u32[]{:S(2)}) collective-permute-start(bf16[512,512]{1,0:T(8,128)(2,1)S(1)} %collective-permute-done.5.refs_1_.rest_10_), channel_id=1, source_target_pairs={{0,480},{16,496},{32,0},{48,16},{64,32},{80,48},{96,64},{112,80},{... | collective-permute-start | bytes 1572872 | tf_op jit(solution)/shard_map/ppermute | solution.py:75
  107.4 7.5 %collective-permute-start.9 = (bf16[256,512]{1,0:T(8,128)(2,1)S(1)}, bf16[256,512]{1,0:T(8,128)(2,1)S(1)}, u32[]{:S(2)}, u32[]{:S(2)}) collective-permute-start(bf16[256,512]{1,0:T(8,128)(2,1)S(1)} %pick.10), channel_id=1, source_target_pairs={{0,16},{16,0},{32,48},{48,32},{64,80},{80,64},{96,112},{112,96},{1... | collective-permute-start | bytes 786440 | tf_op jit(solution)/shard_map/ppermute | solution.py:78
  113.8 39.8 %copy-start.10 = (bf16[512,512]{1,0:T(8,128)(2,1)}, bf16[512,512]{1,0:T(8,128)(2,1)S(1)}, u32[]{:S(2)}) copy-start(bf16[512,512]{1,0:T(8,128)(2,1)S(1)} %collective-permute-done.7.refs_0_.rest_4_) | copy-start | bytes 1572868
  114.9 38.7 %copy-start.11 = (bf16[512,512]{1,0:T(8,128)(2,1)}, bf16[512,512]{1,0:T(8,128)(2,1)S(1)}, u32[]{:S(2)}) copy-start(bf16[512,512]{1,0:T(8,128)(2,1)S(1)} %collective-permute-done.8.refs_1_.rest_11_) | copy-start | bytes 1572868
  115.0 38.7 %copy-start.22 = (bf16[256,512]{1,0:T(8,128)(2,1)}, bf16[256,512]{1,0:T(8,128)(2,1)S(1)}, u32[]{:S(2)}) copy-start(bf16[256,512]{1,0:T(8,128)(2,1)S(1)} %collective-permute-done.9.rest_19_) | copy-start | bytes 786436
  115.0 13.9 %collective-permute-start.10 = (bf16[512,512]{1,0:T(8,128)(2,1)S(1)}, bf16[512,512]{1,0:T(8,128)(2,1)S(1)}, u32[]{:S(2)}, u32[]{:S(2)}) collective-permute-start(bf16[512,512]{1,0:T(8,128)(2,1)S(1)} %collective-permute-done.7.refs_0_.rest_4_), channel_id=1, source_target_pairs={{0,32},{16,48},{32,64},{48,80},{64,96},{80,112},{96,128},{112,144}... | collective-permute-start | bytes 1572872 | tf_op jit(solution)/shard_map/ppermute | solution.py:75
  116.9 13.2 %collective-permute-start.11 = (bf16[512,512]{1,0:T(8,128)(2,1)S(1)}, bf16[512,512]{1,0:T(8,128)(2,1)S(1)}, u32[]{:S(2)}, u32[]{:S(2)}) collective-permute-start(bf16[512,512]{1,0:T(8,128)(2,1)S(1)} %collective-permute-done.8.refs_1_.rest_11_), channel_id=1, source_target_pairs={{0,480},{16,496},{32,0},{48,16},{64,32},{80,48},{96,64},{112,80},{... | collective-permute-start | bytes 1572872 | tf_op jit(solution)/shard_map/ppermute | solution.py:75
  123.5 6.6 %collective-permute-start.12 = (bf16[256,512]{1,0:T(8,128)(2,1)S(1)}, bf16[256,512]{1,0:T(8,128)(2,1)S(1)}, u32[]{:S(2)}, u32[]{:S(2)}) collective-permute-start(bf16[256,512]{1,0:T(8,128)(2,1)S(1)} %pick.11), channel_id=1, source_target_pairs={{0,16},{16,0},{32,48},{48,32},{64,80},{80,64},{96,112},{112,96},{1... | collective-permute-start | bytes 786440 | tf_op jit(solution)/shard_map/ppermute | solution.py:78
  128.9 30.2 %copy-start.12 = (bf16[512,512]{1,0:T(8,128)(2,1)}, bf16[512,512]{1,0:T(8,128)(2,1)S(1)}, u32[]{:S(2)}) copy-start(bf16[512,512]{1,0:T(8,128)(2,1)S(1)} %collective-permute-done.10.refs_0_.rest_5_) | copy-start | bytes 1572868
  130.1 29.0 %copy-start.13 = (bf16[512,512]{1,0:T(8,128)(2,1)}, bf16[512,512]{1,0:T(8,128)(2,1)S(1)}, u32[]{:S(2)}) copy-start(bf16[512,512]{1,0:T(8,128)(2,1)S(1)} %collective-permute-done.11.refs_1_.rest_12_) | copy-start | bytes 1572868
  130.1 30.2 %copy-start.23 = (bf16[256,512]{1,0:T(8,128)(2,1)}, bf16[256,512]{1,0:T(8,128)(2,1)S(1)}, u32[]{:S(2)}) copy-start(bf16[256,512]{1,0:T(8,128)(2,1)S(1)} %collective-permute-done.12.rest_20_) | copy-start | bytes 786436
  130.1 13.9 %collective-permute-start.13 = (bf16[512,512]{1,0:T(8,128)(2,1)S(1)}, bf16[512,512]{1,0:T(8,128)(2,1)S(1)}, u32[]{:S(2)}, u32[]{:S(2)}) collective-permute-start(bf16[512,512]{1,0:T(8,128)(2,1)S(1)} %collective-permute-done.10.refs_0_.rest_5_), channel_id=1, source_target_pairs={{0,32},{16,48},{32,64},{48,80},{64,96},{80,112},{96,128},{112,144}... | collective-permute-start | bytes 1572872 | tf_op jit(solution)/shard_map/ppermute | solution.py:75
  132.0 13.1 %collective-permute-start.14 = (bf16[512,512]{1,0:T(8,128)(2,1)S(1)}, bf16[512,512]{1,0:T(8,128)(2,1)S(1)}, u32[]{:S(2)}, u32[]{:S(2)}) collective-permute-start(bf16[512,512]{1,0:T(8,128)(2,1)S(1)} %collective-permute-done.11.refs_1_.rest_12_), channel_id=1, source_target_pairs={{0,480},{16,496},{32,0},{48,16},{64,32},{80,48},{96,64},{112,80},{... | collective-permute-start | bytes 1572872 | tf_op jit(solution)/shard_map/ppermute | solution.py:75
  138.5 6.6 %collective-permute-start.15 = (bf16[256,512]{1,0:T(8,128)(2,1)S(1)}, bf16[256,512]{1,0:T(8,128)(2,1)S(1)}, u32[]{:S(2)}, u32[]{:S(2)}) collective-permute-start(bf16[256,512]{1,0:T(8,128)(2,1)S(1)} %pick.12), channel_id=1, source_target_pairs={{0,16},{16,0},{32,48},{48,32},{64,80},{80,64},{96,112},{112,96},{1... | collective-permute-start | bytes 786440 | tf_op jit(solution)/shard_map/ppermute | solution.py:78
  143.9 24.8 %copy-start.14 = (bf16[512,512]{1,0:T(8,128)(2,1)}, bf16[512,512]{1,0:T(8,128)(2,1)S(1)}, u32[]{:S(2)}) copy-start(bf16[512,512]{1,0:T(8,128)(2,1)S(1)} %collective-permute-done.13.refs_0_.rest_6_) | copy-start | bytes 1572868
  145.1 23.6 %copy-start.15 = (bf16[512,512]{1,0:T(8,128)(2,1)}, bf16[512,512]{1,0:T(8,128)(2,1)S(1)}, u32[]{:S(2)}) copy-start(bf16[512,512]{1,0:T(8,128)(2,1)S(1)} %collective-permute-done.14.refs_1_.rest_13_) | copy-start | bytes 1572868
  145.1 13.9 %copy-start.24 = (bf16[256,512]{1,0:T(8,128)(2,1)}, bf16[256,512]{1,0:T(8,128)(2,1)S(1)}, u32[]{:S(2)}) copy-start(bf16[256,512]{1,0:T(8,128)(2,1)S(1)} %collective-permute-done.15.rest_21_) | copy-start | bytes 786436
  145.1 13.9 %collective-permute-start.16 = (bf16[512,512]{1,0:T(8,128)(2,1)S(1)}, bf16[512,512]{1,0:T(8,128)(2,1)S(1)}, u32[]{:S(2)}, u32[]{:S(2)}) collective-permute-start(bf16[512,512]{1,0:T(8,128)(2,1)S(1)} %collective-permute-done.13.refs_0_.rest_6_), channel_id=1, source_target_pairs={{0,32},{16,48},{32,64},{48,80},{64,96},{80,112},{96,128},{112,144}... | collective-permute-start | bytes 1572872 | tf_op jit(solution)/shard_map/ppermute | solution.py:75
  147.1 13.2 %collective-permute-start.17 = (bf16[512,512]{1,0:T(8,128)(2,1)S(1)}, bf16[512,512]{1,0:T(8,128)(2,1)S(1)}, u32[]{:S(2)}, u32[]{:S(2)}) collective-permute-start(bf16[512,512]{1,0:T(8,128)(2,1)S(1)} %collective-permute-done.14.refs_1_.rest_13_), channel_id=1, source_target_pairs={{0,480},{16,496},{32,0},{48,16},{64,32},{80,48},{96,64},{112,80},{... | collective-permute-start | bytes 1572872 | tf_op jit(solution)/shard_map/ppermute | solution.py:75
  153.6 6.7 %collective-permute-start.18 = (bf16[256,512]{1,0:T(8,128)(2,1)S(1)}, bf16[256,512]{1,0:T(8,128)(2,1)S(1)}, u32[]{:S(2)}, u32[]{:S(2)}) collective-permute-start(bf16[256,512]{1,0:T(8,128)(2,1)S(1)} %pick.13), channel_id=1, source_target_pairs={{0,16},{16,0},{32,48},{48,32},{64,80},{80,64},{96,112},{112,96},{1... | collective-permute-start | bytes 786440 | tf_op jit(solution)/shard_map/ppermute | solution.py:78
  159.0 12.6 %copy-start.2 = (bf16[512,512]{1,0:T(8,128)(2,1)}, bf16[512,512]{1,0:T(8,128)(2,1)S(1)}, u32[]{:S(2)}) copy-start(bf16[512,512]{1,0:T(8,128)(2,1)S(1)} %collective-permute-done.16.refs_0_.rest_7_) | copy-start | bytes 1572868
  160.2 11.4 %copy-start.3 = (bf16[512,512]{1,0:T(8,128)(2,1)}, bf16[512,512]{1,0:T(8,128)(2,1)S(1)}, u32[]{:S(2)}) copy-start(bf16[512,512]{1,0:T(8,128)(2,1)S(1)} %collective-permute-done.17.refs_1_.rest_14_) | copy-start | bytes 1572868
  160.3 14.6 %copy-start.25 = (bf16[256,512]{1,0:T(8,128)(2,1)}, bf16[256,512]{1,0:T(8,128)(2,1)S(1)}, u32[]{:S(2)}) copy-start(bf16[256,512]{1,0:T(8,128)(2,1)S(1)} %collective-permute-done.18.rest_22_) | copy-start | bytes 786436
  160.3 13.8 %collective-permute-start.19 = (bf16[256,512]{1,0:T(8,128)(2,1)S(1)}, bf16[256,512]{1,0:T(8,128)(2,1)S(1)}, u32[]{:S(2)}, u32[]{:S(2)}) collective-permute-start(bf16[256,512]{1,0:T(8,128)(2,1)S(1)} %slice.14), channel_id=1, source_target_pairs={{0,32},{16,48},{32,64},{48,80},{64,96},{80,112},{96,128},{112,144}... | collective-permute-start | bytes 786440 | tf_op jit(solution)/shard_map/ppermute | solution.py:75
  162.2 11.9 %collective-permute-start.20 = (bf16[256,512]{1,0:T(8,128)(2,1)S(1)}, bf16[256,512]{1,0:T(8,128)(2,1)S(1)}, u32[]{:S(2)}, u32[]{:S(2)}) collective-permute-start(bf16[256,512]{1,0:T(8,128)(2,1)S(1)} %slice.15), channel_id=1, source_target_pairs={{0,480},{16,496},{32,0},{48,16},{64,32},{80,48},{96,64},{112,80},{... | collective-permute-start | bytes 786440 | tf_op jit(solution)/shard_map/ppermute | solution.py:75
  168.8 10.7 %collective-permute-start.22 = (bf16[256,512]{1,0:T(8,128)(2,1)S(1)}, bf16[256,512]{1,0:T(8,128)(2,1)S(1)}, u32[]{:S(2)}, u32[]{:S(2)}) collective-permute-start(bf16[256,512]{1,0:T(8,128)(2,1)S(1)} %pick.15), channel_id=1, source_target_pairs={{0,16},{16,0},{32,48},{48,32},{64,80},{80,64},{96,112},{112,96},{1... | collective-permute-start | bytes 786440 | tf_op jit(solution)/shard_map/ppermute | solution.py:78
  171.7 7.8 %collective-permute-start.23 = (bf16[256,512]{1,0:T(8,128)(2,1)S(1)}, bf16[256,512]{1,0:T(8,128)(2,1)S(1)}, u32[]{:S(2)}, u32[]{:S(2)}) collective-permute-start(bf16[256,512]{1,0:T(8,128)(2,1)S(1)} %pick.16), channel_id=1, source_target_pairs={{0,16},{16,0},{32,48},{48,32},{64,80},{80,64},{96,112},{112,96},{1... | collective-permute-start | bytes 786440 | tf_op jit(solution)/shard_map/ppermute | solution.py:78
  174.1 5.3 %copy-start.16 = (bf16[256,512]{1,0:T(8,128)(2,1)}, bf16[256,512]{1,0:T(8,128)(2,1)S(1)}, u32[]{:S(2)}) copy-start(bf16[256,512]{1,0:T(8,128)(2,1)S(1)} %collective-permute-done.19.refs_0_.rest_15_) | copy-start | bytes 786436
  174.1 5.3 %copy-start.17 = (bf16[256,512]{1,0:T(8,128)(2,1)}, bf16[256,512]{1,0:T(8,128)(2,1)S(1)}, u32[]{:S(2)}) copy-start(bf16[256,512]{1,0:T(8,128)(2,1)S(1)} %collective-permute-done.20.refs_1_.rest_16_) | copy-start | bytes 786436
  174.9 4.6 %collective-permute-start.24 = (bf16[128,512]{1,0:T(8,128)(2,1)S(1)}, bf16[128,512]{1,0:T(8,128)(2,1)S(1)}, u32[]{:S(2)}, u32[]{:S(2)}) collective-permute-start(bf16[128,512]{1,0:T(8,128)(2,1)S(1)} %pick.17), channel_id=1, source_target_pairs={{0,16},{16,0},{32,48},{48,32},{64,80},{80,64},{96,112},{112,96},{1... | collective-permute-start | bytes 393224 | tf_op jit(solution)/shard_map/ppermute | solution.py:78
  179.4 0.7 copy-start.26
  179.5 0.7 copy-start.29
  179.5 0.8 copy-start.27
  188.6 6.8 %copy-start.30 = (s32[64,8]{0,1:T(8,128)S(1)}, s32[64,8]{0,1:T(8,128)}, u32[]{:S(2)}) copy-start(s32[64,8]{0,1:T(8,128)} %param.14) | copy-start | bytes 6148
  188.6 30.5 %all-to-all-start.2 = ((bf16[16,96,512]{2,1,0:T(8,128)(2,1)}), bf16[16,96,512]{2,1,0:T(8,128)(2,1)S(1)}, u32[]{:S(2)}, u32[]{:S(2)}) async-start(bf16[16,96,512]{2,1,0:T(8,128)(2,1)} %bitcast.18), calls=%async_computation.2 | async-start | bytes 3145728 | tf_op jit(solution)/shard_map/all_to_all | solution.py:365
  195.5 53.6 %copy-start.18 = (bf16[512,512]{1,0:T(8,128)(2,1)S(1)}, bf16[512,512]{1,0:T(8,128)(2,1)}, u32[]{:S(2)}) copy-start(bf16[512,512]{1,0:T(8,128)(2,1)} %attn_ref.1) | copy-start | bytes 1572868
  195.5 53.6 %copy-start.19 = (bf16[512,512]{1,0:T(8,128)(2,1)S(1)}, bf16[512,512]{1,0:T(8,128)(2,1)}, u32[]{:S(2)}) copy-start(bf16[512,512]{1,0:T(8,128)(2,1)} %get-tuple-element.77.agg_ref) | copy-start | bytes 1572868
  195.5 53.6 %copy-start.20 = (f32[512]{0:T(512)S(1)}, f32[512]{0:T(512)}, u32[]{:S(2)}) copy-start(f32[512]{0:T(512)} %param.17) | copy-start | bytes 6148

commit v2 on v0

--- a/solution.py
+++ b/solution.py
@@ -17,52 +17,90 @@
 EXP2_SCALE = math.log2(math.e) / math.sqrt(HDIM)
 
 
-def ring_pieces(x, jobs):
-    results = [None] * len(jobs)
-    n = lax.axis_size("dom")
+def start_copies(place_ref, wanted_ref, whole, halves, slot_of, sems):
+    n = wanted_ref.shape[0]
+    core, z = place_ref[0] % 2, place_ref[0] // 2
+    chips, half = n // 2, n // 4
+    copies = []
+
+    def copy_of(slot, piece, block):
+        rows = pl.ds(pl.multiple_of(block * BLOCK, BLOCK), BLOCK)
+        return pltpu.make_async_copy(piece.at[rows, :], slot_of(slot), sems.at[slot])
+
+    def wanted(step):
+        return wanted_ref[2 * ((z + chips - step) % chips) + core]
+
+    steps = list(range(half)) + [chips - k for k in range(1, half)]
+    for slot, (piece, step) in enumerate(zip(whole, steps)):
+        copies.append(copy_of(slot, piece, wanted(step)))
+        copies[-1].start()
+    slot, first = chips - 1, halves[0].shape[0] // BLOCK
+    block = wanted(half)
+
+    @pl.when(block < first)
+    def _():
+        copy_of(slot, halves[0], block).start()
+
+    @pl.when(block >= first)
+    def _():
+        copy_of(slot, halves[1], block - first).start()
+
+    copies.append(copy_of(slot, halves[0], 0))
+    return copies
+
+
+def pick_kernel(place_ref, wanted_ref, *refs):
+    whole, halves, (out_ref, sems) = refs[:-4], refs[-4:-2], refs[-2:]
+    for copy in start_copies(
+        place_ref, wanted_ref, whole, halves, lambda slot: out_ref.at[slot], sems
+    ):
+        copy.wait()
+
+
+def pick(place, wanted, whole, halves):
+    slots = len(whole) + 1
+    return pl.pallas_call(
+        pick_kernel,
+        out_shape=jax.ShapeDtypeStruct((slots, BLOCK, whole[0].shape[1]), jnp.bfloat16),
+        in_specs=[SM, SM] + [FAR] * (len(whole) + 2),
+        out_specs=VM,
+        scratch_shapes=[pltpu.SemaphoreType.DMA((slots,))],
+        name="pick",
+    )(place, wanted, *whole, *halves)
+
+
+def ring_pieces(x, lists, weights, qkv_weight):
+    n, n_head = lax.axis_size("dom"), lax.axis_size("head")
     half = n // 4
     cut = x.shape[0] // 2
 
     def send(v, by):
         return lax.ppermute(v, "dom", [(i, (i + by) % n) for i in range(n)])
 
-    def trade(v):
-        return lax.ppermute(v, "dom", [(i, i ^ 1) for i in range(n)])
-
     up, down = [x], [x]
-    up_t, down_t = [trade(x)], []
+    weight_t = qkv_weight.T
+    mine = lists.reshape(n)
+    swapped = mine.reshape(n // 2, 2)[:, ::-1].reshape(n)
+    served = lax.all_to_all(
+        jnp.stack([mine, swapped], axis=1), "dom", split_axis=0, concat_axis=0, tiled=True
+    )
+    both = jnp.concatenate(weights, axis=1)
+    both, served = lax.optimization_barrier((both, served))
+    ffn = lax.all_to_all(
+        jnp.broadcast_to(both[None], (n_head,) + both.shape),
+        "head", split_axis=0, concat_axis=0, tiled=True,
+    ).reshape(-1, both.shape[1])
     for k in range(1, half + 1):
-        u_in, d_in = lax.optimization_barrier((up[-1], down[-1]))
-        for i, (_, last, _, _) in enumerate(jobs):
-            if k == last:
-                u_in, results[i] = lax.optimization_barrier((u_in, results[i]))
+        u_in, d_in = up[-1], down[-1]
         if k == half:
             u_in, d_in = u_in[:cut], d_in[cut:]
-        if k >= 3:
-            u_in, up_t[k - 2] = lax.optimization_barrier((u_in, up_t[k - 2]))
-            d_in, down_t[k - 3] = lax.optimization_barrier((d_in, down_t[k - 3]))
+        if k == 6:
+            u_in, weight_t = lax.optimization_barrier((u_in, weight_t))
+        if k == half:
+            u_in, ffn = lax.optimization_barrier((u_in, ffn))
         up.append(send(u_in, 2))
         down.append(send(d_in, -2))
-        up_t.append(trade(up[-1]))
-        down_t.append(trade(down[-1]))
-        for i, (first, _, work, operand) in enumerate(jobs):
-            if k == first:
-                up_t[-1], down_t[-1], operand = lax.optimization_barrier(
-                    (up_t[-1], down_t[-1], operand)
-                )
-                results[i] = work(operand)
-    whole = up[:half] + down[1:half] + up_t[:half] + down_t[: half - 1]
-    return whole + [up[half], down[half], up_t[half], down_t[half - 1]], results
-
-
-def piece_sources(d, n):
-    core, z = d % 2, d // 2
-    chips, half = n // 2, n // 4
-    up = [2 * ((z + chips - k) % chips) + core for k in range(half + 1)]
-    down = [2 * ((z + k) % chips) + core for k in range(half + 1)]
-    near = up[:half] + down[1:half]
-    flip = 1 - 2 * core
-    return near + [p + flip for p in near] + [up[half], up[half] + flip]
+    return up[:half] + down[1:half], [up[half], down[half]], served, ffn, weight_t
 
 
 def slot_of_entry(e, d, blocks, n):
@@ -70,43 +108,26 @@
     core, z = d % 2, d // 2
     chips, half = n // 2, n // 4
     k = (z + chips - p // 2) % chips
-    other = jnp.where((p % 2) == core, 0, 1)
+    other = jnp.where((p % 2) == core, 0, chips)
     near = jnp.where(k < half, k, half - 1 + chips - k)
-    piece = jnp.where(k == half, 2 * (2 * half - 1) + other, near + other * (2 * half - 1))
-    return jnp.where(e < blocks, e, blocks + piece)
+    near = jnp.where(k == half, chips - 1, near)
+    return jnp.where(e < blocks, e, blocks + other + near)
 
 
 def aggregate_kernel(place_ref, entry_ref, serve_ref, pattern_ref, own_ref, wt_ref, *rest):
     pieces, (agg_ref, qkv_ref, table, sems) = rest[:-4], rest[-4:]
     blocks, tiles = pattern_ref.shape[0], pattern_ref.shape[1]
-    whole, halves = pieces[:-4], pieces[-4:]
-    n_dom = len(pieces) - 2
+    n_dom = serve_ref.shape[0]
+    chips = n_dom // 2
     d = place_ref[0]
-    sources = piece_sources(d, n_dom)
-    copies = []
-
-    def copy_of(i, piece, block):
-        start = pl.multiple_of(block * BLOCK, BLOCK)
-        return pltpu.make_async_copy(
-            piece.at[pl.ds(start, BLOCK), :], table.at[blocks + i], sems.at[i]
-        )
-
-    for i, piece in enumerate(whole):
-        copies.append(copy_of(i, piece, serve_ref[sources[i]]))
-        copies[-1].start()
-    for i in range(2):
-        slot, first = len(whole) + i, blocks // 2
-        block = serve_ref[sources[slot]]
-
-        @pl.when(block < first)
-        def _(slot=slot, piece=halves[2 * i], block=block):
-            copy_of(slot, piece, block).start()
-
-        @pl.when(block >= first)
-        def _(slot=slot, piece=halves[2 * i + 1], block=block - first):
-            copy_of(slot, piece, block).start()
-
-        copies.append(copy_of(slot, halves[2 * i], 0))
+    copies = start_copies(
+        place_ref, serve_ref, pieces[:-3], pieces[-3:-1], lambda slot: table.at[blocks + slot], sems
+    )
+    handed = pltpu.make_async_copy(
+        pieces[-1], table.at[pl.ds(blocks + chips, chips)], sems.at[chips]
+    )
+    handed.start()
+    copies.append(handed)
     for b in range(blocks):
         table[b] = own_ref[b * BLOCK : (b + 1) * BLOCK, :]
     for copy in copies:
@@ -161,8 +182,8 @@
         in_specs=[SM, SM, SM, VM, VM, VM] + [FAR] * len(pieces),
         out_specs=(VM, VM),
         scratch_shapes=[
-            pltpu.VMEM((blocks + len(pieces) - 2, BLOCK, width), jnp.bfloat16),
-            pltpu.SemaphoreType.DMA((len(pieces) - 2,)),
+            pltpu.VMEM((blocks + serve.shape[0], BLOCK, width), jnp.bfloat16),
+            pltpu.SemaphoreType.DMA((serve.shape[0] // 2 + 1,)),
         ],
         name="aggregate",
     )(place, entries, serve, pattern, own, weight_t, *pieces)
@@ -287,31 +308,21 @@
     expand_weight,
     reduce_weight,
 ):
-    n_dom, n_head = lax.axis_size("dom"), lax.axis_size("head")
+    n_head = lax.axis_size("head")
     width = features.shape[1]
     rows = features.shape[0]
 
-    def exchange_lists(lists):
-        return lax.all_to_all(
-            lists.reshape(n_dom, 1), "dom", split_axis=0, concat_axis=0, tiled=True
-        ).reshape(n_dom)
-
-    def gather_ffn(weights):
-        both = jnp.concatenate(weights, axis=1)
-        return lax.all_to_all(
-            jnp.broadcast_to(both[None], (n_head,) + both.shape),
-            "head", split_axis=0, concat_axis=0, tiled=True,
-        ).reshape(-1, 2 * width)
-
-    jobs = [
-        (1, 5, exchange_lists, serve_list),
-        (2, None, gather_ffn, (expand_weight, reduce_weight)),
-        (4, 7, jnp.transpose, qkv_weight),
-    ]
-    pieces, (served, ffn, weight_t) = ring_pieces(features, jobs)
     place = lax.axis_index("dom").reshape(1)
+    n_dom = lax.axis_size("dom")
+    whole, halves, served, ffn, weight_t = ring_pieces(
+        features, serve_list, (expand_weight, reduce_weight), qkv_weight
+    )
+    handed = lax.ppermute(
+        pick(place, served[:, 1], whole, halves), "dom", [(i, i ^ 1) for i in range(n_dom)]
+    )
     agg, qkv_t = aggregate(
-        place, tile_source, served, tile_pattern, features, weight_t, pieces
+        place, tile_source, served[:, 0], tile_pattern, features, weight_t,
+        whole + halves + [handed],
     )
     qkv = lax.all_to_all(
         qkv_t.reshape(n_head, 3 * HDIM, rows), "head", split_axis=0, concat_axis=0, tiled=True

time: 295 us -> 242 us (0.82)
  starting transfers between devices: 110 us -> 88.2 us
  blocking collectives: 34.4 us -> 13.5 us
  waiting for transfers between devices: 110 us -> 91 us
  Pallas kernels: 31.5 us -> 35.2 us
  local copies, waits for them, and re-layouts: 6.08 us -> 9.54 us
    ppermute x17 -> x1, starting transfers between devices: 36 us -> 1.92 us  [shards(): lax.ppermute(pick(place, served[:, 1], whole, halves), 'dom', [(i, i ^ 1)...]
    all_to_all x1 -> x2, waiting for transfers between devices: 36.6 us -> 11.4 us  [the longest x1 11.4 us: ring_pieces(): lax.all_to_all(jnp.stack([mine, swapped], axis=1), 'dom', split_axis=0, c...]
    all_to_all x1 -> x0, blocking collectives: 20.7 us -> none  [exchange_lists(): lax.all_to_all(lists.reshape(n_dom, 1), 'dom', split_axis=0, concat_axis=...]
    all_to_all x1 -> x2, starting transfers between devices: 5.86 us -> 23 us  [the longest x1 15.5 us: ring_pieces(): lax.all_to_all(jnp.stack([mine, swapped], axis=1), 'dom', split_axis=0, c...]
    unnamed x47 -> x43, local copies, waits for them, and re-layouts: 0.18 us -> 5.31 us
    ppermute x16, starting transfers between devices: 60.5 us -> 56.4 us  [send(): return lax.ppermute(v, 'dom', [(i, (i + by) % n) for i in range(n)])]
    pallas_call x0 -> x1, Pallas kernels: none -> 3.81 us  [pick(): pl.pallas_call(pick_kernel, out_shape=jax.ShapeDtypeStruct((slots, BLOCK,...]
    ppermute x16, waiting for transfers between devices: 48.9 us -> 52.3 us  [send(): return lax.ppermute(v, 'dom', [(i, (i + by) % n) for i in range(n)])]
  transfers between devices with their start and end apart: 35 -> 20, of which waited for: 16 -> 14; matrix products, arithmetic and copies ran while one was open for 2% -> 2% of each run, Pallas kernels for 5% -> 0%
where the time goes in v2:
time: 242 us; the launch traced here: 241 us
  waiting for transfers between devices  91 us (38%)
  starting transfers between devices  88.2 us (36%)
  Pallas kernels  35.2 us (15%)
  blocking collectives  13.5 us (6%)
  local copies, waits for them, and re-layouts  9.54 us (4%)
  other arithmetic  2.97 us (1%)
    ppermute x16, starting transfers between devices, send(): return lax.ppermute(v, 'dom', [(i, (i + by) % n) for i in range(n)])  56.4 us
    ppermute x16, waiting for transfers between devices, send(): return lax.ppermute(v, 'dom', [(i, (i + by) % n) for i in range(n)])  52.3 us
    all_to_all x1, waiting for transfers between devices, shards(): lax.all_to_all(qkv_t.reshape(n_head, 3 * HDIM, rows), 'head', split_axis=...  22.9 us
    pallas_call x1, Pallas kernels, attend(): pl.pallas_call(attend_kernel, out_shape=jax.ShapeDtypeStruct((sources, HD...  15.7 us
    all_to_all x1, starting transfers between devices, ring_pieces(): lax.all_to_all(jnp.stack([mine, swapped], axis=1), 'dom', split_axis=0, c...  15.5 us
    all_to_all x1, blocking collectives, shards(): lax.all_to_all(context, 'head', split_axis=0, concat_axis=0, tiled=True)  13.5 us
    all_to_all x1, waiting for transfers between devices, ring_pieces(): lax.all_to_all(jnp.stack([mine, swapped], axis=1), 'dom', split_axis=0, c...  11.4 us
    pallas_call x1, Pallas kernels, aggregate(): pl.pallas_call(aggregate_kernel, out_shape=(jax.ShapeDtypeStruct((rows, w...  8.34 us
  transfers between devices with their start and end apart: 20, of which 14 were waited for; matrix products, arithmetic and copies ran while one was open for 2% of the time, Pallas kernels for 0%

profile of v2, /device:TPU:8, one launch (start us, length us, event | category | flops | bytes accessed | tf_op | source)
XLA Modules:
  0.0 240.8 jit_solution(7947352447069684962)
XLA Ops:
  0.0 0.5 broadcast.4
  0.5 1.3 reduce.3
  1.8 0.1 reshape_reshape.3
  1.9 0.1 rev.3
  2.0 0.1 stack_reshape.7
  2.1 0.7 add_bitcast_fusion
  2.8 0.7 copy.15
  3.5 15.5 %all-to-all-start = ((s32[32,1,2]{2,1,0:T(1,128)}), s32[32,1,2]{2,1,0:T(1,128)S(1)}, u32[]{:S(2)}, u32[]{:S(2)}) async-start(s32[32,1,2]{2,1,0:T(1,128)} %copy.15), calls=%async_computation | async-start | bytes 32768 | tf_op jit(solution)/shard_map/all_to_all | solution.py:84
  18.9 1.0 pad_maximum_fusion
  19.9 11.4 %all-to-all-done = s32[32,1,2]{2,1,0:T(1,128)S(1)} async-done(((s32[32,1,2]{2,1,0:T(1,128)}), s32[32,1,2]{2,1,0:T(1,128)S(1)}, u32[]{:S(2)}, u32[]{:S(2)}) %all-to-all-start) | async-done | bytes 288 | tf_op jit(solution)/shard_map/all_to_all | solution.py:84
  31.4 0.1 copy.16
  31.4 2.6 %broadcast_in_dim.2 = bf16[16,128,1024]{2,1,0:T(8,128)(2,1)} broadcast(bf16[128,1024]{1,0:T(8,128)(2,1)S(1)} %pad_maximum_fusion), dimensions={1,2} | broadcast | bytes 4456448 | tf_op jit(solution)/shard_map/broadcast_in_dim | solution.py:90
  34.0 7.5 %all-to-all-start.1 = ((bf16[16,128,1024]{2,1,0:T(8,128)(2,1)}), bf16[16,128,1024]{2,1,0:T(8,128)(2,1)}, u32[]{:S(2)}, u32[]{:S(2)}) async-start(bf16[16,128,1024]{2,1,0:T(8,128)(2,1)} %broadcast_in_dim.2), calls=%async_computation.1 | async-start | bytes 8388608 | tf_op jit(solution)/shard_map/all_to_all | solution.py:89
  41.5 2.2 collective-permute-start.7
  43.8 3.6 %collective-permute-start = (bf16[512,512]{1,0:T(8,128)(2,1)S(1)}, bf16[512,512]{1,0:T(8,128)(2,1)S(1)}, u32[]{:S(2)}, u32[]{:S(2)}) collective-permute-start(bf16[512,512]{1,0:T(8,128)(2,1)S(1)} %copy-done.3), channel_id=1, source_target_pairs={{0,32},{16,48},{32,64},{48,80},{64,96},{80,112},{96,128},{112,144}... | collective-permute-start | bytes 1572872 | tf_op jit(solution)/shard_map/ppermute | solution.py:78
  47.4 8.9 %collective-permute-done.7.refs_8_.rest_8_ = bf16[512,512]{1,0:T(8,128)(2,1)S(1)} collective-permute-done((bf16[512,512]{1,0:T(8,128)(2,1)S(1)}, bf16[512,512]{1,0:T(8,128)(2,1)S(1)}, u32[]{:S(2)}, u32[]{:S(2)}) %collective-permute-start.7) | collective-permute-done | bytes 524320 | tf_op jit(solution)/shard_map/ppermute | solution.py:78
  56.3 3.7 %collective-permute-start.8 = (bf16[512,512]{1,0:T(8,128)(2,1)S(1)}, bf16[512,512]{1,0:T(8,128)(2,1)S(1)}, u32[]{:S(2)}, u32[]{:S(2)}) collective-permute-start(bf16[512,512]{1,0:T(8,128)(2,1)S(1)} %collective-permute-done.7.refs_8_.rest_8_), channel_id=1, source_target_pairs={{0,480},{16,496},{32,0},{48,16},{64,32},{80,48},{96,64},{112,80},{... | collective-permute-start | bytes 1572872 | tf_op jit(solution)/shard_map/ppermute | solution.py:78
  60.1 0.0 collective-permute-done.refs_1_.rest_1_
  60.1 0.0 copy-start.8
  60.1 2.1 collective-permute-start.1
  62.2 8.1 %collective-permute-done.8.refs_9_.rest_9_ = bf16[512,512]{1,0:T(8,128)(2,1)S(1)} collective-permute-done((bf16[512,512]{1,0:T(8,128)(2,1)S(1)}, bf16[512,512]{1,0:T(8,128)(2,1)S(1)}, u32[]{:S(2)}, u32[]{:S(2)}) %collective-permute-start.8) | collective-permute-done | bytes 524320 | tf_op jit(solution)/shard_map/ppermute | solution.py:78
  70.3 5.3 %collective-permute-start.9 = (bf16[512,512]{1,0:T(8,128)(2,1)S(1)}, bf16[512,512]{1,0:T(8,128)(2,1)S(1)}, u32[]{:S(2)}, u32[]{:S(2)}) collective-permute-start(bf16[512,512]{1,0:T(8,128)(2,1)S(1)} %collective-permute-done.8.refs_9_.rest_9_), channel_id=1, source_target_pairs={{0,480},{16,496},{32,0},{48,16},{64,32},{80,48},{96,64},{112,80},{... | collective-permute-start | bytes 1572872 | tf_op jit(solution)/shard_map/ppermute | solution.py:78
  75.6 0.0 collective-permute-done.1.refs_2_.rest_2_
  75.6 0.0 copy-start.10
  75.6 1.9 collective-permute-start.2
  77.5 7.2 %collective-permute-done.9.refs_10_.rest_10_ = bf16[512,512]{1,0:T(8,128)(2,1)S(1)} collective-permute-done((bf16[512,512]{1,0:T(8,128)(2,1)S(1)}, bf16[512,512]{1,0:T(8,128)(2,1)S(1)}, u32[]{:S(2)}, u32[]{:S(2)}) %collective-permute-start.9) | collective-permute-done | bytes 524320 | tf_op jit(solution)/shard_map/ppermute | solution.py:78
  84.7 5.6 %collective-permute-start.10 = (bf16[512,512]{1,0:T(8,128)(2,1)S(1)}, bf16[512,512]{1,0:T(8,128)(2,1)S(1)}, u32[]{:S(2)}, u32[]{:S(2)}) collective-permute-start(bf16[512,512]{1,0:T(8,128)(2,1)S(1)} %collective-permute-done.9.refs_10_.rest_10_), channel_id=1, source_target_pairs={{0,480},{16,496},{32,0},{48,16},{64,32},{80,48},{96,64},{112,80},{... | collective-permute-start | bytes 1572872 | tf_op jit(solution)/shard_map/ppermute | solution.py:78
  90.3 0.0 collective-permute-done.2.refs_3_.rest_3_
  90.4 1.9 collective-permute-start.3
  92.3 6.4 %collective-permute-done.10.refs_11_.rest_11_ = bf16[512,512]{1,0:T(8,128)(2,1)S(1)} collective-permute-done((bf16[512,512]{1,0:T(8,128)(2,1)S(1)}, bf16[512,512]{1,0:T(8,128)(2,1)S(1)}, u32[]{:S(2)}, u32[]{:S(2)}) %collective-permute-start.10) | collective-permute-done | bytes 524320 | tf_op jit(solution)/shard_map/ppermute | solution.py:78
  98.7 5.6 %collective-permute-start.11 = (bf16[512,512]{1,0:T(8,128)(2,1)S(1)}, bf16[512,512]{1,0:T(8,128)(2,1)}, u32[]{:S(2)}, u32[]{:S(2)}) collective-permute-start(bf16[512,512]{1,0:T(8,128)(2,1)S(1)} %collective-permute-done.10.refs_11_.rest_11_), channel_id=1, source_target_pairs={{0,480},{16,496},{32,0},{48,16},{64,32},{80,48},{96,64},{112,80},{... | collective-permute-start | bytes 1572872 | tf_op jit(solution)/shard_map/ppermute | solution.py:78
  104.3 0.0 collective-permute-done.3.refs_4_.rest_4_
  104.3 1.9 collective-permute-start.4
  106.2 2.6 %copy.17 = bf16[512,1536]{0,1:T(8,128)(2,1)} copy(bf16[512,1536]{1,0:T(8,128)(2,1)} %param.15) | data formatting | bytes 3145728 | tf_op args[5]
  108.8 2.9 %collective-permute-done.11.refs_12_.rest_12_ = bf16[512,512]{1,0:T(8,128)(2,1)} collective-permute-done((bf16[512,512]{1,0:T(8,128)(2,1)S(1)}, bf16[512,512]{1,0:T(8,128)(2,1)}, u32[]{:S(2)}, u32[]{:S(2)}) %collective-permute-start.11) | collective-permute-done | bytes 524320 | tf_op jit(solution)/shard_map/ppermute | solution.py:78
  111.7 5.7 %collective-permute-start.12 = (bf16[512,512]{1,0:T(8,128)(2,1)}, bf16[512,512]{1,0:T(8,128)(2,1)S(1)}, u32[]{:S(2)}, u32[]{:S(2)}) collective-permute-start(bf16[512,512]{1,0:T(8,128)(2,1)} %collective-permute-done.11.refs_12_.rest_12_), channel_id=1, source_target_pairs={{0,480},{16,496},{32,0},{48,16},{64,32},{80,48},{96,64},{112,80},{... | collective-permute-start | bytes 1572872 | tf_op jit(solution)/shard_map/ppermute | solution.py:78
  117.4 0.0 collective-permute-done.4.refs_5_.rest_5_
  117.5 1.9 collective-permute-start.5
  119.4 5.2 %collective-permute-done.12.refs_13_.rest_13_ = bf16[512,512]{1,0:T(8,128)(2,1)S(1)} collective-permute-done((bf16[512,512]{1,0:T(8,128)(2,1)}, bf16[512,512]{1,0:T(8,128)(2,1)S(1)}, u32[]{:S(2)}, u32[]{:S(2)}) %collective-permute-start.12) | collective-permute-done | bytes 524320 | tf_op jit(solution)/shard_map/ppermute | solution.py:78
  124.6 5.5 %collective-permute-start.13 = (bf16[512,512]{1,0:T(8,128)(2,1)S(1)}, bf16[512,512]{1,0:T(8,128)(2,1)S(1)}, u32[]{:S(2)}, u32[]{:S(2)}) collective-permute-start(bf16[512,512]{1,0:T(8,128)(2,1)S(1)} %collective-permute-done.12.refs_13_.rest_13_), channel_id=1, source_target_pairs={{0,480},{16,496},{32,0},{48,16},{64,32},{80,48},{96,64},{112,80},{... | collective-permute-start | bytes 1572872 | tf_op jit(solution)/shard_map/ppermute | solution.py:78
  130.1 0.4 collective-permute-done.5.refs_6_.rest_6_
  130.5 1.9 collective-permute-start.6
  132.4 5.7 %collective-permute-done.13.refs_14_.rest_14_ = bf16[512,512]{1,0:T(8,128)(2,1)S(1)} collective-permute-done((bf16[512,512]{1,0:T(8,128)(2,1)S(1)}, bf16[512,512]{1,0:T(8,128)(2,1)S(1)}, u32[]{:S(2)}, u32[]{:S(2)}) %collective-permute-start.13) | collective-permute-done | bytes 524320 | tf_op jit(solution)/shard_map/ppermute | solution.py:78
  138.1 5.6 %collective-permute-start.15 = (bf16[256,512]{1,0:T(8,128)(2,1)S(1)}, bf16[256,512]{1,0:T(8,128)(2,1)S(1)}, u32[]{:S(2)}, u32[]{:S(2)}) collective-permute-start(bf16[256,512]{1,0:T(8,128)(2,1)S(1)} %slice.17), channel_id=1, source_target_pairs={{0,480},{16,496},{32,0},{48,16},{64,32},{80,48},{96,64},{112,80},{... | collective-permute-start | bytes 786440 | tf_op jit(solution)/shard_map/ppermute | solution.py:78
  143.7 0.6 collective-permute-done.6.refs_7_.rest_7_
  144.3 0.0 all-to-all-done.1
  144.3 1.9 collective-permute-start.14
  146.3 0.6 slice_bitcast_fusion
  146.8 0.7 collective-permute-done.15.refs_16_.rest_16_
  147.6 6.2 %collective-permute-done.14.refs_15_.rest_15_ = bf16[256,512]{1,0:T(8,128)(2,1)S(1)} collective-permute-done((bf16[256,512]{1,0:T(8,128)(2,1)S(1)}, bf16[256,512]{1,0:T(8,128)(2,1)S(1)}, u32[]{:S(2)}, u32[]{:S(2)}) %collective-permute-start.14) | collective-permute-done | bytes 262176 | tf_op jit(solution)/shard_map/ppermute | solution.py:78
  153.8 0.7 copy-done.18
  154.5 3.8 %pick.1 = bf16[16,128,512]{2,1,0:T(8,128)(2,1)} custom-call(s32[1]{0:T(128)} %bitcast.place_ref, s32[32]{0:T(128)} %get-tuple-element.21.wanted_ref, bf16[512,512]{1,0:T(8,128)(2,1)} %rest_0_.1, bf16[512,512]{1,0:T(8,128)(2,1)} %copy-done.8, bf16[512,512]{1,0:T(8,128)(2,1)} %copy-done.10, bf16[512,512]{1,0:T(8,128)(2,1)} %copy-done.12, ...), custom_call_target="tpu_custom_call" | custom-call | tf_op jit(solution)/shard_map/pick/pallas_call | solution.py:62
  158.3 1.9 collective-permute-start.16
  160.2 4.3 %collective-permute-done.16.rest_17_ = bf16[16,128,512]{2,1,0:T(8,128)(2,1)S(1)} collective-permute-done((bf16[16,128,512]{2,1,0:T(8,128)(2,1)}, bf16[16,128,512]{2,1,0:T(8,128)(2,1)S(1)}, u32[]{:S(2)}, u32[]{:S(2)}) %collective-permute-start.16) | collective-permute-done | bytes 2097184 | tf_op jit(solution)/shard_map/ppermute | solution.py:320
  164.6 1.4 copy-done.6
  166.0 8.3 %aggregate.1 = (bf16[512,512]{1,0:T(8,128)(2,1)}, bf16[1536,512]{1,0:T(8,128)(2,1)}) custom-call(s32[1]{0:T(128)} %bitcast.place_ref, s32[4,6]{1,0:T(4,128)} %entry_ref.1, s32[32]{0:T(128)} %get-tuple-element.22.serve_ref, s32[4,6,128,128]{3,2,1,0:T(8,128)} %pattern_ref.1, bf16[512,512]{1,0:T(8,128)(2,1)} %rest_0_.1, bf16[1536,512]{1,0:T(8,128)(2,1)} %bitcast.17, ...), custom_call_target="tpu_custom_call" | custom-call | tf_op jit(solution)/shard_map/aggregate/pallas_call | solution.py:176
  174.3 0.0 copy-start.19
  174.3 6.8 %all-to-all-start.2 = ((bf16[16,96,512]{2,1,0:T(8,128)(2,1)}), bf16[16,96,512]{2,1,0:T(8,128)(2,1)S(1)}, u32[]{:S(2)}, u32[]{:S(2)}) async-start(bf16[16,96,512]{2,1,0:T(8,128)(2,1)} %bitcast.18), calls=%async_computation.2 | async-start | bytes 3145728 | tf_op jit(solution)/shard_map/all_to_all | solution.py:327
  181.2 0.1 copy.18.key_ref
  181.3 0.0 copy-start.2
  181.3 22.9 %all-to-all-done.2.qkv_ref = bf16[16,96,512]{2,1,0:T(8,128)(2,1)S(1)} async-done(((bf16[16,96,512]{2,1,0:T(8,128)(2,1)}), bf16[16,96,512]{2,1,0:T(8,128)(2,1)S(1)}, u32[]{:S(2)}, u32[]{:S(2)}) %all-to-all-start.2) | async-done | bytes 1572896 | tf_op jit(solution)/shard_map/all_to_all | solution.py:327
  204.2 15.7 %attend.1 = bf16[16,32,512]{2,1,0:T(8,128)(2,1)S(1)} custom-call(s32[64,8]{1,0:T(8,128)S(1)} %copy.18.key_ref, bf16[16,96,512]{2,1,0:T(8,128)(2,1)S(1)} %all-to-all-done.2.qkv_ref), custom_call_target="tpu_custom_call" | custom-call | tf_op jit(solution)/shard_map/attend/pallas_call | solution.py:241
  219.9 13.5 %all_to_all.27 = bf16[16,32,512]{2,1,0:T(8,128)(2,1)S(1)} all-to-all(bf16[16,32,512]{2,1,0:T(8,128)(2,1)S(1)} %attend.1), channel_id=1, replica_groups=mesh['dom'=32,'head'=16] {'head'}, dimensions={0} | all-to-all | bytes 1048576 | tf_op jit(solution)/shard_map/all_to_all | solution.py:331
  233.4 7.4 %finish.1 = bf16[512,512]{1,0:T(8,128)(2,1)} custom-call(bf16[512,512]{1,0:T(8,128)(2,1)S(1)} %bitcast.15, bf16[512,512]{1,0:T(8,128)(2,1)S(1)} %copy-done.1, bf16[512,512]{1,0:T(8,128)(2,1)S(1)} %copy-done, f32[1,512]{1,0:T(1,128)S(1)} %bitcast.16, bf16[2048,1024]{1,0:T(8,128)(2,1)} %bitcast.6.ffn_ref), custom_call_target="tpu_custom_call" | custom-call | tf_op jit(solution)/shard_map/finish/pallas_call | solution.py:285
  (36 shorter events, 0.1 us)
Async XLA Ops:
  3.5 27.9 %all-to-all-start = ((s32[32,1,2]{2,1,0:T(1,128)}), s32[32,1,2]{2,1,0:T(1,128)S(1)}, u32[]{:S(2)}, u32[]{:S(2)}) async-start(s32[32,1,2]{2,1,0:T(1,128)} %copy.15), calls=%async_computation | async-start | bytes 32768 | tf_op jit(solution)/shard_map/all_to_all | solution.py:84
  34.0 7.5 %copy-start.3 = (bf16[512,512]{1,0:T(8,128)(2,1)S(1)}, bf16[512,512]{1,0:T(8,128)(2,1)}, u32[]{:S(2)}) copy-start(bf16[512,512]{1,0:T(8,128)(2,1)} %rest_0_.1) | copy-start | bytes 1572868
  34.0 110.3 %all-to-all-start.1 = ((bf16[16,128,1024]{2,1,0:T(8,128)(2,1)}), bf16[16,128,1024]{2,1,0:T(8,128)(2,1)}, u32[]{:S(2)}, u32[]{:S(2)}) async-start(bf16[16,128,1024]{2,1,0:T(8,128)(2,1)} %broadcast_in_dim.2), calls=%async_computation.1 | async-start | bytes 8388608 | tf_op jit(solution)/shard_map/all_to_all | solution.py:89
  41.5 14.8 %collective-permute-start.7 = (bf16[512,512]{1,0:T(8,128)(2,1)S(1)}, bf16[512,512]{1,0:T(8,128)(2,1)S(1)}, u32[]{:S(2)}, u32[]{:S(2)}) collective-permute-start(bf16[512,512]{1,0:T(8,128)(2,1)S(1)} %copy-done.3), channel_id=1, source_target_pairs={{0,480},{16,496},{32,0},{48,16},{64,32},{80,48},{96,64},{112,80},{... | collective-permute-start | bytes 1572872 | tf_op jit(solution)/shard_map/ppermute | solution.py:78
  43.8 16.3 %collective-permute-start = (bf16[512,512]{1,0:T(8,128)(2,1)S(1)}, bf16[512,512]{1,0:T(8,128)(2,1)S(1)}, u32[]{:S(2)}, u32[]{:S(2)}) collective-permute-start(bf16[512,512]{1,0:T(8,128)(2,1)S(1)} %copy-done.3), channel_id=1, source_target_pairs={{0,32},{16,48},{32,64},{48,80},{64,96},{80,112},{96,128},{112,144}... | collective-permute-start | bytes 1572872 | tf_op jit(solution)/shard_map/ppermute | solution.py:78
  56.3 61.1 %copy-start.7 = (bf16[512,512]{1,0:T(8,128)(2,1)}, bf16[512,512]{1,0:T(8,128)(2,1)S(1)}, u32[]{:S(2)}) copy-start(bf16[512,512]{1,0:T(8,128)(2,1)S(1)} %collective-permute-done.7.refs_8_.rest_8_) | copy-start | bytes 1572868
  56.3 14.0 %collective-permute-start.8 = (bf16[512,512]{1,0:T(8,128)(2,1)S(1)}, bf16[512,512]{1,0:T(8,128)(2,1)S(1)}, u32[]{:S(2)}, u32[]{:S(2)}) collective-permute-start(bf16[512,512]{1,0:T(8,128)(2,1)S(1)} %collective-permute-done.7.refs_8_.rest_8_), channel_id=1, source_target_pairs={{0,480},{16,496},{32,0},{48,16},{64,32},{80,48},{96,64},{112,80},{... | collective-permute-start | bytes 1572872 | tf_op jit(solution)/shard_map/ppermute | solution.py:78
  60.1 57.4 %copy-start.8 = (bf16[512,512]{1,0:T(8,128)(2,1)}, bf16[512,512]{1,0:T(8,128)(2,1)S(1)}, u32[]{:S(2)}) copy-start(bf16[512,512]{1,0:T(8,128)(2,1)S(1)} %collective-permute-done.refs_1_.rest_1_) | copy-start | bytes 1572868
  60.1 15.5 %collective-permute-start.1 = (bf16[512,512]{1,0:T(8,128)(2,1)S(1)}, bf16[512,512]{1,0:T(8,128)(2,1)S(1)}, u32[]{:S(2)}, u32[]{:S(2)}) collective-permute-start(bf16[512,512]{1,0:T(8,128)(2,1)S(1)} %collective-permute-done.refs_1_.rest_1_), channel_id=1, source_target_pairs={{0,32},{16,48},{32,64},{48,80},{64,96},{80,112},{96,128},{112,144}... | collective-permute-start | bytes 1572872 | tf_op jit(solution)/shard_map/ppermute | solution.py:78
  70.3 47.1 %copy-start.9 = (bf16[512,512]{1,0:T(8,128)(2,1)}, bf16[512,512]{1,0:T(8,128)(2,1)S(1)}, u32[]{:S(2)}) copy-start(bf16[512,512]{1,0:T(8,128)(2,1)S(1)} %collective-permute-done.8.refs_9_.rest_9_) | copy-start | bytes 1572868
  70.3 14.4 %collective-permute-start.9 = (bf16[512,512]{1,0:T(8,128)(2,1)S(1)}, bf16[512,512]{1,0:T(8,128)(2,1)S(1)}, u32[]{:S(2)}, u32[]{:S(2)}) collective-permute-start(bf16[512,512]{1,0:T(8,128)(2,1)S(1)} %collective-permute-done.8.refs_9_.rest_9_), channel_id=1, source_target_pairs={{0,480},{16,496},{32,0},{48,16},{64,32},{80,48},{96,64},{112,80},{... | collective-permute-start | bytes 1572872 | tf_op jit(solution)/shard_map/ppermute | solution.py:78
  75.6 41.9 %copy-start.10 = (bf16[512,512]{1,0:T(8,128)(2,1)}, bf16[512,512]{1,0:T(8,128)(2,1)S(1)}, u32[]{:S(2)}) copy-start(bf16[512,512]{1,0:T(8,128)(2,1)S(1)} %collective-permute-done.1.refs_2_.rest_2_) | copy-start | bytes 1572868
  75.6 14.8 %collective-permute-start.2 = (bf16[512,512]{1,0:T(8,128)(2,1)S(1)}, bf16[512,512]{1,0:T(8,128)(2,1)S(1)}, u32[]{:S(2)}, u32[]{:S(2)}) collective-permute-start(bf16[512,512]{1,0:T(8,128)(2,1)S(1)} %collective-permute-done.1.refs_2_.rest_2_), channel_id=1, source_target_pairs={{0,32},{16,48},{32,64},{48,80},{64,96},{80,112},{96,128},{112,144}... | collective-permute-start | bytes 1572872 | tf_op jit(solution)/shard_map/ppermute | solution.py:78
  84.7 5.6 %copy-start.11 = (bf16[512,512]{1,0:T(8,128)(2,1)}, bf16[512,512]{1,0:T(8,128)(2,1)S(1)}, u32[]{:S(2)}) copy-start(bf16[512,512]{1,0:T(8,128)(2,1)S(1)} %collective-permute-done.9.refs_10_.rest_10_) | copy-start | bytes 1572868
  84.7 13.9 %collective-permute-start.10 = (bf16[512,512]{1,0:T(8,128)(2,1)S(1)}, bf16[512,512]{1,0:T(8,128)(2,1)S(1)}, u32[]{:S(2)}, u32[]{:S(2)}) collective-permute-start(bf16[512,512]{1,0:T(8,128)(2,1)S(1)} %collective-permute-done.9.refs_10_.rest_10_), channel_id=1, source_target_pairs={{0,480},{16,496},{32,0},{48,16},{64,32},{80,48},{96,64},{112,80},{... | collective-permute-start | bytes 1572872 | tf_op jit(solution)/shard_map/ppermute | solution.py:78
  90.4 8.3 %copy-start.12 = (bf16[512,512]{1,0:T(8,128)(2,1)}, bf16[512,512]{1,0:T(8,128)(2,1)S(1)}, u32[]{:S(2)}) copy-start(bf16[512,512]{1,0:T(8,128)(2,1)S(1)} %collective-permute-done.2.refs_3_.rest_3_) | copy-start | bytes 1572868
  90.4 13.9 %collective-permute-start.3 = (bf16[512,512]{1,0:T(8,128)(2,1)S(1)}, bf16[512,512]{1,0:T(8,128)(2,1)S(1)}, u32[]{:S(2)}, u32[]{:S(2)}) collective-permute-start(bf16[512,512]{1,0:T(8,128)(2,1)S(1)} %collective-permute-done.2.refs_3_.rest_3_), channel_id=1, source_target_pairs={{0,32},{16,48},{32,64},{48,80},{64,96},{80,112},{96,128},{112,144}... | collective-permute-start | bytes 1572872 | tf_op jit(solution)/shard_map/ppermute | solution.py:78
  98.7 18.8 %copy-start.13 = (bf16[512,512]{1,0:T(8,128)(2,1)}, bf16[512,512]{1,0:T(8,128)(2,1)S(1)}, u32[]{:S(2)}) copy-start(bf16[512,512]{1,0:T(8,128)(2,1)S(1)} %collective-permute-done.10.refs_11_.rest_11_) | copy-start | bytes 1572868
  98.7 13.1 %collective-permute-start.11 = (bf16[512,512]{1,0:T(8,128)(2,1)S(1)}, bf16[512,512]{1,0:T(8,128)(2,1)}, u32[]{:S(2)}, u32[]{:S(2)}) collective-permute-start(bf16[512,512]{1,0:T(8,128)(2,1)S(1)} %collective-permute-done.10.refs_11_.rest_11_), channel_id=1, source_target_pairs={{0,480},{16,496},{32,0},{48,16},{64,32},{80,48},{96,64},{112,80},{... | collective-permute-start | bytes 1572872 | tf_op jit(solution)/shard_map/ppermute | solution.py:78
  104.3 13.2 %copy-start.14 = (bf16[512,512]{1,0:T(8,128)(2,1)}, bf16[512,512]{1,0:T(8,128)(2,1)S(1)}, u32[]{:S(2)}) copy-start(bf16[512,512]{1,0:T(8,128)(2,1)S(1)} %collective-permute-done.3.refs_4_.rest_4_) | copy-start | bytes 1572868
  104.3 13.1 %collective-permute-start.4 = (bf16[512,512]{1,0:T(8,128)(2,1)S(1)}, bf16[512,512]{1,0:T(8,128)(2,1)}, u32[]{:S(2)}, u32[]{:S(2)}) collective-permute-start(bf16[512,512]{1,0:T(8,128)(2,1)S(1)} %collective-permute-done.3.refs_4_.rest_4_), channel_id=1, source_target_pairs={{0,32},{16,48},{32,64},{48,80},{64,96},{80,112},{96,128},{112,144}... | collective-permute-start | bytes 1572872 | tf_op jit(solution)/shard_map/ppermute | solution.py:78
  111.7 12.9 %collective-permute-start.12 = (bf16[512,512]{1,0:T(8,128)(2,1)}, bf16[512,512]{1,0:T(8,128)(2,1)S(1)}, u32[]{:S(2)}, u32[]{:S(2)}) collective-permute-start(bf16[512,512]{1,0:T(8,128)(2,1)} %collective-permute-done.11.refs_12_.rest_12_), channel_id=1, source_target_pairs={{0,480},{16,496},{32,0},{48,16},{64,32},{80,48},{96,64},{112,80},{... | collective-permute-start | bytes 1572872 | tf_op jit(solution)/shard_map/ppermute | solution.py:78
  117.5 13.0 %collective-permute-start.5 = (bf16[512,512]{1,0:T(8,128)(2,1)}, bf16[512,512]{1,0:T(8,128)(2,1)S(1)}, u32[]{:S(2)}, u32[]{:S(2)}) collective-permute-start(bf16[512,512]{1,0:T(8,128)(2,1)} %collective-permute-done.4.refs_5_.rest_5_), channel_id=1, source_target_pairs={{0,32},{16,48},{32,64},{48,80},{64,96},{80,112},{96,128},{112,144}... | collective-permute-start | bytes 1572872 | tf_op jit(solution)/shard_map/ppermute | solution.py:78
  124.6 5.9 %copy-start.15 = (bf16[512,512]{1,0:T(8,128)(2,1)}, bf16[512,512]{1,0:T(8,128)(2,1)S(1)}, u32[]{:S(2)}) copy-start(bf16[512,512]{1,0:T(8,128)(2,1)S(1)} %collective-permute-done.12.refs_13_.rest_13_) | copy-start | bytes 1572868
  124.6 13.5 %collective-permute-start.13 = (bf16[512,512]{1,0:T(8,128)(2,1)S(1)}, bf16[512,512]{1,0:T(8,128)(2,1)S(1)}, u32[]{:S(2)}, u32[]{:S(2)}) collective-permute-start(bf16[512,512]{1,0:T(8,128)(2,1)S(1)} %collective-permute-done.12.refs_13_.rest_13_), channel_id=1, source_target_pairs={{0,480},{16,496},{32,0},{48,16},{64,32},{80,48},{96,64},{112,80},{... | collective-permute-start | bytes 1572872 | tf_op jit(solution)/shard_map/ppermute | solution.py:78
  130.4 13.8 %copy-start.16 = (bf16[512,512]{1,0:T(8,128)(2,1)}, bf16[512,512]{1,0:T(8,128)(2,1)S(1)}, u32[]{:S(2)}) copy-start(bf16[512,512]{1,0:T(8,128)(2,1)S(1)} %collective-permute-done.5.refs_6_.rest_6_) | copy-start | bytes 1572868
  130.5 13.8 %collective-permute-start.6 = (bf16[512,512]{1,0:T(8,128)(2,1)S(1)}, bf16[512,512]{1,0:T(8,128)(2,1)S(1)}, u32[]{:S(2)}, u32[]{:S(2)}) collective-permute-start(bf16[512,512]{1,0:T(8,128)(2,1)S(1)} %collective-permute-done.5.refs_6_.rest_6_), channel_id=1, source_target_pairs={{0,32},{16,48},{32,64},{48,80},{64,96},{80,112},{96,128},{112,144}... | collective-permute-start | bytes 1572872 | tf_op jit(solution)/shard_map/ppermute | solution.py:78
  138.1 15.7 %copy-start.4 = (bf16[512,512]{1,0:T(8,128)(2,1)}, bf16[512,512]{1,0:T(8,128)(2,1)S(1)}, u32[]{:S(2)}) copy-start(bf16[512,512]{1,0:T(8,128)(2,1)S(1)} %collective-permute-done.13.refs_14_.rest_14_) | copy-start | bytes 1572868
  138.1 9.5 %collective-permute-start.15 = (bf16[256,512]{1,0:T(8,128)(2,1)S(1)}, bf16[256,512]{1,0:T(8,128)(2,1)S(1)}, u32[]{:S(2)}, u32[]{:S(2)}) collective-permute-start(bf16[256,512]{1,0:T(8,128)(2,1)S(1)} %slice.17), channel_id=1, source_target_pairs={{0,480},{16,496},{32,0},{48,16},{64,32},{80,48},{96,64},{112,80},{... | collective-permute-start | bytes 786440 | tf_op jit(solution)/shard_map/ppermute | solution.py:78
  144.3 9.5 %copy-start.5 = (bf16[512,512]{1,0:T(8,128)(2,1)}, bf16[512,512]{1,0:T(8,128)(2,1)S(1)}, u32[]{:S(2)}) copy-start(bf16[512,512]{1,0:T(8,128)(2,1)S(1)} %collective-permute-done.6.refs_7_.rest_7_) | copy-start | bytes 1572868
  144.3 9.5 %collective-permute-start.14 = (bf16[256,512]{1,0:T(8,128)(2,1)S(1)}, bf16[256,512]{1,0:T(8,128)(2,1)S(1)}, u32[]{:S(2)}, u32[]{:S(2)}) collective-permute-start(bf16[256,512]{1,0:T(8,128)(2,1)S(1)} %slice.16), channel_id=1, source_target_pairs={{0,32},{16,48},{32,64},{48,80},{64,96},{80,112},{96,128},{112,144}... | collective-permute-start | bytes 786440 | tf_op jit(solution)/shard_map/ppermute | solution.py:78
  147.6 6.3 %copy-start.17 = (bf16[256,512]{1,0:T(8,128)(2,1)}, bf16[256,512]{1,0:T(8,128)(2,1)S(1)}, u32[]{:S(2)}) copy-start(bf16[256,512]{1,0:T(8,128)(2,1)S(1)} %collective-permute-done.15.refs_16_.rest_16_) | copy-start | bytes 786436
  153.8 0.7 copy-start.18
  158.3 6.3 %collective-permute-start.16 = (bf16[16,128,512]{2,1,0:T(8,128)(2,1)}, bf16[16,128,512]{2,1,0:T(8,128)(2,1)S(1)}, u32[]{:S(2)}, u32[]{:S(2)}) collective-permute-start(bf16[16,128,512]{2,1,0:T(8,128)(2,1)} %pick.1), channel_id=1, source_target_pairs={{0,16},{16,0},{32,48},{48,32},{64,80},{80,64},{96,112},{112,96},{1... | collective-permute-start | bytes 6291464 | tf_op jit(solution)/shard_map/ppermute | solution.py:320
  164.6 1.4 copy-start.6
  174.3 6.9 %copy-start.19 = (s32[64,8]{0,1:T(8,128)S(1)}, s32[64,8]{0,1:T(8,128)}, u32[]{:S(2)}) copy-start(s32[64,8]{0,1:T(8,128)} %param.14) | copy-start | bytes 6148
  174.3 29.8 %all-to-all-start.2 = ((bf16[16,96,512]{2,1,0:T(8,128)(2,1)}), bf16[16,96,512]{2,1,0:T(8,128)(2,1)S(1)}, u32[]{:S(2)}, u32[]{:S(2)}) async-start(bf16[16,96,512]{2,1,0:T(8,128)(2,1)} %bitcast.18), calls=%async_computation.2 | async-start | bytes 3145728 | tf_op jit(solution)/shard_map/all_to_all | solution.py:327
  181.2 52.1 %copy-start = (bf16[512,512]{1,0:T(8,128)(2,1)S(1)}, bf16[512,512]{1,0:T(8,128)(2,1)}, u32[]{:S(2)}) copy-start(bf16[512,512]{1,0:T(8,128)(2,1)} %attn_ref.1) | copy-start | bytes 1572868
  181.2 52.1 %copy-start.1 = (bf16[512,512]{1,0:T(8,128)(2,1)S(1)}, bf16[512,512]{1,0:T(8,128)(2,1)}, u32[]{:S(2)}) copy-start(bf16[512,512]{1,0:T(8,128)(2,1)} %get-tuple-element.19.agg_ref) | copy-start | bytes 1572868
  181.3 52.1 %copy-start.2 = (f32[512]{0:T(512)S(1)}, f32[512]{0:T(512)}, u32[]{:S(2)}) copy-start(f32[512]{0:T(512)} %param.17) | copy-start | bytes 6148

commit v3 on v2

--- a/solution.py
+++ b/solution.py
@@ -17,62 +17,74 @@
 EXP2_SCALE = math.log2(math.e) / math.sqrt(HDIM)
 
 
-def start_copies(place_ref, wanted_ref, whole, halves, slot_of, sems):
+def start_copies(place_ref, wanted_ref, far_row, pieces, slot_of, sems):
     n = wanted_ref.shape[0]
     core, z = place_ref[0] % 2, place_ref[0] // 2
     chips, half = n // 2, n // 4
     copies = []
-
-    def copy_of(slot, piece, block):
+    steps = list(range(half)) + [chips - k for k in range(1, half)] + [half]
+    for slot, (piece, step) in enumerate(zip(pieces, steps)):
+        block = wanted_ref[2 * ((z + chips - step) % chips) + core]
+        if step == half:
+            block = far_row
         rows = pl.ds(pl.multiple_of(block * BLOCK, BLOCK), BLOCK)
-        return pltpu.make_async_copy(piece.at[rows, :], slot_of(slot), sems.at[slot])
-
-    def wanted(step):
-        return wanted_ref[2 * ((z + chips - step) % chips) + core]
-
-    steps = list(range(half)) + [chips - k for k in range(1, half)]
-    for slot, (piece, step) in enumerate(zip(whole, steps)):
-        copies.append(copy_of(slot, piece, wanted(step)))
+        copies.append(pltpu.make_async_copy(piece.at[rows, :], slot_of(slot), sems.at[slot]))
         copies[-1].start()
-    slot, first = chips - 1, halves[0].shape[0] // BLOCK
-    block = wanted(half)
-
-    @pl.when(block < first)
-    def _():
-        copy_of(slot, halves[0], block).start()
-
-    @pl.when(block >= first)
-    def _():
-        copy_of(slot, halves[1], block - first).start()
-
-    copies.append(copy_of(slot, halves[0], 0))
     return copies
 
 
 def pick_kernel(place_ref, wanted_ref, *refs):
-    whole, halves, (out_ref, sems) = refs[:-4], refs[-4:-2], refs[-2:]
+    pieces, (out_ref, sems) = refs[:-2], refs[-2:]
     for copy in start_copies(
-        place_ref, wanted_ref, whole, halves, lambda slot: out_ref.at[slot], sems
+        place_ref, wanted_ref, 1, pieces, lambda slot: out_ref.at[slot], sems
     ):
         copy.wait()
 
 
-def pick(place, wanted, whole, halves):
-    slots = len(whole) + 1
+def pick(place, wanted, pieces):
     return pl.pallas_call(
         pick_kernel,
-        out_shape=jax.ShapeDtypeStruct((slots, BLOCK, whole[0].shape[1]), jnp.bfloat16),
-        in_specs=[SM, SM] + [FAR] * (len(whole) + 2),
+        out_shape=jax.ShapeDtypeStruct((len(pieces), BLOCK, pieces[0].shape[1]), jnp.bfloat16),
+        in_specs=[SM, SM] + [FAR] * len(pieces),
         out_specs=VM,
-        scratch_shapes=[pltpu.SemaphoreType.DMA((slots,))],
+        scratch_shapes=[pltpu.SemaphoreType.DMA((len(pieces),))],
         name="pick",
-    )(place, wanted, *whole, *halves)
-
-
-def ring_pieces(x, lists, weights, qkv_weight):
+    )(place, wanted, *pieces)
+
+
+def pass_on_kernel(place_ref, mine_ref, other_ref, piece, out_ref, sems):
+    n = mine_ref.shape[0]
+    core, z = place_ref[0] % 2, place_ref[0] // 2
+    chips, half = n // 2, n // 4
+    source = 2 * ((z + chips - (half - 1)) % chips) + core
+    copies = []
+    for i, ref in enumerate((mine_ref, other_ref)):
+        rows = pl.ds(pl.multiple_of(ref[source] * BLOCK, BLOCK), BLOCK)
+        copies.append(
+            pltpu.make_async_copy(
+                piece.at[rows, :], out_ref.at[pl.ds(i * BLOCK, BLOCK), :], sems.at[i]
+            )
+        )
+        copies[-1].start()
+    for copy in copies:
+        copy.wait()
+
+
+def pass_on(place, mine, other, piece):
+    return pl.pallas_call(
+        pass_on_kernel,
+        out_shape=jax.ShapeDtypeStruct((2 * BLOCK, piece.shape[1]), jnp.bfloat16),
+        in_specs=[SM, SM, SM, pl.BlockSpec(memory_space=pl.ANY)],
+        out_specs=VM,
+        scratch_shapes=[pltpu.SemaphoreType.DMA((2,))],
+        compiler_params=pltpu.CompilerParams(vmem_limit_bytes=1 << 20),
+        name="pass_on",
+    )(place, mine, other, piece)
+
+
+def ring_pieces(x, place, lists, weights, qkv_weight):
     n, n_head = lax.axis_size("dom"), lax.axis_size("head")
     half = n // 4
-    cut = x.shape[0] // 2
 
     def send(v, by):
         return lax.ppermute(v, "dom", [(i, (i + by) % n) for i in range(n)])
@@ -85,22 +97,23 @@
         jnp.stack([mine, swapped], axis=1), "dom", split_axis=0, concat_axis=0, tiled=True
     )
     both = jnp.concatenate(weights, axis=1)
-    both, served = lax.optimization_barrier((both, served))
-    ffn = lax.all_to_all(
-        jnp.broadcast_to(both[None], (n_head,) + both.shape),
-        "head", split_axis=0, concat_axis=0, tiled=True,
-    ).reshape(-1, both.shape[1])
-    for k in range(1, half + 1):
+    copied = jnp.broadcast_to(both[None], (n_head,) + both.shape)
+    copied, served = lax.optimization_barrier((copied, served))
+    ffn = lax.all_to_all(copied, "head", split_axis=0, concat_axis=0, tiled=True)
+    ffn = ffn.reshape(-1, both.shape[1])
+    for k in range(1, half):
         u_in, d_in = up[-1], down[-1]
-        if k == half:
-            u_in, d_in = u_in[:cut], d_in[cut:]
         if k == 6:
-            u_in, weight_t = lax.optimization_barrier((u_in, weight_t))
-        if k == half:
-            u_in, ffn = lax.optimization_barrier((u_in, ffn))
+            u_in, weight_t, above = lax.optimization_barrier((u_in, weight_t, above))
         up.append(send(u_in, 2))
         down.append(send(d_in, -2))
-    return up[:half] + down[1:half], [up[half], down[half]], served, ffn, weight_t
+        if k == 4:
+            up[-2], served = lax.optimization_barrier((up[-2], served))
+            above = send(served, -2)
+    u_in = pass_on(place, above[:, 0], above[:, 1], up[-1])
+    u_in, ffn = lax.optimization_barrier((u_in, ffn))
+    up.append(send(u_in, 2))
+    return up[:half] + down[1:half] + up[half:], served, ffn, weight_t
 
 
 def slot_of_entry(e, d, blocks, n):
@@ -114,48 +127,63 @@
     return jnp.where(e < blocks, e, blocks + other + near)
 
 
-def aggregate_kernel(place_ref, entry_ref, serve_ref, pattern_ref, own_ref, wt_ref, *rest):
-    pieces, (agg_ref, qkv_ref, table, sems) = rest[:-4], rest[-4:]
+def aggregate_kernel(place_ref, entry_ref, serve_ref, pattern_hbm, own_hbm, wt_hbm, *rest):
+    pieces, (agg_ref, qkv_ref, table, wt_ref, pattern_ref, near_ref, sems, load_sems) = (
+        rest[:-8], rest[-8:]
+    )
     blocks, tiles = pattern_ref.shape[0], pattern_ref.shape[1]
     n_dom = serve_ref.shape[0]
     chips = n_dom // 2
     d = place_ref[0]
+    pattern_load = pltpu.make_async_copy(pattern_hbm, pattern_ref, load_sems.at[0])
+    own_load = pltpu.make_async_copy(own_hbm, table.at[pl.ds(0, blocks)], load_sems.at[1])
+    wt_load = pltpu.make_async_copy(wt_hbm, wt_ref, load_sems.at[2])
+    pattern_load.start()
     copies = start_copies(
-        place_ref, serve_ref, pieces[:-3], pieces[-3:-1], lambda slot: table.at[blocks + slot], sems
+        place_ref, serve_ref, 0, pieces[:-1], lambda slot: table.at[blocks + slot], sems
     )
     handed = pltpu.make_async_copy(
         pieces[-1], table.at[pl.ds(blocks + chips, chips)], sems.at[chips]
     )
     handed.start()
-    copies.append(handed)
-    for b in range(blocks):
-        table[b] = own_ref[b * BLOCK : (b + 1) * BLOCK, :]
-    for copy in copies:
+    own_load.start()
+    wt_load.start()
+    pattern_load.wait()
+
+    def convert(b, carry):
+        count = jnp.zeros((BLOCK, BLOCK), jnp.int32)
+        for t in range(tiles):
+            pattern = pattern_ref[b, t]
+            count = count + pattern
+            near_ref[b, :, t * BLOCK : (t + 1) * BLOCK] = pattern.astype(jnp.float32).astype(
+                jnp.bfloat16
+            )
+        pattern_ref[b, 0] = count
+        return carry
+
+    lax.fori_loop(0, blocks, convert, 0)
+    own_load.wait()
+    for copy in copies + [handed]:
         copy.wait()
 
     def one_block(b, carry):
         acc = table[b].astype(jnp.float32)
-        count = jnp.zeros((BLOCK, BLOCK), jnp.int32)
         for t in range(0, tiles, 2):
-            two = []
-            for u in (t, t + 1):
-                pattern = pattern_ref[b, u]
-                count = count + pattern
-                two.append(pattern.astype(jnp.float32).astype(jnp.bfloat16))
             rows = [
                 table[slot_of_entry(entry_ref[b, u], d, blocks, n_dom)] for u in (t, t + 1)
             ]
             acc = acc + jnp.dot(
-                jnp.concatenate(two, axis=1),
+                near_ref[b, :, t * BLOCK : (t + 2) * BLOCK],
                 jnp.concatenate(rows, axis=0),
                 preferred_element_type=jnp.float32,
             )
-        degree = jnp.sum(count.astype(jnp.float32), axis=1, keepdims=True)
+        degree = jnp.sum(pattern_ref[b, 0].astype(jnp.float32), axis=1, keepdims=True)
         span = pl.ds(pl.multiple_of(b * BLOCK, BLOCK), BLOCK)
         agg_ref[span, :] = (acc * lax.rsqrt(1.0 + degree)).astype(jnp.bfloat16)
         return carry
 
     lax.fori_loop(0, blocks, one_block, 0)
+    wt_load.wait()
     third = qkv_ref.shape[0] // 3
 
     def one_third(i, carry):
@@ -179,14 +207,18 @@
             jax.ShapeDtypeStruct((rows, width), jnp.bfloat16),
             jax.ShapeDtypeStruct((weight_t.shape[0], rows), jnp.bfloat16),
         ),
-        in_specs=[SM, SM, SM, VM, VM, VM] + [FAR] * len(pieces),
+        in_specs=[SM, SM, SM] + [FAR] * (3 + len(pieces)),
         out_specs=(VM, VM),
         scratch_shapes=[
             pltpu.VMEM((blocks + serve.shape[0], BLOCK, width), jnp.bfloat16),
+            pltpu.VMEM(weight_t.shape, jnp.bfloat16),
+            pltpu.VMEM(pattern.shape, jnp.int32),
+            pltpu.VMEM((blocks, BLOCK, tiles * BLOCK), jnp.bfloat16),
             pltpu.SemaphoreType.DMA((serve.shape[0] // 2 + 1,)),
+            pltpu.SemaphoreType.DMA((3,)),
         ],
         name="aggregate",
-    )(place, entries, serve, pattern, own, weight_t, *pieces)
+    )(place, entries, serve, pattern, own.reshape(blocks, BLOCK, width), weight_t, *pieces)
 
 
 def attend_kernel(key_ref, qkv_ref, out_ref, q_ref, kv_ref):
@@ -314,15 +346,14 @@
 
     place = lax.axis_index("dom").reshape(1)
     n_dom = lax.axis_size("dom")
-    whole, halves, served, ffn, weight_t = ring_pieces(
-        features, serve_list, (expand_weight, reduce_weight), qkv_weight
+    pieces, served, ffn, weight_t = ring_pieces(
+        features, place, serve_list, (expand_weight, reduce_weight), qkv_weight
     )
     handed = lax.ppermute(
-        pick(place, served[:, 1], whole, halves), "dom", [(i, i ^ 1) for i in range(n_dom)]
+        pick(place, served[:, 1], pieces), "dom", [(i, i ^ 1) for i in range(n_dom)]
     )
     agg, qkv_t = aggregate(
-        place, tile_source, served[:, 0], tile_pattern, features, weight_t,
-        whole + halves + [handed],
+        place, tile_source, served[:, 0], tile_pattern, features, weight_t, pieces + [handed]
     )
     qkv = lax.all_to_all(
         qkv_t.reshape(n_head, 3 * HDIM, rows), "head", split_axis=0, concat_axis=0, tiled=True

time: 242 us -> 240 us (level)
    unnamed x43 -> x37, local copies, waits for them, and re-layouts: 5.31 us -> 5.33 us
  transfers between devices with their start and end apart: 20 -> 20, of which waited for: 14 -> 11; matrix products, arithmetic and copies ran while one was open for 2% -> 2% of each run, Pallas kernels for 0% -> 0%
where the time goes in v3:
time: 240 us; the launch traced here: 239 us
  waiting for transfers between devices  91.3 us (38%)
  starting transfers between devices  86 us (36%)
  Pallas kernels  35.4 us (15%)
  blocking collectives  13.5 us (6%)
  local copies, waits for them, and re-layouts  9.46 us (4%)
  other arithmetic  2.97 us (1%)
    ppermute x16, starting transfers between devices, send(): return lax.ppermute(v, 'dom', [(i, (i + by) % n) for i in range(n)])  54 us
    ppermute x16, waiting for transfers between devices, send(): return lax.ppermute(v, 'dom', [(i, (i + by) % n) for i in range(n)])  52.6 us
    all_to_all x1, waiting for transfers between devices, shards(): lax.all_to_all(qkv_t.reshape(n_head, 3 * HDIM, rows), 'head', split_axis=...  22.9 us
    pallas_call x1, Pallas kernels, attend(): pl.pallas_call(attend_kernel, out_shape=jax.ShapeDtypeStruct((sources, HD...  15.7 us
    all_to_all x1, starting transfers between devices, ring_pieces(): lax.all_to_all(jnp.stack([mine, swapped], axis=1), 'dom', split_axis=0, c...  15.5 us
    all_to_all x1, blocking collectives, shards(): lax.all_to_all(context, 'head', split_axis=0, concat_axis=0, tiled=True)  13.5 us
    all_to_all x1, waiting for transfers between devices, ring_pieces(): lax.all_to_all(jnp.stack([mine, swapped], axis=1), 'dom', split_axis=0, c...  11.4 us
    pallas_call x1, Pallas kernels, aggregate(): pl.pallas_call(aggregate_kernel, out_shape=(jax.ShapeDtypeStruct((rows, w...  7.54 us
  transfers between devices with their start and end apart: 20, of which 11 were waited for; matrix products, arithmetic and copies ran while one was open for 2% of the time, Pallas kernels for 0%

profile of v3, /device:TPU:8, one launch (start us, length us, event | category | flops | bytes accessed | tf_op | source)
XLA Modules:
  0.0 239.0 jit_solution(6971126438554862850)
XLA Ops:
  0.0 0.5 broadcast.4
  0.5 1.3 reduce.3
  1.8 0.1 reshape_reshape.3
  1.9 0.1 rev.3
  2.0 0.1 stack_reshape.7
  2.1 0.7 add_bitcast_fusion
  2.8 0.7 copy.15
  3.5 15.5 %all-to-all-start = ((s32[32,1,2]{2,1,0:T(1,128)}), s32[32,1,2]{2,1,0:T(1,128)S(1)}, u32[]{:S(2)}, u32[]{:S(2)}) async-start(s32[32,1,2]{2,1,0:T(1,128)} %copy.15), calls=%async_computation | async-start | bytes 32768 | tf_op jit(solution)/shard_map/all_to_all | solution.py:96
  18.9 1.0 pad_maximum_fusion
  19.9 11.4 %all-to-all-done = s32[32,1,2]{2,1,0:T(1,128)S(1)} async-done(((s32[32,1,2]{2,1,0:T(1,128)}), s32[32,1,2]{2,1,0:T(1,128)S(1)}, u32[]{:S(2)}, u32[]{:S(2)}) %all-to-all-start) | async-done | bytes 288 | tf_op jit(solution)/shard_map/all_to_all | solution.py:96
  31.4 0.1 copy.16
  31.4 2.6 %broadcast_in_dim.2 = bf16[16,128,1024]{2,1,0:T(8,128)(2,1)} broadcast(bf16[128,1024]{1,0:T(8,128)(2,1)S(1)} %pad_maximum_fusion), dimensions={1,2} | broadcast | bytes 4456448 | tf_op jit(solution)/shard_map/broadcast_in_dim | solution.py:100
  34.0 7.5 %all-to-all-start.1 = ((bf16[16,128,1024]{2,1,0:T(8,128)(2,1)}), bf16[16,128,1024]{2,1,0:T(8,128)(2,1)}, u32[]{:S(2)}, u32[]{:S(2)}) async-start(bf16[16,128,1024]{2,1,0:T(8,128)(2,1)} %broadcast_in_dim.2), calls=%async_computation.1 | async-start | bytes 8388608 | tf_op jit(solution)/shard_map/all_to_all | solution.py:102
  41.5 2.5 %collective-permute-start = (bf16[512,512]{1,0:T(8,128)(2,1)S(1)}, bf16[512,512]{1,0:T(8,128)(2,1)S(1)}, u32[]{:S(2)}, u32[]{:S(2)}) collective-permute-start(bf16[512,512]{1,0:T(8,128)(2,1)S(1)} %copy-done.4), channel_id=1, source_target_pairs={{0,32},{16,48},{32,64},{48,80},{64,96},{80,112},{96,128},{112,144}... | collective-permute-start | bytes 1572872 | tf_op jit(solution)/shard_map/ppermute | solution.py:90
  44.0 4.6 %collective-permute-start.8 = (bf16[512,512]{1,0:T(8,128)(2,1)S(1)}, bf16[512,512]{1,0:T(8,128)(2,1)S(1)}, u32[]{:S(2)}, u32[]{:S(2)}) collective-permute-start(bf16[512,512]{1,0:T(8,128)(2,1)S(1)} %copy-done.4), channel_id=1, source_target_pairs={{0,480},{16,496},{32,0},{48,16},{64,32},{80,48},{96,64},{112,80},{... | collective-permute-start | bytes 1572872 | tf_op jit(solution)/shard_map/ppermute | solution.py:90
  48.6 8.9 %collective-permute-done.refs_1_.rest_1_ = bf16[512,512]{1,0:T(8,128)(2,1)S(1)} collective-permute-done((bf16[512,512]{1,0:T(8,128)(2,1)S(1)}, bf16[512,512]{1,0:T(8,128)(2,1)S(1)}, u32[]{:S(2)}, u32[]{:S(2)}) %collective-permute-start) | collective-permute-done | bytes 524320 | tf_op jit(solution)/shard_map/ppermute | solution.py:90
  57.5 1.9 collective-permute-start.1
  59.4 0.0 collective-permute-done.8.refs_8_.rest_8_
  59.4 5.1 %collective-permute-start.9 = (bf16[512,512]{1,0:T(8,128)(2,1)S(1)}, bf16[512,512]{1,0:T(8,128)(2,1)S(1)}, u32[]{:S(2)}, u32[]{:S(2)}) collective-permute-start(bf16[512,512]{1,0:T(8,128)(2,1)S(1)} %collective-permute-done.8.refs_8_.rest_8_), channel_id=1, source_target_pairs={{0,480},{16,496},{32,0},{48,16},{64,32},{80,48},{96,64},{112,80},{... | collective-permute-start | bytes 1572872 | tf_op jit(solution)/shard_map/ppermute | solution.py:90
  64.6 8.1 %collective-permute-done.1.refs_2_.rest_2_ = bf16[512,512]{1,0:T(8,128)(2,1)S(1)} collective-permute-done((bf16[512,512]{1,0:T(8,128)(2,1)S(1)}, bf16[512,512]{1,0:T(8,128)(2,1)S(1)}, u32[]{:S(2)}, u32[]{:S(2)}) %collective-permute-start.1) | collective-permute-done | bytes 524320 | tf_op jit(solution)/shard_map/ppermute | solution.py:90
  72.7 1.9 collective-permute-start.2
  74.6 0.0 collective-permute-done.9.refs_9_.rest_9_
  74.7 5.1 %collective-permute-start.10 = (bf16[512,512]{1,0:T(8,128)(2,1)S(1)}, bf16[512,512]{1,0:T(8,128)(2,1)S(1)}, u32[]{:S(2)}, u32[]{:S(2)}) collective-permute-start(bf16[512,512]{1,0:T(8,128)(2,1)S(1)} %collective-permute-done.9.refs_9_.rest_9_), channel_id=1, source_target_pairs={{0,480},{16,496},{32,0},{48,16},{64,32},{80,48},{96,64},{112,80},{... | collective-permute-start | bytes 1572872 | tf_op jit(solution)/shard_map/ppermute | solution.py:90
  79.8 7.4 %collective-permute-done.2.refs_3_.rest_3_ = bf16[512,512]{1,0:T(8,128)(2,1)S(1)} collective-permute-done((bf16[512,512]{1,0:T(8,128)(2,1)S(1)}, bf16[512,512]{1,0:T(8,128)(2,1)S(1)}, u32[]{:S(2)}, u32[]{:S(2)}) %collective-permute-start.2) | collective-permute-done | bytes 524320 | tf_op jit(solution)/shard_map/ppermute | solution.py:90
  87.2 1.9 collective-permute-start.3
  89.1 0.0 collective-permute-done.10.refs_10_.rest_10_
  89.1 0.0 copy-done.10
  89.1 5.1 %collective-permute-start.11 = (bf16[512,512]{1,0:T(8,128)(2,1)S(1)}, bf16[512,512]{1,0:T(8,128)(2,1)}, u32[]{:S(2)}, u32[]{:S(2)}) collective-permute-start(bf16[512,512]{1,0:T(8,128)(2,1)S(1)} %collective-permute-done.10.refs_10_.rest_10_), channel_id=1, source_target_pairs={{0,480},{16,496},{32,0},{48,16},{64,32},{80,48},{96,64},{112,80},{... | collective-permute-start | bytes 1572872 | tf_op jit(solution)/shard_map/ppermute | solution.py:90
  94.3 6.5 %collective-permute-done.3.refs_4_.rest_4_ = bf16[512,512]{1,0:T(8,128)(2,1)S(1)} collective-permute-done((bf16[512,512]{1,0:T(8,128)(2,1)S(1)}, bf16[512,512]{1,0:T(8,128)(2,1)S(1)}, u32[]{:S(2)}, u32[]{:S(2)}) %collective-permute-start.3) | collective-permute-done | bytes 524320 | tf_op jit(solution)/shard_map/ppermute | solution.py:90
  100.8 1.9 collective-permute-start.4
  102.7 0.0 collective-permute-done.11.refs_11_.rest_11_
  102.7 5.1 %collective-permute-start.12 = (bf16[512,512]{1,0:T(8,128)(2,1)}, bf16[512,512]{1,0:T(8,128)(2,1)}, u32[]{:S(2)}, u32[]{:S(2)}) collective-permute-start(bf16[512,512]{1,0:T(8,128)(2,1)} %collective-permute-done.11.refs_11_.rest_11_), channel_id=1, source_target_pairs={{0,480},{16,496},{32,0},{48,16},{64,32},{80,48},{96,64},{112,80},{... | collective-permute-start | bytes 1572872 | tf_op jit(solution)/shard_map/ppermute | solution.py:90
  107.9 1.9 collective-permute-start.5
  109.8 2.6 %copy.17 = bf16[512,1536]{0,1:T(8,128)(2,1)} copy(bf16[512,1536]{1,0:T(8,128)(2,1)} %param.15) | data formatting | bytes 3145728 | tf_op args[5]
  112.4 2.7 %collective-permute-done.5 = s32[32,2]{0,1:T(2,128)S(1)} collective-permute-done((s32[32,2]{0,1:T(2,128)S(1)}, s32[32,2]{0,1:T(2,128)S(1)}, u32[]{:S(2)}, u32[]{:S(2)}) %collective-permute-start.5) | collective-permute-done | bytes 288 | tf_op jit(solution)/shard_map/ppermute | solution.py:90
  115.1 0.0 collective-permute-done.4.refs_5_.rest_5_
  115.1 1.9 collective-permute-start.6
  117.0 0.0 collective-permute-done.12.refs_12_.rest_12_
  117.0 5.6 %collective-permute-start.13 = (bf16[512,512]{1,0:T(8,128)(2,1)}, bf16[512,512]{1,0:T(8,128)(2,1)S(1)}, u32[]{:S(2)}, u32[]{:S(2)}) collective-permute-start(bf16[512,512]{1,0:T(8,128)(2,1)} %collective-permute-done.12.refs_12_.rest_12_), channel_id=1, source_target_pairs={{0,480},{16,496},{32,0},{48,16},{64,32},{80,48},{96,64},{112,80},{... | collective-permute-start | bytes 1572872 | tf_op jit(solution)/shard_map/ppermute | solution.py:90
  122.6 5.7 %collective-permute-done.6.refs_6_.rest_6_ = bf16[512,512]{1,0:T(8,128)(2,1)} collective-permute-done((bf16[512,512]{1,0:T(8,128)(2,1)}, bf16[512,512]{1,0:T(8,128)(2,1)}, u32[]{:S(2)}, u32[]{:S(2)}) %collective-permute-start.6) | collective-permute-done | bytes 524320 | tf_op jit(solution)/shard_map/ppermute | solution.py:90
  128.3 1.9 collective-permute-start.7
  130.3 0.0 collective-permute-done.13.refs_13_.rest_13_
  130.3 5.5 %collective-permute-start.14 = (bf16[512,512]{1,0:T(8,128)(2,1)S(1)}, bf16[512,512]{1,0:T(8,128)(2,1)S(1)}, u32[]{:S(2)}, u32[]{:S(2)}) collective-permute-start(bf16[512,512]{1,0:T(8,128)(2,1)S(1)} %collective-permute-done.13.refs_13_.rest_13_), channel_id=1, source_target_pairs={{0,480},{16,496},{32,0},{48,16},{64,32},{80,48},{96,64},{112,80},{... | collective-permute-start | bytes 1572872 | tf_op jit(solution)/shard_map/ppermute | solution.py:90
  135.8 6.3 %collective-permute-done.7.piece.refs_7_.rest_7_ = bf16[512,512]{1,0:T(8,128)(2,1)S(1)} collective-permute-done((bf16[512,512]{1,0:T(8,128)(2,1)}, bf16[512,512]{1,0:T(8,128)(2,1)S(1)}, u32[]{:S(2)}, u32[]{:S(2)}) %collective-permute-start.7) | collective-permute-done | bytes 524320 | tf_op jit(solution)/shard_map/ppermute | solution.py:90
  142.1 0.9 pass_on.1
  143.0 0.0 all-to-all-done.1
  143.0 1.9 collective-permute-start.15
  144.9 0.5 slice_bitcast_fusion
  145.5 0.0 collective-permute-done.14.refs_14_.rest_14_
  145.5 7.0 %collective-permute-done.15.refs_15_.rest_15_ = bf16[256,512]{1,0:T(8,128)(2,1)S(1)} collective-permute-done((bf16[256,512]{1,0:T(8,128)(2,1)S(1)}, bf16[256,512]{1,0:T(8,128)(2,1)S(1)}, u32[]{:S(2)}, u32[]{:S(2)}) %collective-permute-start.15) | collective-permute-done | bytes 262176 | tf_op jit(solution)/shard_map/ppermute | solution.py:90
  152.5 0.7 copy-done.15
  153.2 3.8 %pick.1 = bf16[16,128,512]{2,1,0:T(8,128)(2,1)} custom-call(s32[1]{0:T(128)} %bitcast.place_ref, s32[32]{0:T(128)} %get-tuple-element.27.wanted_ref, bf16[512,512]{1,0:T(8,128)(2,1)} %rest_0_.1, bf16[512,512]{1,0:T(8,128)(2,1)} %copy-done.6, bf16[512,512]{1,0:T(8,128)(2,1)} %copy-done.8, bf16[512,512]{1,0:T(8,128)(2,1)} %copy-done.10, ...), custom_call_target="tpu_custom_call" | custom-call | tf_op jit(solution)/shard_map/pick/pallas_call | solution.py:45
  157.0 1.9 collective-permute-start.16
  158.9 4.3 %collective-permute-done.16.rest_16_ = bf16[16,128,512]{2,1,0:T(8,128)(2,1)S(1)} collective-permute-done((bf16[16,128,512]{2,1,0:T(8,128)(2,1)}, bf16[16,128,512]{2,1,0:T(8,128)(2,1)S(1)}, u32[]{:S(2)}, u32[]{:S(2)}) %collective-permute-start.16) | collective-permute-done | bytes 2097184 | tf_op jit(solution)/shard_map/ppermute | solution.py:352
  163.3 1.4 copy-done.5
  164.7 7.5 %aggregate.1 = (bf16[512,512]{1,0:T(8,128)(2,1)}, bf16[1536,512]{1,0:T(8,128)(2,1)}) custom-call(s32[1]{0:T(128)} %bitcast.place_ref, s32[4,6]{1,0:T(4,128)} %entry_ref.1, s32[32]{0:T(128)} %get-tuple-element.28.serve_ref, s32[4,6,128,128]{3,2,1,0:T(8,128)} %pattern_hbm.1, bf16[4,128,512]{2,1,0:T(8,128)(2,1)} %bitcast.23, bf16[1536,512]{1,0:T(8,128)(2,1)} %bitcast.22, ...), custom_call_target="tpu_custom_call" | custom-call | tf_op jit(solution)/shard_map/aggregate/pallas_call | solution.py:204
  172.2 0.0 copy-start.16
  172.2 7.1 %all-to-all-start.2 = ((bf16[16,96,512]{2,1,0:T(8,128)(2,1)}), bf16[16,96,512]{2,1,0:T(8,128)(2,1)S(1)}, u32[]{:S(2)}, u32[]{:S(2)}) async-start(bf16[16,96,512]{2,1,0:T(8,128)(2,1)} %bitcast.24), calls=%async_computation.2 | async-start | bytes 3145728 | tf_op jit(solution)/shard_map/all_to_all | solution.py:358
  179.4 0.1 copy.18.key_ref
  179.4 0.0 copy-start.3
  179.5 22.9 %all-to-all-done.2.qkv_ref = bf16[16,96,512]{2,1,0:T(8,128)(2,1)S(1)} async-done(((bf16[16,96,512]{2,1,0:T(8,128)(2,1)}), bf16[16,96,512]{2,1,0:T(8,128)(2,1)S(1)}, u32[]{:S(2)}, u32[]{:S(2)}) %all-to-all-start.2) | async-done | bytes 1572896 | tf_op jit(solution)/shard_map/all_to_all | solution.py:358
  202.3 15.7 %attend.1 = bf16[16,32,512]{2,1,0:T(8,128)(2,1)S(1)} custom-call(s32[64,8]{1,0:T(8,128)S(1)} %copy.18.key_ref, bf16[16,96,512]{2,1,0:T(8,128)(2,1)S(1)} %all-to-all-done.2.qkv_ref), custom_call_target="tpu_custom_call" | custom-call | tf_op jit(solution)/shard_map/attend/pallas_call | solution.py:273
  218.0 13.5 %all_to_all.27 = bf16[16,32,512]{2,1,0:T(8,128)(2,1)S(1)} all-to-all(bf16[16,32,512]{2,1,0:T(8,128)(2,1)S(1)} %attend.1), channel_id=1, replica_groups=mesh['dom'=32,'head'=16] {'head'}, dimensions={0} | all-to-all | bytes 1048576 | tf_op jit(solution)/shard_map/all_to_all | solution.py:362
  231.6 7.4 %finish.1 = bf16[512,512]{1,0:T(8,128)(2,1)} custom-call(bf16[512,512]{1,0:T(8,128)(2,1)S(1)} %bitcast.20, bf16[512,512]{1,0:T(8,128)(2,1)S(1)} %copy-done.2, bf16[512,512]{1,0:T(8,128)(2,1)S(1)} %copy-done.1, f32[1,512]{1,0:T(1,128)S(1)} %bitcast.21, bf16[2048,1024]{1,0:T(8,128)(2,1)} %bitcast.9.ffn_ref), custom_call_target="tpu_custom_call" | custom-call | tf_op jit(solution)/shard_map/finish/pallas_call | solution.py:317
  (30 shorter events, 0.1 us)
Async XLA Ops:
  3.5 27.9 %all-to-all-start = ((s32[32,1,2]{2,1,0:T(1,128)}), s32[32,1,2]{2,1,0:T(1,128)S(1)}, u32[]{:S(2)}, u32[]{:S(2)}) async-start(s32[32,1,2]{2,1,0:T(1,128)} %copy.15), calls=%async_computation | async-start | bytes 32768 | tf_op jit(solution)/shard_map/all_to_all | solution.py:96
  34.0 7.5 %copy-start.4 = (bf16[512,512]{1,0:T(8,128)(2,1)S(1)}, bf16[512,512]{1,0:T(8,128)(2,1)}, u32[]{:S(2)}) copy-start(bf16[512,512]{1,0:T(8,128)(2,1)} %rest_0_.1) | copy-start | bytes 1572868
  34.0 109.0 %all-to-all-start.1 = ((bf16[16,128,1024]{2,1,0:T(8,128)(2,1)}), bf16[16,128,1024]{2,1,0:T(8,128)(2,1)}, u32[]{:S(2)}, u32[]{:S(2)}) async-start(bf16[16,128,1024]{2,1,0:T(8,128)(2,1)} %broadcast_in_dim.2), calls=%async_computation.1 | async-start | bytes 8388608 | tf_op jit(solution)/shard_map/all_to_all | solution.py:102
  41.5 16.0 %collective-permute-start = (bf16[512,512]{1,0:T(8,128)(2,1)S(1)}, bf16[512,512]{1,0:T(8,128)(2,1)S(1)}, u32[]{:S(2)}, u32[]{:S(2)}) collective-permute-start(bf16[512,512]{1,0:T(8,128)(2,1)S(1)} %copy-done.4), channel_id=1, source_target_pairs={{0,32},{16,48},{32,64},{48,80},{64,96},{80,112},{96,128},{112,144}... | collective-permute-start | bytes 1572872 | tf_op jit(solution)/shard_map/ppermute | solution.py:90
  44.0 15.4 %collective-permute-start.8 = (bf16[512,512]{1,0:T(8,128)(2,1)S(1)}, bf16[512,512]{1,0:T(8,128)(2,1)S(1)}, u32[]{:S(2)}, u32[]{:S(2)}) collective-permute-start(bf16[512,512]{1,0:T(8,128)(2,1)S(1)} %copy-done.4), channel_id=1, source_target_pairs={{0,480},{16,496},{32,0},{48,16},{64,32},{80,48},{96,64},{112,80},{... | collective-permute-start | bytes 1572872 | tf_op jit(solution)/shard_map/ppermute | solution.py:90
  57.5 57.6 %copy-start.6 = (bf16[512,512]{1,0:T(8,128)(2,1)}, bf16[512,512]{1,0:T(8,128)(2,1)S(1)}, u32[]{:S(2)}) copy-start(bf16[512,512]{1,0:T(8,128)(2,1)S(1)} %collective-permute-done.refs_1_.rest_1_) | copy-start | bytes 1572868
  57.5 15.2 %collective-permute-start.1 = (bf16[512,512]{1,0:T(8,128)(2,1)S(1)}, bf16[512,512]{1,0:T(8,128)(2,1)S(1)}, u32[]{:S(2)}, u32[]{:S(2)}) collective-permute-start(bf16[512,512]{1,0:T(8,128)(2,1)S(1)} %collective-permute-done.refs_1_.rest_1_), channel_id=1, source_target_pairs={{0,32},{16,48},{32,64},{48,80},{64,96},{80,112},{96,128},{112,144}... | collective-permute-start | bytes 1572872 | tf_op jit(solution)/shard_map/ppermute | solution.py:90
  59.4 55.6 %copy-start.7 = (bf16[512,512]{1,0:T(8,128)(2,1)}, bf16[512,512]{1,0:T(8,128)(2,1)S(1)}, u32[]{:S(2)}) copy-start(bf16[512,512]{1,0:T(8,128)(2,1)S(1)} %collective-permute-done.8.refs_8_.rest_8_) | copy-start | bytes 1572868
  59.4 15.2 %collective-permute-start.9 = (bf16[512,512]{1,0:T(8,128)(2,1)S(1)}, bf16[512,512]{1,0:T(8,128)(2,1)S(1)}, u32[]{:S(2)}, u32[]{:S(2)}) collective-permute-start(bf16[512,512]{1,0:T(8,128)(2,1)S(1)} %collective-permute-done.8.refs_8_.rest_8_), channel_id=1, source_target_pairs={{0,480},{16,496},{32,0},{48,16},{64,32},{80,48},{96,64},{112,80},{... | collective-permute-start | bytes 1572872 | tf_op jit(solution)/shard_map/ppermute | solution.py:90
  72.7 42.4 %copy-start.8 = (bf16[512,512]{1,0:T(8,128)(2,1)}, bf16[512,512]{1,0:T(8,128)(2,1)S(1)}, u32[]{:S(2)}) copy-start(bf16[512,512]{1,0:T(8,128)(2,1)S(1)} %collective-permute-done.1.refs_2_.rest_2_) | copy-start | bytes 1572868
  72.7 14.5 %collective-permute-start.2 = (bf16[512,512]{1,0:T(8,128)(2,1)S(1)}, bf16[512,512]{1,0:T(8,128)(2,1)S(1)}, u32[]{:S(2)}, u32[]{:S(2)}) collective-permute-start(bf16[512,512]{1,0:T(8,128)(2,1)S(1)} %collective-permute-done.1.refs_2_.rest_2_), channel_id=1, source_target_pairs={{0,32},{16,48},{32,64},{48,80},{64,96},{80,112},{96,128},{112,144}... | collective-permute-start | bytes 1572872 | tf_op jit(solution)/shard_map/ppermute | solution.py:90
  74.6 40.4 %copy-start.9 = (bf16[512,512]{1,0:T(8,128)(2,1)}, bf16[512,512]{1,0:T(8,128)(2,1)S(1)}, u32[]{:S(2)}) copy-start(bf16[512,512]{1,0:T(8,128)(2,1)S(1)} %collective-permute-done.9.refs_9_.rest_9_) | copy-start | bytes 1572868
  74.7 14.4 %collective-permute-start.10 = (bf16[512,512]{1,0:T(8,128)(2,1)S(1)}, bf16[512,512]{1,0:T(8,128)(2,1)S(1)}, u32[]{:S(2)}, u32[]{:S(2)}) collective-permute-start(bf16[512,512]{1,0:T(8,128)(2,1)S(1)} %collective-permute-done.9.refs_9_.rest_9_), channel_id=1, source_target_pairs={{0,480},{16,496},{32,0},{48,16},{64,32},{80,48},{96,64},{112,80},{... | collective-permute-start | bytes 1572872 | tf_op jit(solution)/shard_map/ppermute | solution.py:90
  87.2 1.9 copy-start.10
  87.2 13.6 %collective-permute-start.3 = (bf16[512,512]{1,0:T(8,128)(2,1)S(1)}, bf16[512,512]{1,0:T(8,128)(2,1)S(1)}, u32[]{:S(2)}, u32[]{:S(2)}) collective-permute-start(bf16[512,512]{1,0:T(8,128)(2,1)S(1)} %collective-permute-done.2.refs_3_.rest_3_), channel_id=1, source_target_pairs={{0,32},{16,48},{32,64},{48,80},{64,96},{80,112},{96,128},{112,144}... | collective-permute-start | bytes 1572872 | tf_op jit(solution)/shard_map/ppermute | solution.py:90
  89.1 11.7 %copy-start.11 = (bf16[512,512]{1,0:T(8,128)(2,1)}, bf16[512,512]{1,0:T(8,128)(2,1)S(1)}, u32[]{:S(2)}) copy-start(bf16[512,512]{1,0:T(8,128)(2,1)S(1)} %collective-permute-done.10.refs_10_.rest_10_) | copy-start | bytes 1572868
  89.1 13.6 %collective-permute-start.11 = (bf16[512,512]{1,0:T(8,128)(2,1)S(1)}, bf16[512,512]{1,0:T(8,128)(2,1)}, u32[]{:S(2)}, u32[]{:S(2)}) collective-permute-start(bf16[512,512]{1,0:T(8,128)(2,1)S(1)} %collective-permute-done.10.refs_10_.rest_10_), channel_id=1, source_target_pairs={{0,480},{16,496},{32,0},{48,16},{64,32},{80,48},{96,64},{112,80},{... | collective-permute-start | bytes 1572872 | tf_op jit(solution)/shard_map/ppermute | solution.py:90
  100.8 14.3 %copy-start.12 = (bf16[512,512]{1,0:T(8,128)(2,1)}, bf16[512,512]{1,0:T(8,128)(2,1)S(1)}, u32[]{:S(2)}) copy-start(bf16[512,512]{1,0:T(8,128)(2,1)S(1)} %collective-permute-done.3.refs_4_.rest_4_) | copy-start | bytes 1572868
  100.8 14.3 %collective-permute-start.4 = (bf16[512,512]{1,0:T(8,128)(2,1)S(1)}, bf16[512,512]{1,0:T(8,128)(2,1)}, u32[]{:S(2)}, u32[]{:S(2)}) collective-permute-start(bf16[512,512]{1,0:T(8,128)(2,1)S(1)} %collective-permute-done.3.refs_4_.rest_4_), channel_id=1, source_target_pairs={{0,32},{16,48},{32,64},{48,80},{64,96},{80,112},{96,128},{112,144}... | collective-permute-start | bytes 1572872 | tf_op jit(solution)/shard_map/ppermute | solution.py:90
  102.7 14.3 %collective-permute-start.12 = (bf16[512,512]{1,0:T(8,128)(2,1)}, bf16[512,512]{1,0:T(8,128)(2,1)}, u32[]{:S(2)}, u32[]{:S(2)}) collective-permute-start(bf16[512,512]{1,0:T(8,128)(2,1)} %collective-permute-done.11.refs_11_.rest_11_), channel_id=1, source_target_pairs={{0,480},{16,496},{32,0},{48,16},{64,32},{80,48},{96,64},{112,80},{... | collective-permute-start | bytes 1572872 | tf_op jit(solution)/shard_map/ppermute | solution.py:90
  107.9 7.2 %collective-permute-start.5 = (s32[32,2]{0,1:T(2,128)S(1)}, s32[32,2]{0,1:T(2,128)S(1)}, u32[]{:S(2)}, u32[]{:S(2)}) collective-permute-start(s32[32,2]{0,1:T(2,128)S(1)} %bitcast.25), channel_id=1, source_target_pairs={{0,480},{16,496},{32,0},{48,16},{64,32},{80,48},{96,64},{112,80},{... | collective-permute-start | bytes 776 | tf_op jit(solution)/shard_map/ppermute | solution.py:90
  115.1 13.2 %collective-permute-start.6 = (bf16[512,512]{1,0:T(8,128)(2,1)}, bf16[512,512]{1,0:T(8,128)(2,1)}, u32[]{:S(2)}, u32[]{:S(2)}) collective-permute-start(bf16[512,512]{1,0:T(8,128)(2,1)} %collective-permute-done.4.refs_5_.rest_5_), channel_id=1, source_target_pairs={{0,32},{16,48},{32,64},{48,80},{64,96},{80,112},{96,128},{112,144}... | collective-permute-start | bytes 1572872 | tf_op jit(solution)/shard_map/ppermute | solution.py:90
  117.0 13.2 %collective-permute-start.13 = (bf16[512,512]{1,0:T(8,128)(2,1)}, bf16[512,512]{1,0:T(8,128)(2,1)S(1)}, u32[]{:S(2)}, u32[]{:S(2)}) collective-permute-start(bf16[512,512]{1,0:T(8,128)(2,1)} %collective-permute-done.12.refs_12_.rest_12_), channel_id=1, source_target_pairs={{0,480},{16,496},{32,0},{48,16},{64,32},{80,48},{96,64},{112,80},{... | collective-permute-start | bytes 1572872 | tf_op jit(solution)/shard_map/ppermute | solution.py:90
  128.3 13.7 %collective-permute-start.7 = (bf16[512,512]{1,0:T(8,128)(2,1)}, bf16[512,512]{1,0:T(8,128)(2,1)S(1)}, u32[]{:S(2)}, u32[]{:S(2)}) collective-permute-start(bf16[512,512]{1,0:T(8,128)(2,1)} %collective-permute-done.6.refs_6_.rest_6_), channel_id=1, source_target_pairs={{0,32},{16,48},{32,64},{48,80},{64,96},{80,112},{96,128},{112,144}... | collective-permute-start | bytes 1572872 | tf_op jit(solution)/shard_map/ppermute | solution.py:90
  130.3 22.2 %copy-start.13 = (bf16[512,512]{1,0:T(8,128)(2,1)}, bf16[512,512]{1,0:T(8,128)(2,1)S(1)}, u32[]{:S(2)}) copy-start(bf16[512,512]{1,0:T(8,128)(2,1)S(1)} %collective-permute-done.13.refs_13_.rest_13_) | copy-start | bytes 1572868
  130.3 15.2 %collective-permute-start.14 = (bf16[512,512]{1,0:T(8,128)(2,1)S(1)}, bf16[512,512]{1,0:T(8,128)(2,1)S(1)}, u32[]{:S(2)}, u32[]{:S(2)}) collective-permute-start(bf16[512,512]{1,0:T(8,128)(2,1)S(1)} %collective-permute-done.13.refs_13_.rest_13_), channel_id=1, source_target_pairs={{0,480},{16,496},{32,0},{48,16},{64,32},{80,48},{96,64},{112,80},{... | collective-permute-start | bytes 1572872 | tf_op jit(solution)/shard_map/ppermute | solution.py:90
  142.1 10.4 %copy-start = (bf16[512,512]{1,0:T(8,128)(2,1)}, bf16[512,512]{1,0:T(8,128)(2,1)S(1)}, u32[]{:S(2)}) copy-start(bf16[512,512]{1,0:T(8,128)(2,1)S(1)} %collective-permute-done.7.piece.refs_7_.rest_7_) | copy-start | bytes 1572868
  143.0 9.5 %collective-permute-start.15 = (bf16[256,512]{1,0:T(8,128)(2,1)S(1)}, bf16[256,512]{1,0:T(8,128)(2,1)S(1)}, u32[]{:S(2)}, u32[]{:S(2)}) collective-permute-start(bf16[256,512]{1,0:T(8,128)(2,1)S(1)} %pass_on.1), channel_id=1, source_target_pairs={{0,32},{16,48},{32,64},{48,80},{64,96},{80,112},{96,128},{112,144}... | collective-permute-start | bytes 786440 | tf_op jit(solution)/shard_map/ppermute | solution.py:90
  145.5 7.0 %copy-start.14 = (bf16[512,512]{1,0:T(8,128)(2,1)}, bf16[512,512]{1,0:T(8,128)(2,1)S(1)}, u32[]{:S(2)}) copy-start(bf16[512,512]{1,0:T(8,128)(2,1)S(1)} %collective-permute-done.14.refs_14_.rest_14_) | copy-start | bytes 1572868
  152.5 0.7 copy-start.15
  157.0 6.3 %collective-permute-start.16 = (bf16[16,128,512]{2,1,0:T(8,128)(2,1)}, bf16[16,128,512]{2,1,0:T(8,128)(2,1)S(1)}, u32[]{:S(2)}, u32[]{:S(2)}) collective-permute-start(bf16[16,128,512]{2,1,0:T(8,128)(2,1)} %pick.1), channel_id=1, source_target_pairs={{0,16},{16,0},{32,48},{48,32},{64,80},{80,64},{96,112},{112,96},{1... | collective-permute-start | bytes 6291464 | tf_op jit(solution)/shard_map/ppermute | solution.py:352
  163.3 1.4 copy-start.5
  172.2 7.1 %copy-start.16 = (s32[64,8]{0,1:T(8,128)S(1)}, s32[64,8]{0,1:T(8,128)}, u32[]{:S(2)}) copy-start(s32[64,8]{0,1:T(8,128)} %param.14) | copy-start | bytes 6148
  172.2 30.1 %all-to-all-start.2 = ((bf16[16,96,512]{2,1,0:T(8,128)(2,1)}), bf16[16,96,512]{2,1,0:T(8,128)(2,1)S(1)}, u32[]{:S(2)}, u32[]{:S(2)}) async-start(bf16[16,96,512]{2,1,0:T(8,128)(2,1)} %bitcast.24), calls=%async_computation.2 | async-start | bytes 3145728 | tf_op jit(solution)/shard_map/all_to_all | solution.py:358
  179.4 52.1 %copy-start.1 = (bf16[512,512]{1,0:T(8,128)(2,1)S(1)}, bf16[512,512]{1,0:T(8,128)(2,1)}, u32[]{:S(2)}) copy-start(bf16[512,512]{1,0:T(8,128)(2,1)} %attn_ref.1) | copy-start | bytes 1572868
  179.4 52.1 %copy-start.2 = (bf16[512,512]{1,0:T(8,128)(2,1)S(1)}, bf16[512,512]{1,0:T(8,128)(2,1)}, u32[]{:S(2)}) copy-start(bf16[512,512]{1,0:T(8,128)(2,1)} %get-tuple-element.25.agg_ref) | copy-start | bytes 1572868
  179.4 52.1 %copy-start.3 = (f32[512]{0:T(512)S(1)}, f32[512]{0:T(512)}, u32[]{:S(2)}) copy-start(f32[512]{0:T(512)} %param.17) | copy-start | bytes 6148
